TPU v7x, 256 devices: a whole 4x4x8 slice. The times are simulated.
256 devices in a mesh: dp: 16 (over z_hi, y), fsdp: 16 (over x, z_lo, core).
Axes of the slice: x: 4, y: 4, z: 8 (z_hi: 4, z_lo: 2; z = z_hi * 2 + z_lo), core: 2. Of those that a mesh axis runs over, the one named last changes fastest.
Arguments:
- tokens: bfloat16 [32768, 4096], P(('dp', 'fsdp')), may hold values from -6 to 6
- route_ids: int32 [32768, 4], P(('dp', 'fsdp')), may hold values from 0 to 15, all different within a row; in each aligned block of 128 rows (0 to 127, 128 to 255, ...) at most 48 rows name the same one
- gate_values: float32 [32768, 4], P(('dp', 'fsdp')), may hold values from 0.1 to 1
- w_gate_up: bfloat16 [16, 4096, 1536], P('dp', 'fsdp'), may hold values from -0.09375 to 0.09375
- w_down: bfloat16 [16, 768, 4096], P('dp', None, 'fsdp'), may hold values from -0.21875 to 0.21875
Outputs:
- combined: bfloat16 [32768, 4096], P(('dp', 'fsdp'))
Inputs may be any that keep to these rules, and one draw needn't show every extreme that they name: `route_ids`: each row names 4 different experts. Among the rows of one device no expert is named by more than 48 rows, a bound that some block reaches of some device in every draw.
All inputs are finite; a program needn't handle non-finite values.
Results may differ from a plain program's by a relative error of at most 0.0058.
Values may be sent and summed in bfloat16 or wider, within the bound.
No kernel may reach another device: no remote copies, remote signals or barrier semaphores. Data moves between devices by JAX's collectives and lax.ppermute only.
A program may use at most 128 MiB of HBM per device.

v0:
```python
import jax
import jax.numpy as jnp
from jax import lax
from jax.sharding import PartitionSpec as P


def on_device(tokens, route_ids, gate_values, w_gate_up, w_down):
    dp_count = lax.axis_size("dp")
    tok_rows, top_count = route_ids.shape
    model_width = tokens.shape[1]
    hidden_units = w_down.shape[1]
    capacity = 3 * tok_rows * top_count // (2 * dp_count)
    flat_routes = route_ids.reshape(-1)
    matched = (flat_routes[:, None] == jnp.arange(dp_count, dtype=jnp.int32)[None, :]).astype(
        jnp.int32
    )
    ranked = jnp.cumsum(matched, axis=0) - 1
    slot_index = jnp.sum(ranked * matched, axis=1)
    target = flat_routes * capacity + slot_index
    owner_token = jnp.arange(tok_rows * top_count, dtype=jnp.int32) // top_count
    source = jnp.full((dp_count * capacity,), tok_rows, jnp.int32).at[target].set(owner_token)
    padded = jnp.concatenate([tokens, jnp.zeros((1, model_width), tokens.dtype)], axis=0)
    outgoing = jnp.take(padded, source, axis=0).reshape(dp_count, capacity, model_width)
    arrived = lax.all_to_all(outgoing, "dp", split_axis=0, concat_axis=0, tiled=True)
    expert_rows = arrived.reshape(dp_count * capacity, model_width)
    projected = jnp.dot(
        expert_rows,
        lax.all_gather(w_gate_up, "fsdp", axis=1, tiled=True)[0],
        preferred_element_type=jnp.float32,
    )
    hidden = (jax.nn.silu(projected[:, :hidden_units]) * projected[:, hidden_units:]).astype(
        jnp.bfloat16
    )
    produced = jnp.dot(
        hidden,
        lax.all_gather(w_down, "fsdp", axis=2, tiled=True)[0],
        preferred_element_type=jnp.float32,
    ).astype(jnp.bfloat16)
    returned = lax.all_to_all(
        produced.reshape(dp_count, capacity, model_width),
        "dp",
        split_axis=0,
        concat_axis=0,
        tiled=True,
    )
    picked = jnp.take(returned.reshape(dp_count * capacity, model_width), target, axis=0)
    picked = picked.reshape(tok_rows, top_count, model_width)
    combined = jnp.sum(gate_values[:, :, None] * picked.astype(jnp.float32), axis=1)
    return combined.astype(jnp.bfloat16)


def solution(mesh):
    in_specs = (
        P(("dp", "fsdp"), None),
        P(("dp", "fsdp"), None),
        P(("dp", "fsdp"), None),
        P("dp", "fsdp", None),
        P("dp", None, "fsdp"),
    )
    out_specs = P(("dp", "fsdp"), None)
    return jax.shard_map(
        on_device, mesh=mesh, in_specs=in_specs, out_specs=out_specs, check_vma=False
    )
```

profile of v0, /device:TPU:10, one launch (start us, length us, event | category | flops | bytes accessed | tf_op | source)
XLA Modules:
  0.0 465.0 jit_solution(13075663889717124449)
XLA Ops:
  6.5 0.7 all-gather.3.cloned.1.call-update
  7.3 0.8 copy.14
  8.0 0.1 eq.26
  8.2 0.1 reshape.86
  8.3 1.2 reduce-window.6
  9.4 0.2 slice_reduce_fusion
  9.7 0.7 broadcast_multiply_fusion
  10.4 0.1 copy.19
  10.5 0.1 mul.41
  10.6 0.1 fusion.7
  10.7 2.4 scatter_custom_fusion
  13.2 0.1 broadcast_in_dim.33
  13.3 1.3 concatenate.3
  14.6 5.8 %gather_fusion = bf16[768,4096]{1,0:T(8,128)(2,1)} fusion(bf16[129,4096]{1,0:T(8,128)(2,1)S(1)} %concatenate.3, s32[1024]{0:T(1024)S(1)} %pad_clamp_fusion.1), kind=kCustom, calls=%fused_computation | custom fusion | bytes 12585984 | tf_op jit(solution)/shard_map/jit(_take)/gather | solution.py:23
  20.4 6.1 %broadcast_select_fusion = bf16[16,48,4096]{2,1,0:T(8,128)(2,1)} fusion(bf16[16,48,4096]{2,1,0:T(8,128)(2,1)} %bitcast.28, pred[16,48]{1,0:T(8,128)(4,1)S(1)} %broadcast_in_dim.33), kind=kLoop, calls=%fused_computation.8 | loop fusion | flops 3145728 | bytes 12583680 | tf_op jit(solution)/shard_map/jit(_take)/select_n | solution.py:23
  26.5 12.1 %all-to-all-start = ((bf16[16,48,4096]{2,1,0:T(8,128)(2,1)}), bf16[16,48,4096]{2,1,0:T(8,128)(2,1)}, u32[]{:S(2)}, u32[]{:S(2)}) async-start(bf16[16,48,4096]{2,1,0:T(8,128)(2,1)} %broadcast_select_fusion), calls=%async_computation | async-start | bytes 12582912 | tf_op jit(solution)/shard_map/all_to_all | solution.py:24
  38.6 0.0 all-gather.5.cloned.1.call-start
  38.6 0.7 all-gather.5.cloned.1.call-update
  39.3 135.6 %all-to-all-done = bf16[16,48,4096]{2,1,0:T(8,128)(2,1)} async-done(((bf16[16,48,4096]{2,1,0:T(8,128)(2,1)}), bf16[16,48,4096]{2,1,0:T(8,128)(2,1)}, u32[]{:S(2)}, u32[]{:S(2)}) %all-to-all-start) | async-done | bytes 6291488 | tf_op jit(solution)/shard_map/all_to_all | solution.py:24
  174.9 16.1 %fusion = f32[768,1536]{1,0:T(8,128)} fusion(bf16[768,4096]{1,0:T(8,128)(2,1)} %bitcast.4, bf16[1,4096,1536]{2,1,0:T(8,128)(2,1)} %all-gather.3.cloned.1.call-done), kind=kOutput, calls=%fused_computation.3 | convolution fusion | flops 9663676416 | bytes 23592960 | tf_op jit(solution)/shard_map/dot_general | solution.py:26
  191.1 65.4 %all-gather.5.cloned.1.call-done = bf16[1,768,4096]{2,1,0:T(8,128)(2,1)} async-done(((bf16[1,768,256]{2,1,0:T(8,128)(2,1)}), bf16[1,768,4096]{2,1,0:T(8,128)(2,1)}) %all-gather.5.cloned.1.call-update) | async-done | bytes 6291472 | tf_op jit(solution)/shard_map/all_gather | solution.py:36
  256.4 10.3 %convolution_convert_fusion = bf16[768,4096]{1,0:T(8,128)(2,1)} fusion(bf16[1,768,4096]{2,1,0:T(8,128)(2,1)} %all-gather.5.cloned.1.call-done, f32[768,1536]{1,0:T(8,128)} %fusion), kind=kOutput, calls=%fused_computation.6 | convolution fusion | flops 4838522880 | bytes 17301504 | tf_op jit(solution)/shard_map/dot_general | solution.py:34
  266.7 12.5 %all-to-all-start.1 = ((bf16[16,48,4096]{2,1,0:T(8,128)(2,1)}), bf16[16,48,4096]{2,1,0:T(8,128)(2,1)}, u32[]{:S(2)}, u32[]{:S(2)}) async-start(bf16[16,48,4096]{2,1,0:T(8,128)(2,1)} %bitcast.29), calls=%async_computation.1 | async-start | bytes 12582912 | tf_op jit(solution)/shard_map/all_to_all | solution.py:39
  279.2 0.1 reduce_sum.23
  279.3 0.1 copy.17
  279.4 0.1 copy.18
  279.5 0.0 copy-done.1
  279.5 0.1 copy.13
  279.7 146.8 %all-to-all-done.1 = bf16[16,48,4096]{2,1,0:T(8,128)(2,1)} async-done(((bf16[16,48,4096]{2,1,0:T(8,128)(2,1)}), bf16[16,48,4096]{2,1,0:T(8,128)(2,1)}, u32[]{:S(2)}, u32[]{:S(2)}) %all-to-all-start.1) | async-done | bytes 6291488 | tf_op jit(solution)/shard_map/all_to_all | solution.py:39
  426.5 12.2 %gather_fusion.1 = bf16[512,4096]{1,0:T(8,128)(2,1)} fusion(bf16[768,4096]{1,0:T(8,128)(2,1)} %bitcast.8, s32[1024]{0:T(1024)S(1)} %pad_clamp_fusion), kind=kCustom, calls=%fused_computation.1 | custom fusion | bytes 8390656 | tf_op jit(solution)/shard_map/jit(_take)/gather | solution.py:46
  438.6 7.2 %gather.15 = bf16[128,4,4096]{2,1,0:T(4,128)(2,1)} reshape(bf16[512,4096]{1,0:T(8,128)(2,1)} %gather_fusion.1) | data formatting | bytes 8388608 | tf_op jit(solution)/shard_map/jit(_take)/gather | solution.py:46
  445.8 12.3 %multiply_reduce_fusion = bf16[128,4096]{1,0:T(8,128)(2,1)} fusion(bf16[128,4,4096]{2,1,0:T(4,128)(2,1)} %gather.15, f32[128,4]{1,0:T(8,128)S(1)} %copy.13, pred[128,4]{1,0:T(8,128)(4,1)S(1)} %copy.18), kind=kLoop, calls=%fused_computation.5 | loop fusion | flops 7864320 | bytes 5245440 | tf_op jit(solution)/shard_map/reduce_sum | solution.py:48
  (15 shorter events, 0.1 us)
Async XLA Ops:
  6.5 168.4 %all-gather.3.cloned.1.call-start = ((), (), s32[]{:S(2)}) async-start(), calls=%async_computation.2 | async-start | bytes 13369344 | tf_op jit(solution)/shard_map/all_gather | solution.py:28
  26.5 148.4 %all-to-all-start = ((bf16[16,48,4096]{2,1,0:T(8,128)(2,1)}), bf16[16,48,4096]{2,1,0:T(8,128)(2,1)}, u32[]{:S(2)}, u32[]{:S(2)}) async-start(bf16[16,48,4096]{2,1,0:T(8,128)(2,1)} %broadcast_select_fusion), calls=%async_computation | async-start | bytes 12582912 | tf_op jit(solution)/shard_map/all_to_all | solution.py:24
  38.6 217.9 %all-gather.5.cloned.1.call-start = ((), (), s32[]{:S(2)}) async-start(), calls=%async_computation.3 | async-start | bytes 6684672 | tf_op jit(solution)/shard_map/all_gather | solution.py:36
  266.7 12.7 %copy-start = (s32[128,4]{0,1:T(4,128)S(1)}, s32[128,4]{0,1:T(4,128)}, u32[]{:S(2)}) copy-start(s32[128,4]{0,1:T(4,128)} %param.6) | copy-start | bytes 6148
  266.7 12.8 %copy-start.1 = (f32[128,4]{0,1:T(4,128)S(1)}, f32[128,4]{0,1:T(4,128)}, u32[]{:S(2)}) copy-start(f32[128,4]{0,1:T(4,128)} %param.7) | copy-start | bytes 6148
  266.7 159.8 %all-to-all-start.1 = ((bf16[16,48,4096]{2,1,0:T(8,128)(2,1)}), bf16[16,48,4096]{2,1,0:T(8,128)(2,1)}, u32[]{:S(2)}, u32[]{:S(2)}) async-start(bf16[16,48,4096]{2,1,0:T(8,128)(2,1)} %bitcast.29), calls=%async_computation.1 | async-start | bytes 12582912 | tf_op jit(solution)/shard_map/all_to_all | solution.py:39
Sparse Core Ops, SparseCore 0:
  9.2 161.6 all-gather.2
  172.6 83.7 all-gather.4
where the time goes:
time: 469 us; the launch traced here: 465 us
  waiting for transfers between devices  349 us (74%)
  local copies, waits for them, and re-layouts  30.8 us (7%)
  matrix products  26.4 us (6%)
  starting transfers between devices  24.6 us (5%)
  other arithmetic  20.5 us (4%)
  between operations  13.5 us (3%)
    all_to_all x1, waiting for transfers between devices, on_device(): lax.all_to_all(produced.reshape(dp_count, capacity, model_width), 'dp', s...  147 us
    all_to_all x1, waiting for transfers between devices, on_device(): lax.all_to_all(outgoing, 'dp', split_axis=0, concat_axis=0, tiled=True)  136 us
    all_gather x1, waiting for transfers between devices, on_device(): lax.all_gather(w_down, 'fsdp', axis=2, tiled=True)[0]  65.4 us
    gather x2, local copies, waits for them, and re-layouts, on_device(): jnp.take(returned.reshape(dp_count * capacity, model_width), target, axis=0)  19.3 us
    dot_general x1, matrix products, on_device(): jnp.dot(expert_rows, lax.all_gather(w_gate_up, 'fsdp', axis=1, tiled=True...  16.1 us
    all_to_all x1, starting transfers between devices, on_device(): lax.all_to_all(produced.reshape(dp_count, capacity, model_width), 'dp', s...  12.5 us
    reduce_sum x1, other arithmetic, on_device(): jnp.sum(gate_values[:, :, None] * picked.astype(jnp.float32), axis=1)  12.3 us
    all_to_all x1, starting transfers between devices, on_device(): lax.all_to_all(outgoing, 'dp', split_axis=0, concat_axis=0, tiled=True)  12.1 us
  transfers between devices with their start and end apart: 4, of which 3 were waited for; matrix products, arithmetic and copies ran while one was open for 8% of the time, Pallas kernels for 0%

commit v1 on v0

v1 whole, which is shorter than its diff:
```python
import jax
import jax.numpy as jnp
from jax import lax
from jax.experimental import pallas as pl
from jax.experimental.pallas import tpu as pltpu
from jax.sharding import Mesh, PartitionSpec as P

BF, F32 = jnp.bfloat16, jnp.float32
ZH, YS = 4, 4
CHUNKS = 4
PARAMS = pltpu.CompilerParams(vmem_limit_bytes=48 << 20)


def ring(step):
    return [(i, (i + step) % ZH) for i in range(ZH)]


def plan_kernel(group_ref, *refs):
    metas, (pick_ref, high_ref, low_ref) = refs[:ZH], refs[ZH:]
    rows = metas[0].shape[1]
    slots = pick_ref.shape[1] // YS
    group = group_ref[0]
    named, gates = [], []
    for k in range(ZH):
        ids, weights = metas[k][0:4, :], metas[k][4:8, :]
        for y in range(YS):
            match = ids == (group * YS + y).astype(F32)
            named.append(jnp.sum(match.astype(F32), axis=0, keepdims=True))
            gates.append(jnp.sum(jnp.where(match, weights, 0.0), axis=0, keepdims=True))
    stacked = jnp.concatenate(named, axis=0)
    earlier = lax.broadcasted_iota(jnp.int32, (rows, rows), 0)
    later = lax.broadcasted_iota(jnp.int32, (rows, rows), 1)
    rank = jnp.dot(
        stacked.astype(BF), (earlier < later).astype(F32).astype(BF), preferred_element_type=F32
    )
    slot = lax.broadcasted_iota(jnp.int32, (slots, rows), 0).astype(F32)
    for k in range(ZH):
        for y in range(YS):
            i = k * YS + y
            here = (rank[i : i + 1, :] == slot) & (named[i] > 0.5)
            at = slice(y * slots, (y + 1) * slots)
            scaled = jnp.where(here, gates[i], 0.0)
            high = scaled.astype(BF)
            pick_ref[k, at, :] = here.astype(F32).astype(BF)
            high_ref[k, at, :] = high
            low_ref[k, at, :] = (scaled - high.astype(F32)).astype(BF)


def plan(group, metas, slots):
    rows = metas[0].shape[1]
    out = jax.ShapeDtypeStruct((ZH, YS * slots, rows), BF)
    return pl.pallas_call(
        plan_kernel,
        out_shape=(out, out, out),
        in_specs=[pl.BlockSpec(memory_space=pltpu.SMEM)] + [pl.BlockSpec()] * ZH,
        compiler_params=PARAMS,
        name="plan",
    )(group, *metas)


def gather_kernel(pick_ref, *refs):
    blocks, out_ref = refs[:ZH], refs[ZH]
    slots = out_ref.shape[2]
    for k in range(ZH):
        got = jnp.dot(pick_ref[k], blocks[k][...], preferred_element_type=F32).astype(BF)
        for y in range(YS):
            out_ref[y, k] = got[y * slots : (y + 1) * slots]


def gather(pick, blocks, slots):
    width = blocks[0].shape[1]
    return pl.pallas_call(
        gather_kernel,
        out_shape=jax.ShapeDtypeStruct((YS, ZH, slots, width), BF),
        compiler_params=PARAMS,
        name="gather",
    )(pick, *blocks)


def first_kernel(x_ref, wg_ref, wu_ref, *refs):
    g = jnp.dot(x_ref[...], wg_ref[...], preferred_element_type=F32)
    u = jnp.dot(x_ref[...], wu_ref[...], preferred_element_type=F32)
    n_in = len(refs) - (1 if refs[-1].dtype == BF else 2)
    if n_in:
        g, u = g + refs[0][...], u + refs[1][...]
    if refs[-1].dtype == BF:
        refs[-1][...] = (g / (1.0 + jnp.exp(-g)) * u).astype(BF)
    else:
        refs[-2][...], refs[-1][...] = g, u


def first(x, w, at, sums, last):
    rows, width = x.shape
    half = w.shape[1] // 2
    tile = 256
    steps = half // tile
    part = pl.BlockSpec((rows, tile), lambda j: (0, j))
    shape = jax.ShapeDtypeStruct((rows, half), BF if last else F32)
    return pl.pallas_call(
        first_kernel,
        grid=(steps,),
        out_shape=shape if last else (shape, shape),
        in_specs=[
            pl.BlockSpec((rows, width), lambda j: (0, 0)),
            pl.BlockSpec((width, tile), lambda j: (at, j)),
            pl.BlockSpec((width, tile), lambda j: (at, j + steps)),
        ]
        + [part] * len(sums),
        out_specs=part if last else (part, part),
        compiler_params=PARAMS,
        name="first",
    )(x, w, w, *sums)


def second_kernel(h_ref, w_ref, out_ref):
    out_ref[...] = jnp.dot(h_ref[...], w_ref[...], preferred_element_type=F32).astype(BF)


def second(hidden, w, at, width):
    rows, inner = hidden.shape
    tile = 256
    steps = width // tile
    return pl.pallas_call(
        second_kernel,
        grid=(steps,),
        out_shape=jax.ShapeDtypeStruct((rows, width), BF),
        in_specs=[
            pl.BlockSpec((rows, inner), lambda j: (0, 0)),
            pl.BlockSpec((pl.Squeezed(), inner, tile), lambda j: (at * steps + j, 0, 0)),
        ],
        out_specs=pl.BlockSpec((rows, tile), lambda j: (0, j)),
        compiler_params=PARAMS,
        name="second",
    )(hidden, w)


def combine_kernel(high_ref, low_ref, rows_ref, *outs):
    for k in range(ZH):
        rows = jnp.concatenate([rows_ref[y, k] for y in range(YS)], axis=0)
        total = sum(
            lax.dot_general(
                s[k], rows, (((0,), (0,)), ((), ())), preferred_element_type=F32
            )
            for s in (high_ref, low_ref)
        )
        outs[k][...] = total.astype(outs[k].dtype)


def combine(high, low, rows, tok_rows):
    width = rows.shape[-1]
    return pl.pallas_call(
        combine_kernel,
        out_shape=tuple(
            jax.ShapeDtypeStruct((tok_rows, width), F32 if k == 0 else BF) for k in range(ZH)
        ),
        compiler_params=PARAMS,
        name="combine",
    )(high, low, rows)


def on_device(tokens, route_ids, gate_values, w_gate_up, w_down):
    tok_rows, top = route_ids.shape
    model = tokens.shape[1]
    slots = 3 * tok_rows * top // (2 * ZH * YS)
    width = model // CHUNKS
    meta = jnp.concatenate([route_ids.astype(F32).T, gate_values.T], axis=0)
    metas = [meta] + [lax.ppermute(meta, "zh", ring(k)) for k in range(1, ZH)]
    w_in = lax.all_gather(w_gate_up[0], "fsdp", axis=0, tiled=True)
    w_out = lax.all_gather(w_down[0], "fsdp", axis=0, tiled=False)
    group = lax.axis_index("zh").reshape(1)
    pick, high, low = plan(group, metas, slots)

    sums = ()
    for c in range(CHUNKS):
        own = tokens[:, c * width : (c + 1) * width]
        blocks = [own] + [lax.ppermute(own, "zh", ring(k)) for k in range(1, ZH)]
        sent = gather(pick, blocks, slots).reshape(YS, ZH * slots, width)
        rows = lax.all_to_all(sent, "y", split_axis=0, concat_axis=0, tiled=True)
        sums = first(rows.reshape(-1, width), w_in, c, sums, c == CHUNKS - 1)
    hidden = sums

    outs = []
    for c in range(CHUNKS):
        made = second(hidden, w_out, c, width).reshape(YS, ZH * slots, width)
        back = lax.all_to_all(made, "y", split_axis=0, concat_axis=0, tiled=True)
        parts = combine(high, low, back.reshape(YS, ZH, slots, width), tok_rows)
        total = parts[0]
        for k in range(1, ZH):
            total = total + lax.ppermute(parts[k], "zh", ring(-k)).astype(F32)
        outs.append(total.astype(BF))
    return jnp.concatenate(outs, axis=1)


def solution(mesh):
    split = Mesh(mesh.devices.reshape(ZH, YS, -1), ("zh", "y", "fsdp"))
    every, owner = ("zh", "y", "fsdp"), ("zh", "y")
    in_specs = (P(every, None),) * 3 + (P(owner, "fsdp", None), P(owner, None, "fsdp"))
    return jax.shard_map(
        on_device, mesh=split, in_specs=in_specs, out_specs=P(every, None), check_vma=False
    )
```

time: 469 us -> 417 us (0.89)
  waiting for transfers between devices: 349 us -> 214 us
  starting transfers between devices: 24.6 us -> 106 us
  Pallas kernels: 0 us -> 51.9 us
  matrix products: 26.4 us -> 0 us
  other arithmetic: 20.5 us -> 3.77 us
  local copies, waits for them, and re-layouts: 30.8 us -> 25.7 us
    all_to_all x2 -> x8, waiting for transfers between devices: 282 us -> 42.2 us  [the longest x4 42.2 us: on_device(): back = lax.all_to_all(made, 'y', split_axis=0, concat_axis=0, tiled=True)]
    ppermute x0 -> x27, waiting for transfers between devices: none -> 149 us  [the longest x12 74.3 us: on_device(): total = total + lax.ppermute(parts[k], 'zh', ring(-k)).astype(F32)]
    ppermute x0 -> x27, starting transfers between devices: none -> 66 us  [the longest x12 33.6 us: on_device(): blocks = [own] + [lax.ppermute(own, 'zh', ring(k)) for k in range(1, ZH)]]
    pallas_call x0 -> x17, Pallas kernels: none -> 51.9 us  [the longest x4 24.8 us: first(): pl.pallas_call(first_kernel, grid=(steps,), out_shape=shape if last else...]
    all_gather x2, waiting for transfers between devices: 65.4 us -> 22 us  [the longest x1 22 us: on_device(): w_out = lax.all_gather(w_down[0], 'fsdp', axis=0, tiled=False)]
    dot_general x2 -> x0, matrix products: 26.4 us -> none  [the longest x1 16.1 us: on_device(): jnp.dot(expert_rows, lax.all_gather(w_gate_up, 'fsdp', axis=1, tiled=True...]
    gather x3 -> x0, local copies, waits for them, and re-layouts: 25.1 us -> none  [the longest x2 19.3 us: on_device(): jnp.take(returned.reshape(dp_count * capacity, model_width), target, axis=0)]
    unnamed x6 -> x64, local copies, waits for them, and re-layouts: 0.91 us -> 24.8 us
  transfers between devices with their start and end apart: 4 -> 37, of which waited for: 3 -> 18; matrix products, arithmetic and copies ran while one was open for 8% -> 1% of each run, Pallas kernels for 0% -> 12%
where the time goes in v1:
time: 417 us; the launch traced here: 415 us
  waiting for transfers between devices  214 us (51%)
  starting transfers between devices  106 us (25%)
  Pallas kernels  51.9 us (12%)
  local copies, waits for them, and re-layouts  25.7 us (6%)
  between operations  13.7 us (3%)
    ppermute x12, waiting for transfers between devices, on_device(): total = total + lax.ppermute(parts[k], 'zh', ring(-k)).astype(F32)  74.3 us
    ppermute x12, waiting for transfers between devices, on_device(): blocks = [own] + [lax.ppermute(own, 'zh', ring(k)) for k in range(1, ZH)]  53.9 us
    all_to_all x4, waiting for transfers between devices, on_device(): back = lax.all_to_all(made, 'y', split_axis=0, concat_axis=0, tiled=True)  42.2 us
    ppermute x12, starting transfers between devices, on_device(): blocks = [own] + [lax.ppermute(own, 'zh', ring(k)) for k in range(1, ZH)]  33.6 us
    ppermute x12, starting transfers between devices, on_device(): total = total + lax.ppermute(parts[k], 'zh', ring(-k)).astype(F32)  30 us
    pallas_call x4, Pallas kernels, first(): pl.pallas_call(first_kernel, grid=(steps,), out_shape=shape if last else...  24.8 us
    unnamed x64, local copies, waits for them, and re-layouts  24.8 us
    all_gather x1, waiting for transfers between devices, on_device(): w_out = lax.all_gather(w_down[0], 'fsdp', axis=0, tiled=False)  22 us
  transfers between devices with their start and end apart: 37, of which 18 were waited for; matrix products, arithmetic and copies ran while one was open for 1% of the time, Pallas kernels for 12%

profile of v1, /device:TPU:10, one launch (start us, length us, event | category | flops | bytes accessed | tf_op | source)
XLA Modules:
  0.0 415.3 jit_solution(5499139798031674164)
XLA Ops:
  12.2 5.4 %collective-permute-start.13 = (bf16[128,1024]{1,0:T(8,128)(2,1)S(1)}, bf16[128,1024]{1,0:T(8,128)(2,1)S(1)}, u32[]{:S(2)}, u32[]{:S(2)}) collective-permute-start(bf16[128,1024]{1,0:T(8,128)(2,1)S(1)} %get-tuple-element.55.refs_0_), channel_id=1, source_target_pairs={{0,128},{64,192},{128,0},{192,64},{1,129},{65,193},{129,1},{193,65... | collective-permute-start | bytes 786440 | tf_op jit(solution)/shard_map/ppermute | solution.py:176
  22.7 16.0 %collective-permute-done.refs_1_ = f32[8,128]{1,0:T(8,128)S(1)} collective-permute-done((f32[8,128]{1,0:T(8,128)S(1)}, f32[8,128]{1,0:T(8,128)S(1)}, u32[]{:S(2)}, u32[]{:S(2)}) %collective-permute-start) | collective-permute-done | bytes 4128 | tf_op jit(solution)/shard_map/ppermute | solution.py:167
  38.8 4.5 %collective-permute-done.2.refs_3_ = f32[8,128]{1,0:T(8,128)S(1)} collective-permute-done((f32[8,128]{1,0:T(8,128)S(1)}, f32[8,128]{1,0:T(8,128)S(1)}, u32[]{:S(2)}, u32[]{:S(2)}) %collective-permute-start.2) | collective-permute-done | bytes 4128 | tf_op jit(solution)/shard_map/ppermute | solution.py:167
  45.3 4.9 %all-to-all-start.3 = ((bf16[4,192,1024]{2,1,0:T(8,128)(2,1)}), bf16[4,192,1024]{2,1,0:T(8,128)(2,1)S(1)}, u32[]{:S(2)}, u32[]{:S(2)}) async-start(bf16[4,192,1024]{2,1,0:T(8,128)(2,1)} %bitcast.10), calls=%async_computation.3 | async-start | bytes 3145728 | tf_op jit(solution)/shard_map/all_to_all | solution.py:178
  50.2 4.6 %collective-permute-start.10 = (bf16[128,1024]{1,0:T(8,128)(2,1)S(1)}, bf16[128,1024]{1,0:T(8,128)(2,1)S(1)}, u32[]{:S(2)}, u32[]{:S(2)}) collective-permute-start(bf16[128,1024]{1,0:T(8,128)(2,1)S(1)} %get-tuple-element.58.refs_0_), channel_id=1, source_target_pairs={{0,128},{64,192},{128,0},{192,64},{1,129},{65,193},{129,1},{193,65... | collective-permute-start | bytes 786440 | tf_op jit(solution)/shard_map/ppermute | solution.py:176
  57.7 14.3 %collective-permute-done.10.refs_2_ = bf16[128,1024]{1,0:T(8,128)(2,1)S(1)} collective-permute-done((bf16[128,1024]{1,0:T(8,128)(2,1)S(1)}, bf16[128,1024]{1,0:T(8,128)(2,1)S(1)}, u32[]{:S(2)}, u32[]{:S(2)}) %collective-permute-start.10) | collective-permute-done | bytes 262176 | tf_op jit(solution)/shard_map/ppermute | solution.py:176
  77.8 4.8 %all-to-all-start.2 = ((bf16[4,192,1024]{2,1,0:T(8,128)(2,1)}), bf16[4,192,1024]{2,1,0:T(8,128)(2,1)S(1)}, u32[]{:S(2)}, u32[]{:S(2)}) async-start(bf16[4,192,1024]{2,1,0:T(8,128)(2,1)} %bitcast.8), calls=%async_computation.2 | async-start | bytes 3145728 | tf_op jit(solution)/shard_map/all_to_all | solution.py:178
  86.7 3.8 collective-permute-start.8
  90.5 15.0 %collective-permute-done.6.refs_1_ = bf16[128,1024]{1,0:T(8,128)(2,1)S(1)} collective-permute-done((bf16[128,1024]{1,0:T(8,128)(2,1)}, bf16[128,1024]{1,0:T(8,128)(2,1)S(1)}, u32[]{:S(2)}, u32[]{:S(2)}) %collective-permute-start.6) | collective-permute-done | bytes 262176 | tf_op jit(solution)/shard_map/ppermute | solution.py:176
  105.4 6.8 %collective-permute-done.8.refs_3_ = bf16[128,1024]{1,0:T(8,128)(2,1)S(1)} collective-permute-done((bf16[128,1024]{1,0:T(8,128)(2,1)}, bf16[128,1024]{1,0:T(8,128)(2,1)S(1)}, u32[]{:S(2)}, u32[]{:S(2)}) %collective-permute-start.8) | collective-permute-done | bytes 262176 | tf_op jit(solution)/shard_map/ppermute | solution.py:176
  115.8 4.8 %all-to-all-start.1 = ((bf16[4,192,1024]{2,1,0:T(8,128)(2,1)}), bf16[4,192,1024]{2,1,0:T(8,128)(2,1)S(1)}, u32[]{:S(2)}, u32[]{:S(2)}) async-start(bf16[4,192,1024]{2,1,0:T(8,128)(2,1)} %bitcast.6), calls=%async_computation.1 | async-start | bytes 3145728 | tf_op jit(solution)/shard_map/all_to_all | solution.py:178
  123.7 3.8 collective-permute-start.4
  127.5 4.6 %collective-permute-done.3.refs_1_ = bf16[128,1024]{1,0:T(8,128)(2,1)S(1)} collective-permute-done((bf16[128,1024]{1,0:T(8,128)(2,1)}, bf16[128,1024]{1,0:T(8,128)(2,1)S(1)}, u32[]{:S(2)}, u32[]{:S(2)}) %collective-permute-start.3) | collective-permute-done | bytes 262176 | tf_op jit(solution)/shard_map/ppermute | solution.py:176
  132.0 10.4 %collective-permute-done.4.refs_2_ = bf16[128,1024]{1,0:T(8,128)(2,1)S(1)} collective-permute-done((bf16[128,1024]{1,0:T(8,128)(2,1)}, bf16[128,1024]{1,0:T(8,128)(2,1)S(1)}, u32[]{:S(2)}, u32[]{:S(2)}) %collective-permute-start.4) | collective-permute-done | bytes 262176 | tf_op jit(solution)/shard_map/ppermute | solution.py:176
  147.3 4.8 %all-to-all-start = ((bf16[4,192,1024]{2,1,0:T(8,128)(2,1)}), bf16[4,192,1024]{2,1,0:T(8,128)(2,1)S(1)}, u32[]{:S(2)}, u32[]{:S(2)}) async-start(bf16[4,192,1024]{2,1,0:T(8,128)(2,1)} %bitcast.3), calls=%async_computation | async-start | bytes 3145728 | tf_op jit(solution)/shard_map/all_to_all | solution.py:178
  153.5 5.7 %first.4 = (f32[768,768]{1,0:T(8,128)S(1)}, f32[768,768]{1,0:T(8,128)}) custom-call(bf16[768,1024]{1,0:T(8,128)(2,1)S(1)} %bitcast.22, bf16[4096,1536]{1,0:T(8,128)(2,1)} %bitcast.32, bf16[4096,1536]{1,0:T(8,128)(2,1)} %bitcast.33), custom_call_target="tpu_custom_call" | custom-call | tf_op jit(solution)/shard_map/first/pallas_call | solution.py:99
  160.7 7.0 %first.5 = (f32[768,768]{1,0:T(8,128)S(1)}, f32[768,768]{1,0:T(8,128)}) custom-call(bf16[768,1024]{1,0:T(8,128)(2,1)S(1)} %bitcast.30, bf16[4096,1536]{1,0:T(8,128)(2,1)} %bitcast.34, bf16[4096,1536]{1,0:T(8,128)(2,1)} %bitcast.35, f32[768,768]{1,0:T(8,128)} %copy-done.18, f32[768,768]{1,0:T(8,128)} %get-tuple-element.34.refs_1_), custom_call_target="tpu_custom_call" | custom-call | tf_op jit(solution)/shard_map/first/pallas_call | solution.py:99
  169.1 7.0 %first.6 = (f32[768,768]{1,0:T(8,128)S(1)}, f32[768,768]{1,0:T(8,128)}) custom-call(bf16[768,1024]{1,0:T(8,128)(2,1)S(1)} %bitcast.31, bf16[4096,1536]{1,0:T(8,128)(2,1)} %bitcast.36, bf16[4096,1536]{1,0:T(8,128)(2,1)} %bitcast.37, f32[768,768]{1,0:T(8,128)} %copy-done.17, f32[768,768]{1,0:T(8,128)} %get-tuple-element.36.refs_1_), custom_call_target="tpu_custom_call" | custom-call | tf_op jit(solution)/shard_map/first/pallas_call | solution.py:99
  179.2 5.1 %first.7.h_ref = bf16[768,768]{1,0:T(8,128)(2,1)S(1)} custom-call(bf16[768,1024]{1,0:T(8,128)(2,1)S(1)} %bitcast.21, bf16[4096,1536]{1,0:T(8,128)(2,1)} %bitcast.38, bf16[4096,1536]{1,0:T(8,128)(2,1)} %bitcast.39, f32[768,768]{1,0:T(8,128)S(1)} %copy-done.16, f32[768,768]{1,0:T(8,128)} %get-tuple-element.38.refs_1_), custom_call_target="tpu_custom_call" | custom-call | tf_op jit(solution)/shard_map/first/pallas_call | solution.py:99
  184.3 22.0 %all-gather.4.cloned.1.call-done.w_ref = bf16[16,768,256]{2,1,0:T(8,128)(2,1)} async-done(((bf16[1,768,256]{2,1,0:T(8,128)(2,1)}), bf16[16,768,256]{2,1,0:T(8,128)(2,1)}) %all-gather.4.cloned.1.call-update) | async-done | bytes 6291472 | tf_op jit(solution)/shard_map/all_gather | solution.py:169
  211.1 4.8 %all-to-all-start.4 = ((bf16[4,192,1024]{2,1,0:T(8,128)(2,1)}), bf16[4,192,1024]{2,1,0:T(8,128)(2,1)S(1)}, u32[]{:S(2)}, u32[]{:S(2)}) async-start(bf16[4,192,1024]{2,1,0:T(8,128)(2,1)} %bitcast.29), calls=%async_computation.4 | async-start | bytes 3145728 | tf_op jit(solution)/shard_map/all_to_all | solution.py:185
  220.6 14.9 %all-to-all-done.4 = bf16[4,192,1024]{2,1,0:T(8,128)(2,1)S(1)} async-done(((bf16[4,192,1024]{2,1,0:T(8,128)(2,1)}), bf16[4,192,1024]{2,1,0:T(8,128)(2,1)S(1)}, u32[]{:S(2)}, u32[]{:S(2)}) %all-to-all-start.4) | async-done | bytes 1572896 | tf_op jit(solution)/shard_map/all_to_all | solution.py:185
  236.7 5.0 %all-to-all-start.5 = ((bf16[4,192,1024]{2,1,0:T(8,128)(2,1)}), bf16[4,192,1024]{2,1,0:T(8,128)(2,1)S(1)}, u32[]{:S(2)}, u32[]{:S(2)}) async-start(bf16[4,192,1024]{2,1,0:T(8,128)(2,1)} %bitcast.28), calls=%async_computation.5 | async-start | bytes 3145728 | tf_op jit(solution)/shard_map/all_to_all | solution.py:185
  246.4 14.1 %all-to-all-done.5 = bf16[4,192,1024]{2,1,0:T(8,128)(2,1)S(1)} async-done(((bf16[4,192,1024]{2,1,0:T(8,128)(2,1)}), bf16[4,192,1024]{2,1,0:T(8,128)(2,1)S(1)}, u32[]{:S(2)}, u32[]{:S(2)}) %all-to-all-start.5) | async-done | bytes 1572896 | tf_op jit(solution)/shard_map/all_to_all | solution.py:185
  261.7 5.0 %all-to-all-start.6 = ((bf16[4,192,1024]{2,1,0:T(8,128)(2,1)}), bf16[4,192,1024]{2,1,0:T(8,128)(2,1)S(1)}, u32[]{:S(2)}, u32[]{:S(2)}) async-start(bf16[4,192,1024]{2,1,0:T(8,128)(2,1)} %bitcast.27), calls=%async_computation.6 | async-start | bytes 3145728 | tf_op jit(solution)/shard_map/all_to_all | solution.py:185
  271.4 13.2 %all-to-all-done.6 = bf16[4,192,1024]{2,1,0:T(8,128)(2,1)S(1)} async-done(((bf16[4,192,1024]{2,1,0:T(8,128)(2,1)}), bf16[4,192,1024]{2,1,0:T(8,128)(2,1)S(1)}, u32[]{:S(2)}, u32[]{:S(2)}) %all-to-all-start.6) | async-done | bytes 1572896 | tf_op jit(solution)/shard_map/all_to_all | solution.py:185
  284.5 5.8 %all-to-all-start.7 = ((bf16[4,192,1024]{2,1,0:T(8,128)(2,1)}), bf16[4,192,1024]{2,1,0:T(8,128)(2,1)}, u32[]{:S(2)}, u32[]{:S(2)}) async-start(bf16[4,192,1024]{2,1,0:T(8,128)(2,1)} %bitcast.26), calls=%async_computation.7 | async-start | bytes 3145728 | tf_op jit(solution)/shard_map/all_to_all | solution.py:185
  300.9 4.1 collective-permute-start.18
  313.3 50.0 %collective-permute-done.15 = bf16[128,1024]{1,0:T(8,128)(2,1)} collective-permute-done((bf16[128,1024]{1,0:T(8,128)(2,1)}, bf16[128,1024]{1,0:T(8,128)(2,1)}, u32[]{:S(2)}, u32[]{:S(2)}) %collective-permute-start.15) | collective-permute-done | bytes 262176 | tf_op jit(solution)/shard_map/ppermute | solution.py:189
  382.9 4.8 %collective-permute-done.22 = bf16[128,1024]{1,0:T(8,128)(2,1)S(1)} collective-permute-done((bf16[128,1024]{1,0:T(8,128)(2,1)S(1)}, bf16[128,1024]{1,0:T(8,128)(2,1)S(1)}, u32[]{:S(2)}, u32[]{:S(2)}) %collective-permute-start.22) | collective-permute-done | bytes 262176 | tf_op jit(solution)/shard_map/ppermute | solution.py:189
  387.7 3.9 collective-permute-done.23
  391.7 12.8 %collective-permute-done.25 = bf16[128,1024]{1,0:T(8,128)(2,1)S(1)} collective-permute-done((bf16[128,1024]{1,0:T(8,128)(2,1)S(1)}, bf16[128,1024]{1,0:T(8,128)(2,1)S(1)}, u32[]{:S(2)}, u32[]{:S(2)}) %collective-permute-start.25) | collective-permute-done | bytes 262176 | tf_op jit(solution)/shard_map/ppermute | solution.py:189
  (133 shorter events, 108.0 us)
Async XLA Ops:
  6.5 145.5 %all-gather.6.cloned.1.call-start = ((), (), s32[]{:S(2)}) async-start(), calls=%async_computation.9 | async-start | bytes 13369344 | tf_op jit(solution)/shard_map/all_gather | solution.py:168
  7.3 199.1 %all-gather.4.cloned.1.call-start = ((), (), s32[]{:S(2)}) async-start(), calls=%async_computation.8 | async-start | bytes 6684672 | tf_op jit(solution)/shard_map/all_gather | solution.py:169
  8.9 34.6 %collective-permute-start.12 = (bf16[128,1024]{1,0:T(8,128)(2,1)S(1)}, bf16[128,1024]{1,0:T(8,128)(2,1)S(1)}, u32[]{:S(2)}, u32[]{:S(2)}) collective-permute-start(bf16[128,1024]{1,0:T(8,128)(2,1)S(1)} %get-tuple-element.55.refs_0_), channel_id=1, source_target_pairs={{0,64},{64,128},{128,192},{192,0},{1,65},{65,129},{129,193},{193,1... | collective-permute-start | bytes 786440 | tf_op jit(solution)/shard_map/ppermute | solution.py:176
  12.2 31.3 %collective-permute-start.13 = (bf16[128,1024]{1,0:T(8,128)(2,1)S(1)}, bf16[128,1024]{1,0:T(8,128)(2,1)S(1)}, u32[]{:S(2)}, u32[]{:S(2)}) collective-permute-start(bf16[128,1024]{1,0:T(8,128)(2,1)S(1)} %get-tuple-element.55.refs_0_), channel_id=1, source_target_pairs={{0,128},{64,192},{128,0},{192,64},{1,129},{65,193},{129,1},{193,65... | collective-permute-start | bytes 786440 | tf_op jit(solution)/shard_map/ppermute | solution.py:176
  17.6 25.9 %collective-permute-start.14 = (bf16[128,1024]{1,0:T(8,128)(2,1)S(1)}, bf16[128,1024]{1,0:T(8,128)(2,1)S(1)}, u32[]{:S(2)}, u32[]{:S(2)}) collective-permute-start(bf16[128,1024]{1,0:T(8,128)(2,1)S(1)} %get-tuple-element.55.refs_0_), channel_id=1, source_target_pairs={{0,192},{64,0},{128,64},{192,128},{1,193},{65,1},{129,65},{193,129... | collective-permute-start | bytes 786440 | tf_op jit(solution)/shard_map/ppermute | solution.py:176
  20.3 18.5 %collective-permute-start = (f32[8,128]{1,0:T(8,128)S(1)}, f32[8,128]{1,0:T(8,128)S(1)}, u32[]{:S(2)}, u32[]{:S(2)}) collective-permute-start(f32[8,128]{1,0:T(8,128)S(1)} %pad_maximum_fusion.1.refs_0_), channel_id=1, source_target_pairs={{0,64},{64,128},{128,192},{192,0},{1,65},{65,129},{129,193},{193,1... | collective-permute-start | bytes 12296 | tf_op jit(solution)/shard_map/ppermute | solution.py:167
  20.6 18.1 %collective-permute-start.1 = (f32[8,128]{1,0:T(8,128)S(1)}, f32[8,128]{1,0:T(8,128)S(1)}, u32[]{:S(2)}, u32[]{:S(2)}) collective-permute-start(f32[8,128]{1,0:T(8,128)S(1)} %pad_maximum_fusion.1.refs_0_), channel_id=1, source_target_pairs={{0,128},{64,192},{128,0},{192,64},{1,129},{65,193},{129,1},{193,65... | collective-permute-start | bytes 12296 | tf_op jit(solution)/shard_map/ppermute | solution.py:167
  45.3 31.3 %all-to-all-start.3 = ((bf16[4,192,1024]{2,1,0:T(8,128)(2,1)}), bf16[4,192,1024]{2,1,0:T(8,128)(2,1)S(1)}, u32[]{:S(2)}, u32[]{:S(2)}) async-start(bf16[4,192,1024]{2,1,0:T(8,128)(2,1)} %bitcast.10), calls=%async_computation.3 | async-start | bytes 3145728 | tf_op jit(solution)/shard_map/all_to_all | solution.py:178
  50.2 21.9 %collective-permute-start.10 = (bf16[128,1024]{1,0:T(8,128)(2,1)S(1)}, bf16[128,1024]{1,0:T(8,128)(2,1)S(1)}, u32[]{:S(2)}, u32[]{:S(2)}) collective-permute-start(bf16[128,1024]{1,0:T(8,128)(2,1)S(1)} %get-tuple-element.58.refs_0_), channel_id=1, source_target_pairs={{0,128},{64,192},{128,0},{192,64},{1,129},{65,193},{129,1},{193,65... | collective-permute-start | bytes 786440 | tf_op jit(solution)/shard_map/ppermute | solution.py:176
  54.8 17.8 %collective-permute-start.11 = (bf16[128,1024]{1,0:T(8,128)(2,1)S(1)}, bf16[128,1024]{1,0:T(8,128)(2,1)S(1)}, u32[]{:S(2)}, u32[]{:S(2)}) collective-permute-start(bf16[128,1024]{1,0:T(8,128)(2,1)S(1)} %get-tuple-element.58.refs_0_), channel_id=1, source_target_pairs={{0,192},{64,0},{128,64},{192,128},{1,193},{65,1},{129,65},{193,129... | collective-permute-start | bytes 786440 | tf_op jit(solution)/shard_map/ppermute | solution.py:176
  56.0 18.9 %collective-permute-start.9 = (bf16[128,1024]{1,0:T(8,128)(2,1)S(1)}, bf16[128,1024]{1,0:T(8,128)(2,1)S(1)}, u32[]{:S(2)}, u32[]{:S(2)}) collective-permute-start(bf16[128,1024]{1,0:T(8,128)(2,1)S(1)} %get-tuple-element.58.refs_0_), channel_id=1, source_target_pairs={{0,64},{64,128},{128,192},{192,0},{1,65},{65,129},{129,193},{193,1... | collective-permute-start | bytes 786440 | tf_op jit(solution)/shard_map/ppermute | solution.py:176
  77.8 38.0 %all-to-all-start.2 = ((bf16[4,192,1024]{2,1,0:T(8,128)(2,1)}), bf16[4,192,1024]{2,1,0:T(8,128)(2,1)S(1)}, u32[]{:S(2)}, u32[]{:S(2)}) async-start(bf16[4,192,1024]{2,1,0:T(8,128)(2,1)} %bitcast.8), calls=%async_computation.2 | async-start | bytes 3145728 | tf_op jit(solution)/shard_map/all_to_all | solution.py:178
  82.6 22.8 %collective-permute-start.6 = (bf16[128,1024]{1,0:T(8,128)(2,1)}, bf16[128,1024]{1,0:T(8,128)(2,1)S(1)}, u32[]{:S(2)}, u32[]{:S(2)}) collective-permute-start(bf16[128,1024]{1,0:T(8,128)(2,1)} %get-tuple-element.56.refs_0_), channel_id=1, source_target_pairs={{0,64},{64,128},{128,192},{192,0},{1,65},{65,129},{129,193},{193,1... | collective-permute-start | bytes 786440 | tf_op jit(solution)/shard_map/ppermute | solution.py:176
  85.0 20.4 %collective-permute-start.7 = (bf16[128,1024]{1,0:T(8,128)(2,1)}, bf16[128,1024]{1,0:T(8,128)(2,1)S(1)}, u32[]{:S(2)}, u32[]{:S(2)}) collective-permute-start(bf16[128,1024]{1,0:T(8,128)(2,1)} %get-tuple-element.56.refs_0_), channel_id=1, source_target_pairs={{0,128},{64,192},{128,0},{192,64},{1,129},{65,193},{129,1},{193,65... | collective-permute-start | bytes 786440 | tf_op jit(solution)/shard_map/ppermute | solution.py:176
  86.7 25.5 %collective-permute-start.8 = (bf16[128,1024]{1,0:T(8,128)(2,1)}, bf16[128,1024]{1,0:T(8,128)(2,1)S(1)}, u32[]{:S(2)}, u32[]{:S(2)}) collective-permute-start(bf16[128,1024]{1,0:T(8,128)(2,1)} %get-tuple-element.56.refs_0_), channel_id=1, source_target_pairs={{0,192},{64,0},{128,64},{192,128},{1,193},{65,1},{129,65},{193,129... | collective-permute-start | bytes 786440 | tf_op jit(solution)/shard_map/ppermute | solution.py:176
  115.8 30.2 %all-to-all-start.1 = ((bf16[4,192,1024]{2,1,0:T(8,128)(2,1)}), bf16[4,192,1024]{2,1,0:T(8,128)(2,1)S(1)}, u32[]{:S(2)}, u32[]{:S(2)}) async-start(bf16[4,192,1024]{2,1,0:T(8,128)(2,1)} %bitcast.6), calls=%async_computation.1 | async-start | bytes 3145728 | tf_op jit(solution)/shard_map/all_to_all | solution.py:178
  123.7 18.8 %collective-permute-start.4 = (bf16[128,1024]{1,0:T(8,128)(2,1)}, bf16[128,1024]{1,0:T(8,128)(2,1)S(1)}, u32[]{:S(2)}, u32[]{:S(2)}) collective-permute-start(bf16[128,1024]{1,0:T(8,128)(2,1)} %get-tuple-element.57.refs_0_), channel_id=1, source_target_pairs={{0,128},{64,192},{128,0},{192,64},{1,129},{65,193},{129,1},{193,65... | collective-permute-start | bytes 786440 | tf_op jit(solution)/shard_map/ppermute | solution.py:176
  147.3 30.3 %all-to-all-start = ((bf16[4,192,1024]{2,1,0:T(8,128)(2,1)}), bf16[4,192,1024]{2,1,0:T(8,128)(2,1)S(1)}, u32[]{:S(2)}, u32[]{:S(2)}) async-start(bf16[4,192,1024]{2,1,0:T(8,128)(2,1)} %bitcast.3), calls=%async_computation | async-start | bytes 3145728 | tf_op jit(solution)/shard_map/all_to_all | solution.py:178
  211.1 24.5 %all-to-all-start.4 = ((bf16[4,192,1024]{2,1,0:T(8,128)(2,1)}), bf16[4,192,1024]{2,1,0:T(8,128)(2,1)S(1)}, u32[]{:S(2)}, u32[]{:S(2)}) async-start(bf16[4,192,1024]{2,1,0:T(8,128)(2,1)} %bitcast.29), calls=%async_computation.4 | async-start | bytes 3145728 | tf_op jit(solution)/shard_map/all_to_all | solution.py:185
  236.7 23.8 %all-to-all-start.5 = ((bf16[4,192,1024]{2,1,0:T(8,128)(2,1)}), bf16[4,192,1024]{2,1,0:T(8,128)(2,1)S(1)}, u32[]{:S(2)}, u32[]{:S(2)}) async-start(bf16[4,192,1024]{2,1,0:T(8,128)(2,1)} %bitcast.28), calls=%async_computation.5 | async-start | bytes 3145728 | tf_op jit(solution)/shard_map/all_to_all | solution.py:185
  261.7 22.9 %all-to-all-start.6 = ((bf16[4,192,1024]{2,1,0:T(8,128)(2,1)}), bf16[4,192,1024]{2,1,0:T(8,128)(2,1)S(1)}, u32[]{:S(2)}, u32[]{:S(2)}) async-start(bf16[4,192,1024]{2,1,0:T(8,128)(2,1)} %bitcast.27), calls=%async_computation.6 | async-start | bytes 3145728 | tf_op jit(solution)/shard_map/all_to_all | solution.py:185
  284.5 26.5 %all-to-all-start.7 = ((bf16[4,192,1024]{2,1,0:T(8,128)(2,1)}), bf16[4,192,1024]{2,1,0:T(8,128)(2,1)}, u32[]{:S(2)}, u32[]{:S(2)}) async-start(bf16[4,192,1024]{2,1,0:T(8,128)(2,1)} %bitcast.26), calls=%async_computation.7 | async-start | bytes 3145728 | tf_op jit(solution)/shard_map/all_to_all | solution.py:185
  293.3 70.0 %collective-permute-start.15 = (bf16[128,1024]{1,0:T(8,128)(2,1)}, bf16[128,1024]{1,0:T(8,128)(2,1)}, u32[]{:S(2)}, u32[]{:S(2)}) collective-permute-start(bf16[128,1024]{1,0:T(8,128)(2,1)} %get-tuple-element.40), channel_id=1, source_target_pairs={{0,192},{64,0},{128,64},{192,128},{1,193},{65,1},{129,65},{193,129... | collective-permute-start | bytes 786440 | tf_op jit(solution)/shard_map/ppermute | solution.py:189
  296.1 70.0 %collective-permute-start.16 = (bf16[128,1024]{1,0:T(8,128)(2,1)}, bf16[128,1024]{1,0:T(8,128)(2,1)}, u32[]{:S(2)}, u32[]{:S(2)}) collective-permute-start(bf16[128,1024]{1,0:T(8,128)(2,1)} %get-tuple-element.41), channel_id=1, source_target_pairs={{0,128},{64,192},{128,0},{192,64},{1,129},{65,193},{129,1},{193,65... | collective-permute-start | bytes 786440 | tf_op jit(solution)/shard_map/ppermute | solution.py:189
  298.9 68.6 %collective-permute-start.17 = (bf16[128,1024]{1,0:T(8,128)(2,1)}, bf16[128,1024]{1,0:T(8,128)(2,1)}, u32[]{:S(2)}, u32[]{:S(2)}) collective-permute-start(bf16[128,1024]{1,0:T(8,128)(2,1)} %get-tuple-element.42), channel_id=1, source_target_pairs={{0,64},{64,128},{128,192},{192,0},{1,65},{65,129},{129,193},{193,1... | collective-permute-start | bytes 786440 | tf_op jit(solution)/shard_map/ppermute | solution.py:189
  300.9 70.6 %collective-permute-start.18 = (bf16[128,1024]{1,0:T(8,128)(2,1)}, bf16[128,1024]{1,0:T(8,128)(2,1)}, u32[]{:S(2)}, u32[]{:S(2)}) collective-permute-start(bf16[128,1024]{1,0:T(8,128)(2,1)} %get-tuple-element.44), channel_id=1, source_target_pairs={{0,192},{64,0},{128,64},{192,128},{1,193},{65,1},{129,65},{193,129... | collective-permute-start | bytes 786440 | tf_op jit(solution)/shard_map/ppermute | solution.py:189
  305.0 68.6 %collective-permute-start.19 = (bf16[128,1024]{1,0:T(8,128)(2,1)}, bf16[128,1024]{1,0:T(8,128)(2,1)}, u32[]{:S(2)}, u32[]{:S(2)}) collective-permute-start(bf16[128,1024]{1,0:T(8,128)(2,1)} %get-tuple-element.45), channel_id=1, source_target_pairs={{0,128},{64,192},{128,0},{192,64},{1,129},{65,193},{129,1},{193,65... | collective-permute-start | bytes 786440 | tf_op jit(solution)/shard_map/ppermute | solution.py:189
  367.5 20.2 %collective-permute-start.22 = (bf16[128,1024]{1,0:T(8,128)(2,1)S(1)}, bf16[128,1024]{1,0:T(8,128)(2,1)S(1)}, u32[]{:S(2)}, u32[]{:S(2)}) collective-permute-start(bf16[128,1024]{1,0:T(8,128)(2,1)S(1)} %copy-done.24), channel_id=1, source_target_pairs={{0,128},{64,192},{128,0},{192,64},{1,129},{65,193},{129,1},{193,65... | collective-permute-start | bytes 786440 | tf_op jit(solution)/shard_map/ppermute | solution.py:189
  371.6 20.0 %collective-permute-start.23 = (bf16[128,1024]{1,0:T(8,128)(2,1)S(1)}, bf16[128,1024]{1,0:T(8,128)(2,1)S(1)}, u32[]{:S(2)}, u32[]{:S(2)}) collective-permute-start(bf16[128,1024]{1,0:T(8,128)(2,1)S(1)} %copy-done.22), channel_id=1, source_target_pairs={{0,64},{64,128},{128,192},{192,0},{1,65},{65,129},{129,193},{193,1... | collective-permute-start | bytes 786440 | tf_op jit(solution)/shard_map/ppermute | solution.py:189
  373.6 18.1 %collective-permute-start.24 = (bf16[128,1024]{1,0:T(8,128)(2,1)S(1)}, bf16[128,1024]{1,0:T(8,128)(2,1)S(1)}, u32[]{:S(2)}, u32[]{:S(2)}) collective-permute-start(bf16[128,1024]{1,0:T(8,128)(2,1)S(1)} %get-tuple-element.52), channel_id=1, source_target_pairs={{0,192},{64,0},{128,64},{192,128},{1,193},{65,1},{129,65},{193,129... | collective-permute-start | bytes 786440 | tf_op jit(solution)/shard_map/ppermute | solution.py:189
  375.8 28.8 %collective-permute-start.25 = (bf16[128,1024]{1,0:T(8,128)(2,1)S(1)}, bf16[128,1024]{1,0:T(8,128)(2,1)S(1)}, u32[]{:S(2)}, u32[]{:S(2)}) collective-permute-start(bf16[128,1024]{1,0:T(8,128)(2,1)S(1)} %get-tuple-element.53), channel_id=1, source_target_pairs={{0,128},{64,192},{128,0},{192,64},{1,129},{65,193},{129,1},{193,65... | collective-permute-start | bytes 786440 | tf_op jit(solution)/shard_map/ppermute | solution.py:189
  380.1 27.2 %collective-permute-start.26 = (bf16[128,1024]{1,0:T(8,128)(2,1)S(1)}, bf16[128,1024]{1,0:T(8,128)(2,1)S(1)}, u32[]{:S(2)}, u32[]{:S(2)}) collective-permute-start(bf16[128,1024]{1,0:T(8,128)(2,1)S(1)} %get-tuple-element.54), channel_id=1, source_target_pairs={{0,64},{64,128},{128,192},{192,0},{1,65},{65,129},{129,193},{193,1... | collective-permute-start | bytes 786440 | tf_op jit(solution)/shard_map/ppermute | solution.py:189
  (37 other events, 383.8 us)
Sparse Core Ops, SparseCore 0:
  9.2 128.7 all-gather.5
  139.8 66.4 all-gather.3

commit v2 on v0

v2 whole, which is shorter than its diff:
```python
import functools

import jax
import jax.numpy as jnp
from jax import lax
from jax.experimental import pallas as pl
from jax.experimental.pallas import tpu as pltpu
from jax.sharding import Mesh, PartitionSpec as P

BF, F32 = jnp.bfloat16, jnp.float32
ZH, YS, XS = 4, 4, 4
PARAMS = pltpu.CompilerParams(vmem_limit_bytes=48 << 20)
BLOCK = 256
ANY = pl.BlockSpec(memory_space=pl.ANY)


def ring(step):
    return [(i, (i + step) % ZH) for i in range(ZH)]


def plan_kernel(group_ref, meta_ref, pick_ref, high_ref, low_ref):
    sources, _, rows = meta_ref.shape
    slots = pick_ref.shape[1] // YS
    group = group_ref[0]
    named, gates = [], []
    for k in range(sources):
        ids, weights = meta_ref[k, 0:4, :], meta_ref[k, 4:8, :]
        for y in range(YS):
            match = ids == (group * YS + y).astype(F32)
            named.append(jnp.sum(match.astype(F32), axis=0, keepdims=True))
            gates.append(jnp.sum(jnp.where(match, weights, 0.0), axis=0, keepdims=True))
    stacked = jnp.concatenate(named, axis=0)
    earlier = lax.broadcasted_iota(jnp.int32, (rows, rows), 0)
    later = lax.broadcasted_iota(jnp.int32, (rows, rows), 1)
    rank = jnp.dot(
        stacked.astype(BF), (earlier < later).astype(F32).astype(BF), preferred_element_type=F32
    )
    slot = lax.broadcasted_iota(jnp.int32, (slots, rows), 0).astype(F32)
    for k in range(sources):
        for y in range(YS):
            i = k * YS + y
            here = (rank[i : i + 1, :] == slot) & (named[i] > 0.5)
            at = slice(y * slots, (y + 1) * slots)
            scaled = jnp.where(here, gates[i], 0.0)
            high = scaled.astype(BF)
            pick_ref[k, at, :] = here.astype(F32).astype(BF)
            high_ref[k, at, :] = high
            low_ref[k, at, :] = (scaled - high.astype(F32)).astype(BF)


def plan(group, metas, slots):
    out = jax.ShapeDtypeStruct((metas.shape[0], YS * slots, metas.shape[2]), BF)
    return pl.pallas_call(
        plan_kernel,
        out_shape=(out, out, out),
        in_specs=[pl.BlockSpec(memory_space=pltpu.SMEM), pl.BlockSpec()],
        compiler_params=PARAMS,
        name="plan",
    )(group, metas)


def gather_kernel(pick_ref, *refs):
    blocks, out_ref = refs[:-1], refs[-1]
    rows = jnp.concatenate([ref[...] for ref in blocks], axis=0)
    out_ref[...] = jnp.dot(pick_ref[0], rows, preferred_element_type=F32).astype(BF)


def gather(pick, k, *blocks):
    _, routes, rows = pick.shape
    width = blocks[0].shape[1]
    tile = 1024
    return pl.pallas_call(
        gather_kernel,
        grid=(width // tile,),
        out_shape=jax.ShapeDtypeStruct((routes, width), BF),
        in_specs=[pl.BlockSpec((1, routes, rows), lambda j: (k, 0, 0))]
        + [pl.BlockSpec((b.shape[0], tile), lambda j: (0, j)) for b in blocks],
        out_specs=pl.BlockSpec((routes, tile), lambda j: (0, j)),
        compiler_params=PARAMS,
        name="gather",
    )(pick, *blocks)


def expert_kernel(place_ref, x_ref, *refs):
    ins, downs = refs[0:4], refs[4:8]
    out_ref, sums_ref, hidden_ref = refs[-3:]
    step = pl.program_id(0)
    parts = sums_ref.shape[0]
    half = parts // 2

    def columns(x, r):
        return pl.ds(pl.multiple_of((x * 4 + place_ref[r]) * BLOCK, BLOCK), BLOCK)

    @pl.when(step == 0)
    def _():
        sums_ref[...] = jnp.zeros_like(sums_ref)

    @pl.when(step < XS)
    def _():
        rows = [x_ref[:, columns(step, r)] for r in range(4)]
        for n in range(parts):
            sums_ref[n] += sum(
                jnp.dot(rows[r], ins[r][n], preferred_element_type=F32) for r in range(4)
            )

    @pl.when(step == XS)
    def _():
        for n in range(half):
            g, u = sums_ref[n], sums_ref[half + n]
            hidden_ref[n] = (g / (1.0 + jnp.exp(-g)) * u).astype(BF)

    @pl.when(step >= XS)
    def _():
        for r in range(4):
            made = sum(
                jnp.dot(hidden_ref[n], downs[r][n], preferred_element_type=F32) for n in range(half)
            )
            out_ref[:, columns(step - XS, r)] = made.astype(BF)


def expert(place, rows, packs, after):
    count, width = rows.shape
    total = packs[0].shape[1]
    half = total // 3
    return pl.pallas_call(
        expert_kernel,
        grid_spec=pltpu.PrefetchScalarGridSpec(
            num_scalar_prefetch=1,
            grid=(2 * XS,),
            in_specs=[pl.BlockSpec((count, width), lambda s, p: (0, 0))]
            + [
                pl.BlockSpec(
                    (pl.Squeezed(), 2 * half, BLOCK, BLOCK),
                    lambda s, p: (jnp.minimum(s, XS - 1), 0, 0, 0),
                )
            ]
            * 4
            + [
                pl.BlockSpec(
                    (pl.Squeezed(), half, BLOCK, BLOCK),
                    lambda s, p: (jnp.maximum(s - XS, 0), 2, 0, 0),
                )
            ]
            * 4
            + [ANY] * len(after),
            out_specs=pl.BlockSpec((count, width), lambda s, p: (0, 0)),
            scratch_shapes=[
                pltpu.VMEM((2 * half, count, BLOCK), F32),
                pltpu.VMEM((half, count, BLOCK), BF),
            ],
        ),
        out_shape=jax.ShapeDtypeStruct((count, width), BF),
        compiler_params=PARAMS,
        name="expert",
    )(place, rows, *packs, *packs, *after)


def combine_kernel(start, high_ref, low_ref, rows_ref, *refs):
    rows, out_ref = rows_ref[...], refs[-1]
    total = sum(
        lax.dot_general(s[0], rows, (((0,), (0,)), ((), ())), preferred_element_type=F32)
        for s in (high_ref, low_ref)
    )
    if len(refs) == 1:
        out_ref[...] = total.astype(out_ref.dtype)
        return
    half = refs[0].shape[0]
    for at in (0, half):
        part = total[at : at + half]
        if at == start:
            part = part + refs[0][...].astype(F32)
        out_ref[at : at + half, :] = part.astype(out_ref.dtype)


def combine(plans, k, rows, dtype, passed=(), start=0):
    _, high, low = plans
    _, routes, tok_rows = high.shape
    width = rows.shape[1]
    tile = 1024
    pick = pl.BlockSpec((1, routes, tok_rows), lambda j: (k, 0, 0))
    return pl.pallas_call(
        functools.partial(combine_kernel, start),
        grid=(width // tile,),
        out_shape=jax.ShapeDtypeStruct((tok_rows, width), dtype),
        in_specs=[pick, pick, pl.BlockSpec((routes, tile), lambda j: (0, j))]
        + [pl.BlockSpec((p.shape[0], tile), lambda j: (0, j)) for p in passed],
        out_specs=pl.BlockSpec((tok_rows, tile), lambda j: (0, j)),
        compiler_params=PARAMS,
        name="combine",
    )(high, low, rows, *passed)


def over_y(rows):
    routes, width = rows.shape
    split = rows.reshape(YS, routes // YS, width)
    return lax.all_to_all(split, "y", split_axis=0, concat_axis=0, tiled=True).reshape(rows.shape)


def on_device(tokens, route_ids, gate_values, w_gate_up, w_down):
    tok_rows, top = route_ids.shape
    slots = 3 * tok_rows * top // (2 * ZH * YS)
    parts = w_gate_up.shape[2] // BLOCK
    swap = [(0, 1), (1, 0)]
    pack = jnp.concatenate(
        [
            w_gate_up[0].reshape(BLOCK, parts, BLOCK).transpose(1, 0, 2),
            w_down[0].reshape(parts // 2, BLOCK, BLOCK),
        ],
        axis=0,
    )
    meta = jnp.concatenate([route_ids.astype(F32).T, gate_values.T], axis=0)
    group = lax.axis_index("zh").reshape(1)
    barrier = lax.optimization_barrier

    near = [lax.ppermute(tokens, "zh", ring(k)) for k in (1, 3)]
    swapped = lax.ppermute(pack, "zl", swap)
    metas = [lax.ppermute(meta, "zh", ring(k)) for k in (1, 2, 3)]
    mine = lax.all_gather(pack, "x")
    own_plan = plan(group, meta[None], slots)
    arrived = {0: over_y(gather(own_plan[0], 0, tokens))}
    near, swapped, metas, arrived[0] = barrier((near, swapped, metas, arrived[0]))
    other = lax.all_gather(swapped, "x")
    far_plan = plan(group, jnp.stack(metas), slots)

    half = tok_rows // 2
    far = [lax.ppermute(near[0][:half], "zh", ring(1)), lax.ppermute(near[1][half:], "zh", ring(3))]
    arrived[1] = over_y(gather(far_plan[0], 0, near[0]))
    far, mine, near[1], arrived[1] = barrier((far, mine, near[1], arrived[1]))
    mine_swapped = lax.ppermute(mine, "core", swap)
    arrived[3] = over_y(gather(far_plan[0], 2, near[1]))
    arrived[2] = over_y(gather(far_plan[0], 1, *far))
    other, arrived[2], arrived[3], mine_swapped = barrier((other, arrived[2], arrived[3], mine_swapped))
    packs = [mine, mine_swapped, other, lax.ppermute(other, "core", swap)]
    zl, core = lax.axis_index("zl"), lax.axis_index("core")
    place = jnp.stack([zl * 2 + core, zl * 2 + 1 - core, (1 - zl) * 2 + core, (1 - zl) * 2 + 1 - core])

    def returned(k, after):
        return over_y(expert(place, arrived[k], packs, after))

    across = combine(far_plan, 1, returned(2, []), BF)
    back = {1: returned(1, [])}
    passed = [lax.ppermute(across[:half], "zh", ring(3)), lax.ppermute(across[half:], "zh", ring(1))]
    back[3] = returned(3, [across])
    below = combine(far_plan, 0, back[1], BF, passed[:1], 0)
    back[0] = returned(0, [below])
    above = combine(far_plan, 2, back[3], BF, passed[1:], half)
    total = combine(own_plan, 0, back[0], F32)
    for part, step in ((below, 3), (above, 1)):
        total = total + lax.ppermute(part, "zh", ring(step)).astype(F32)
    return total.astype(BF)


def solution(mesh):
    split = Mesh(mesh.devices.reshape(ZH, YS, XS, 2, 2), ("zh", "y", "x", "zl", "core"))
    owner, shard = ("zh", "y"), ("x", "zl", "core")
    every = owner + shard
    in_specs = (P(every, None),) * 3 + (P(owner, shard, None), P(owner, None, shard))
    return jax.shard_map(
        on_device, mesh=split, in_specs=in_specs, out_specs=P(every, None), check_vma=False
    )
```

time: 469 us -> 373 us (0.80)
  waiting for transfers between devices: 349 us -> 179 us
  Pallas kernels: 0 us -> 71.9 us
  starting transfers between devices: 24.6 us -> 60.2 us
  matrix products: 26.4 us -> 0 us
  blocking collectives: 0 us -> 23.8 us
  other arithmetic: 20.5 us -> 4.09 us
  local copies, waits for them, and re-layouts: 30.8 us -> 17.2 us
    all_to_all x2 -> x7, waiting for transfers between devices: 282 us -> 37.5 us  [over_y(): lax.all_to_all(split, 'y', split_axis=0, concat_axis=0, tiled=True)]
    ppermute x0 -> x14, waiting for transfers between devices: none -> 142 us  [the longest x3 61.5 us: on_device(): metas = [lax.ppermute(meta, 'zh', ring(k)) for k in (1, 2, 3)]]
    pallas_call x0 -> x14, Pallas kernels: none -> 71.9 us  [the longest x4 51.2 us: expert(): pl.pallas_call(expert_kernel, grid_spec=pltpu.PrefetchScalarGridSpec(num_...]
    all_gather x2, waiting for transfers between devices: 65.4 us -> 0.01 us  [the longest x1 0.01 us: on_device(): mine = lax.all_gather(pack, 'x')]
    dot_general x2 -> x0, matrix products: 26.4 us -> none  [the longest x1 16.1 us: on_device(): jnp.dot(expert_rows, lax.all_gather(w_gate_up, 'fsdp', axis=1, tiled=True...]
    gather x3 -> x0, local copies, waits for them, and re-layouts: 25.1 us -> none  [the longest x2 19.3 us: on_device(): jnp.take(returned.reshape(dp_count * capacity, model_width), target, axis=0)]
    ppermute x0 -> x14, starting transfers between devices: none -> 24.2 us  [the longest x3 5.92 us: on_device(): metas = [lax.ppermute(meta, 'zh', ring(k)) for k in (1, 2, 3)]]
    all_to_all x0 -> x1, blocking collectives: none -> 23.8 us  [over_y(): lax.all_to_all(split, 'y', split_axis=0, concat_axis=0, tiled=True)]
  transfers between devices with their start and end apart: 4 -> 23, of which waited for: 3 -> 11; matrix products, arithmetic and copies ran while one was open for 8% -> 1% of each run, Pallas kernels for 0% -> 16%
where the time goes in v2:
time: 373 us; the launch traced here: 370 us
  waiting for transfers between devices  179 us (48%)
  Pallas kernels  71.9 us (19%)
  starting transfers between devices  60.2 us (16%)
  blocking collectives  23.8 us (6%)
  local copies, waits for them, and re-layouts  17.2 us (5%)
  between operations  13.6 us (4%)
  other arithmetic  4.09 us (1%)
    ppermute x3, waiting for transfers between devices, on_device(): metas = [lax.ppermute(meta, 'zh', ring(k)) for k in (1, 2, 3)]  61.5 us
    pallas_call x4, Pallas kernels, expert(): pl.pallas_call(expert_kernel, grid_spec=pltpu.PrefetchScalarGridSpec(num_...  51.2 us
    all_to_all x7, waiting for transfers between devices, over_y(): lax.all_to_all(split, 'y', split_axis=0, concat_axis=0, tiled=True)  37.5 us
    all_to_all x7, starting transfers between devices, over_y(): lax.all_to_all(split, 'y', split_axis=0, concat_axis=0, tiled=True)  35.9 us
    ppermute x2, waiting for transfers between devices, on_device(): total = total + lax.ppermute(part, 'zh', ring(step)).astype(F32)  30.7 us
    all_to_all x1, blocking collectives, over_y(): lax.all_to_all(split, 'y', split_axis=0, concat_axis=0, tiled=True)  23.8 us
    ppermute x1, waiting for transfers between devices, on_device(): lax.ppermute(across[:half], 'zh', ring(3))  21.5 us
    ppermute x1, waiting for transfers between devices, on_device(): lax.ppermute(near[1][half:], 'zh', ring(3))  20.1 us
  transfers between devices with their start and end apart: 23, of which 11 were waited for; matrix products, arithmetic and copies ran while one was open for 1% of the time, Pallas kernels for 16%

profile of v2, /device:TPU:10, one launch (start us, length us, event | category | flops | bytes accessed | tf_op | source)
XLA Modules:
  0.0 370.3 jit_solution(6889175756092337685)
XLA Ops:
  14.9 4.0 %gather.4 = bf16[192,4096]{1,0:T(8,128)(2,1)} custom-call(bf16[1,192,128]{2,1,0:T(8,128)(2,1)S(1)} %get-tuple-element.29.pick_ref, bf16[128,4096]{1,0:T(8,128)(2,1)} %refs_0_.1), custom_call_target="tpu_custom_call" | custom-call | tf_op jit(solution)/shard_map/gather/pallas_call | solution.py:72
  18.9 4.9 %all-to-all-start = ((bf16[4,48,4096]{2,1,0:T(8,128)(2,1)}), bf16[4,48,4096]{2,1,0:T(8,128)(2,1)S(1)}, u32[]{:S(2)}, u32[]{:S(2)}) async-start(bf16[4,48,4096]{2,1,0:T(8,128)(2,1)} %bitcast.11), calls=%async_computation | async-start | bytes 3145728 | tf_op jit(solution)/shard_map/all_to_all | solution.py:196
  23.8 3.3 collective-permute-start
  29.2 5.0 %collective-permute-start.4 = (f32[8,128]{1,0:T(8,128)S(1)}, f32[8,128]{1,0:T(8,128)S(1)}, u32[]{:S(2)}, u32[]{:S(2)}) collective-permute-start(f32[8,128]{1,0:T(8,128)S(1)} %get-tuple-element.52), channel_id=1, source_target_pairs={{0,128},{64,192},{128,0},{192,64},{1,129},{65,193},{129,1},{193,65... | collective-permute-start | bytes 12296 | tf_op jit(solution)/shard_map/ppermute | solution.py:217
  34.5 57.6 %collective-permute-done.4 = f32[8,128]{1,0:T(8,128)S(1)} collective-permute-done((f32[8,128]{1,0:T(8,128)S(1)}, f32[8,128]{1,0:T(8,128)S(1)}, u32[]{:S(2)}, u32[]{:S(2)}) %collective-permute-start.4) | collective-permute-done | bytes 4128 | tf_op jit(solution)/shard_map/ppermute | solution.py:217
  92.7 3.9 %collective-permute-done.5 = f32[8,128]{1,0:T(8,128)S(1)} collective-permute-done((f32[8,128]{1,0:T(8,128)S(1)}, f32[8,128]{1,0:T(8,128)S(1)}, u32[]{:S(2)}, u32[]{:S(2)}) %collective-permute-start.5) | collective-permute-done | bytes 4128 | tf_op jit(solution)/shard_map/ppermute | solution.py:217
  97.6 2.8 copy.17
  104.4 4.9 %all-to-all-start.1 = ((bf16[4,48,4096]{2,1,0:T(8,128)(2,1)}), bf16[4,48,4096]{2,1,0:T(8,128)(2,1)}, u32[]{:S(2)}, u32[]{:S(2)}) async-start(bf16[4,48,4096]{2,1,0:T(8,128)(2,1)} %bitcast.17), calls=%async_computation.1 | async-start | bytes 3145728 | tf_op jit(solution)/shard_map/all_to_all | solution.py:196
  113.4 20.1 %collective-permute-done.7.refs_1_ = bf16[64,4096]{1,0:T(8,128)(2,1)S(1)} collective-permute-done((bf16[64,4096]{1,0:T(8,128)(2,1)S(1)}, bf16[64,4096]{1,0:T(8,128)(2,1)S(1)}, u32[]{:S(2)}, u32[]{:S(2)}) %collective-permute-start.7) | collective-permute-done | bytes 524320 | tf_op jit(solution)/shard_map/ppermute | solution.py:226
  136.0 4.8 %all-to-all-start.2 = ((bf16[4,48,4096]{2,1,0:T(8,128)(2,1)}), bf16[4,48,4096]{2,1,0:T(8,128)(2,1)}, u32[]{:S(2)}, u32[]{:S(2)}) async-start(bf16[4,48,4096]{2,1,0:T(8,128)(2,1)} %bitcast.20), calls=%async_computation.2 | async-start | bytes 3145728 | tf_op jit(solution)/shard_map/all_to_all | solution.py:196
  144.2 16.8 %all-to-all-done.2 = bf16[4,48,4096]{2,1,0:T(8,128)(2,1)} async-done(((bf16[4,48,4096]{2,1,0:T(8,128)(2,1)}), bf16[4,48,4096]{2,1,0:T(8,128)(2,1)}, u32[]{:S(2)}, u32[]{:S(2)}) %all-to-all-start.2) | async-done | bytes 1572896 | tf_op jit(solution)/shard_map/all_to_all | solution.py:196
  161.0 23.8 %all_to_all.40 = bf16[4,48,4096]{2,1,0:T(8,128)(2,1)} all-to-all(bf16[4,48,4096]{2,1,0:T(8,128)(2,1)S(1)} %bitcast.40), channel_id=1, replica_groups=mesh['zh'=4,'y'=4,'x'=4,'zl'=2,'core'=2] {'y'}, dimensions={0} | all-to-all | bytes 3145728 | tf_op jit(solution)/shard_map/all_to_all | solution.py:196
  184.9 8.2 %collective-permute-done.9.refs_3_.refs_7_ = bf16[4,9,256,256]{3,2,1,0:T(8,128)(2,1)} collective-permute-done((bf16[4,9,256,256]{3,2,1,0:T(8,128)(2,1)}, bf16[4,9,256,256]{3,2,1,0:T(8,128)(2,1)}, u32[]{:S(2)}, u32[]{:S(2)}) %collective-permute-start.9) | collective-permute-done | bytes 4718624 | tf_op jit(solution)/shard_map/ppermute | solution.py:233
  193.1 13.6 %expert.5 = bf16[192,4096]{1,0:T(8,128)(2,1)} custom-call(s32[4]{0:T(128)S(1)} %pad_add_fusion.place_ref, bf16[192,4096]{1,0:T(8,128)(2,1)} %bitcast.21.x_ref, bf16[4,9,256,256]{3,2,1,0:T(8,128)(2,1)} %bitcast.42, bf16[4,9,256,256]{3,2,1,0:T(8,128)(2,1)} %collective-permute-done.8.refs_1_.refs_5_, bf16[4,9,256,256]{3,2,1,0:T(8,128)(2,1)} %bitcast.51, ...), custom_call_target="tpu_custom_call" | custom-call | tf_op jit(solution)/shard_map/expert/pallas_call | solution.py:125
  206.7 5.0 %all-to-all-start.5 = ((bf16[4,48,4096]{2,1,0:T(8,128)(2,1)}), bf16[4,48,4096]{2,1,0:T(8,128)(2,1)S(1)}, u32[]{:S(2)}, u32[]{:S(2)}) async-start(bf16[4,48,4096]{2,1,0:T(8,128)(2,1)} %bitcast.26), calls=%async_computation.5 | async-start | bytes 3145728 | tf_op jit(solution)/shard_map/all_to_all | solution.py:196
  211.7 13.6 %expert.4 = bf16[192,4096]{1,0:T(8,128)(2,1)} custom-call(s32[4]{0:T(128)S(1)} %pad_add_fusion.place_ref, bf16[192,4096]{1,0:T(8,128)(2,1)} %bitcast.18.x_ref, bf16[4,9,256,256]{3,2,1,0:T(8,128)(2,1)} %bitcast.44, bf16[4,9,256,256]{3,2,1,0:T(8,128)(2,1)} %collective-permute-done.8.refs_1_.refs_5_, bf16[4,9,256,256]{3,2,1,0:T(8,128)(2,1)} %bitcast.53, ...), custom_call_target="tpu_custom_call" | custom-call | tf_op jit(solution)/shard_map/expert/pallas_call | solution.py:125
  225.3 6.3 %all-to-all-done.5 = bf16[4,48,4096]{2,1,0:T(8,128)(2,1)S(1)} async-done(((bf16[4,48,4096]{2,1,0:T(8,128)(2,1)}), bf16[4,48,4096]{2,1,0:T(8,128)(2,1)S(1)}, u32[]{:S(2)}, u32[]{:S(2)}) %all-to-all-start.5) | async-done | bytes 1572896 | tf_op jit(solution)/shard_map/all_to_all | solution.py:196
  232.7 5.8 %all-to-all-start.4 = ((bf16[4,48,4096]{2,1,0:T(8,128)(2,1)}), bf16[4,48,4096]{2,1,0:T(8,128)(2,1)}, u32[]{:S(2)}, u32[]{:S(2)}) async-start(bf16[4,48,4096]{2,1,0:T(8,128)(2,1)} %bitcast.24), calls=%async_computation.4 | async-start | bytes 3145728 | tf_op jit(solution)/shard_map/all_to_all | solution.py:196
  241.5 11.4 %expert.7 = bf16[192,4096]{1,0:T(8,128)(2,1)S(1)} custom-call(s32[4]{0:T(128)S(1)} %pad_add_fusion.place_ref, bf16[192,4096]{1,0:T(8,128)(2,1)S(1)} %bitcast.36, bf16[4,9,256,256]{3,2,1,0:T(8,128)(2,1)} %bitcast.46, bf16[4,9,256,256]{3,2,1,0:T(8,128)(2,1)} %collective-permute-done.8.refs_1_.refs_5_, bf16[4,9,256,256]{3,2,1,0:T(8,128)(2,1)} %bitcast.55, ...), custom_call_target="tpu_custom_call" | custom-call | tf_op jit(solution)/shard_map/expert/pallas_call | solution.py:125
  254.1 3.4 all-to-all-done.4
  257.6 5.8 %all-to-all-start.7 = ((bf16[4,48,4096]{2,1,0:T(8,128)(2,1)}), bf16[4,48,4096]{2,1,0:T(8,128)(2,1)}, u32[]{:S(2)}, u32[]{:S(2)}) async-start(bf16[4,48,4096]{2,1,0:T(8,128)(2,1)} %bitcast.37), calls=%async_computation.7 | async-start | bytes 3145728 | tf_op jit(solution)/shard_map/all_to_all | solution.py:196
  263.4 3.1 collective-permute-start.10
  267.4 21.5 %collective-permute-done.10.refs_0_ = bf16[64,4096]{1,0:T(8,128)(2,1)S(1)} collective-permute-done((bf16[64,4096]{1,0:T(8,128)(2,1)S(1)}, bf16[64,4096]{1,0:T(8,128)(2,1)S(1)}, u32[]{:S(2)}, u32[]{:S(2)}) %collective-permute-start.10) | collective-permute-done | bytes 524320 | tf_op jit(solution)/shard_map/ppermute | solution.py:242
  288.9 4.1 %combine.5.refs_8_ = bf16[128,4096]{1,0:T(8,128)(2,1)} custom-call(bf16[3,192,128]{2,1,0:T(8,128)(2,1)S(1)} %get-tuple-element.44.high_ref, bf16[3,192,128]{2,1,0:T(8,128)(2,1)S(1)} %get-tuple-element.45.low_ref, bf16[192,4096]{1,0:T(8,128)(2,1)} %bitcast.25.rows_ref, bf16[64,4096]{1,0:T(8,128)(2,1)S(1)} %collective-permute-done.10.refs_0_), custom_call_target="tpu_custom_call" | custom-call | tf_op jit(solution)/shard_map/combine/pallas_call | solution.py:181
  293.0 12.6 %expert.6 = bf16[192,4096]{1,0:T(8,128)(2,1)} custom-call(s32[4]{0:T(128)S(1)} %pad_add_fusion.place_ref, bf16[192,4096]{1,0:T(8,128)(2,1)S(1)} %bitcast.35, bf16[4,9,256,256]{3,2,1,0:T(8,128)(2,1)} %bitcast.48, bf16[4,9,256,256]{3,2,1,0:T(8,128)(2,1)} %collective-permute-done.8.refs_1_.refs_5_, bf16[4,9,256,256]{3,2,1,0:T(8,128)(2,1)} %bitcast.57, ...), custom_call_target="tpu_custom_call" | custom-call | tf_op jit(solution)/shard_map/expert/pallas_call | solution.py:125
  305.6 4.8 %all-to-all-start.6 = ((bf16[4,48,4096]{2,1,0:T(8,128)(2,1)}), bf16[4,48,4096]{2,1,0:T(8,128)(2,1)S(1)}, u32[]{:S(2)}, u32[]{:S(2)}) async-start(bf16[4,48,4096]{2,1,0:T(8,128)(2,1)} %bitcast.28), calls=%async_computation.6 | async-start | bytes 3145728 | tf_op jit(solution)/shard_map/all_to_all | solution.py:196
  310.4 2.9 collective-permute-start.11
  313.3 3.1 combine.7
  317.3 11.0 %all-to-all-done.6 = bf16[4,48,4096]{2,1,0:T(8,128)(2,1)S(1)} async-done(((bf16[4,48,4096]{2,1,0:T(8,128)(2,1)}), bf16[4,48,4096]{2,1,0:T(8,128)(2,1)S(1)}, u32[]{:S(2)}, u32[]{:S(2)}) %all-to-all-start.6) | async-done | bytes 1572896 | tf_op jit(solution)/shard_map/all_to_all | solution.py:196
  329.8 22.7 %collective-permute-done.11 = bf16[128,4096]{1,0:T(8,128)(2,1)} collective-permute-done((bf16[128,4096]{1,0:T(8,128)(2,1)}, bf16[128,4096]{1,0:T(8,128)(2,1)}, u32[]{:S(2)}, u32[]{:S(2)}) %collective-permute-start.11) | collective-permute-done | bytes 1048608 | tf_op jit(solution)/shard_map/ppermute | solution.py:249
  352.5 8.1 %collective-permute-done.13 = bf16[128,4096]{1,0:T(8,128)(2,1)} collective-permute-done((bf16[128,4096]{1,0:T(8,128)(2,1)S(1)}, bf16[128,4096]{1,0:T(8,128)(2,1)}, u32[]{:S(2)}, u32[]{:S(2)}) %collective-permute-start.13) | collective-permute-done | bytes 1048608 | tf_op jit(solution)/shard_map/ppermute | solution.py:249
  360.5 2.9 add_convert_fusion
  (68 shorter events, 35.3 us)
Async XLA Ops:
  6.5 127.0 %all-gather.5.cloned.1.call-start = ((), (), s32[]{:S(2)}) async-start(), calls=%async_computation.8 | async-start | bytes 5898240 | tf_op jit(solution)/shard_map/all_gather | solution.py:218
  10.2 4.5 %copy-start.10 = (s32[128,4]{0,1:T(4,128)S(1)}, s32[128,4]{0,1:T(4,128)}, u32[]{:S(2)}) copy-start(s32[128,4]{0,1:T(4,128)} %param.6) | copy-start | bytes 6148
  10.2 4.5 %copy-start.11 = (f32[128,4]{0,1:T(4,128)S(1)}, f32[128,4]{0,1:T(4,128)}, u32[]{:S(2)}) copy-start(f32[128,4]{0,1:T(4,128)} %param.7) | copy-start | bytes 6148
  12.7 84.9 %collective-permute-start.2 = (bf16[9,256,256]{1,2,0:T(8,128)(2,1)}, bf16[9,256,256]{1,2,0:T(8,128)(2,1)}, u32[]{:S(2)}, u32[]{:S(2)}) collective-permute-start(bf16[9,256,256]{1,2,0:T(8,128)(2,1)} %pad_maximum_fusion), channel_id=1, source_target_pairs={{0,2},{2,0},{1,3},{3,1},{4,6},{6,4},{5,7},{7,5},{8,10},{10,8},{9,1... | collective-permute-start | bytes 3538952 | tf_op jit(solution)/shard_map/ppermute | solution.py:216
  18.9 78.7 %all-to-all-start = ((bf16[4,48,4096]{2,1,0:T(8,128)(2,1)}), bf16[4,48,4096]{2,1,0:T(8,128)(2,1)S(1)}, u32[]{:S(2)}, u32[]{:S(2)}) async-start(bf16[4,48,4096]{2,1,0:T(8,128)(2,1)} %bitcast.11), calls=%async_computation | async-start | bytes 3145728 | tf_op jit(solution)/shard_map/all_to_all | solution.py:196
  23.8 161.0 %all-gather.7.cloned.1.call-start = ((), (), s32[]{:S(2)}) async-start(), calls=%async_computation.9 | async-start | bytes 5898240 | tf_op jit(solution)/shard_map/all_gather | solution.py:222
  23.8 72.8 %collective-permute-start = (bf16[128,4096]{1,0:T(8,128)(2,1)}, bf16[128,4096]{1,0:T(8,128)(2,1)S(1)}, u32[]{:S(2)}, u32[]{:S(2)}) collective-permute-start(bf16[128,4096]{1,0:T(8,128)(2,1)} %refs_0_.1), channel_id=1, source_target_pairs={{0,64},{64,128},{128,192},{192,0},{1,65},{65,129},{129,193},{193,1... | collective-permute-start | bytes 3145736 | tf_op jit(solution)/shard_map/ppermute | solution.py:215
  27.1 70.5 %collective-permute-start.1 = (bf16[128,4096]{1,0:T(8,128)(2,1)}, bf16[128,4096]{1,0:T(8,128)(2,1)S(1)}, u32[]{:S(2)}, u32[]{:S(2)}) collective-permute-start(bf16[128,4096]{1,0:T(8,128)(2,1)} %refs_0_.1), channel_id=1, source_target_pairs={{0,192},{64,0},{128,64},{192,128},{1,193},{65,1},{129,65},{193,129... | collective-permute-start | bytes 3145736 | tf_op jit(solution)/shard_map/ppermute | solution.py:215
  29.2 62.9 %collective-permute-start.4 = (f32[8,128]{1,0:T(8,128)S(1)}, f32[8,128]{1,0:T(8,128)S(1)}, u32[]{:S(2)}, u32[]{:S(2)}) collective-permute-start(f32[8,128]{1,0:T(8,128)S(1)} %get-tuple-element.52), channel_id=1, source_target_pairs={{0,128},{64,192},{128,0},{192,64},{1,129},{65,193},{129,1},{193,65... | collective-permute-start | bytes 12296 | tf_op jit(solution)/shard_map/ppermute | solution.py:217
  34.2 58.5 %collective-permute-start.3 = (f32[8,128]{1,0:T(8,128)S(1)}, f32[8,128]{1,0:T(8,128)S(1)}, u32[]{:S(2)}, u32[]{:S(2)}) collective-permute-start(f32[8,128]{1,0:T(8,128)S(1)} %get-tuple-element.52), channel_id=1, source_target_pairs={{0,64},{64,128},{128,192},{192,0},{1,65},{65,129},{129,193},{193,1... | collective-permute-start | bytes 12296 | tf_op jit(solution)/shard_map/ppermute | solution.py:217
  92.1 4.5 %collective-permute-start.5 = (f32[8,128]{1,0:T(8,128)S(1)}, f32[8,128]{1,0:T(8,128)S(1)}, u32[]{:S(2)}, u32[]{:S(2)}) collective-permute-start(f32[8,128]{1,0:T(8,128)S(1)} %get-tuple-element.52), channel_id=1, source_target_pairs={{0,192},{64,0},{128,64},{192,128},{1,193},{65,1},{129,65},{193,129... | collective-permute-start | bytes 12296 | tf_op jit(solution)/shard_map/ppermute | solution.py:217
  97.6 12.8 %copy-start.4 = (bf16[128,4096]{1,0:T(8,128)(2,1)}, bf16[128,4096]{1,0:T(8,128)(2,1)S(1)}, u32[]{:S(2)}) copy-start(bf16[128,4096]{1,0:T(8,128)(2,1)S(1)} %collective-permute-done.1.refs_0_) | copy-start | bytes 3145732
  100.6 33.0 %copy-start.8 = (bf16[3,192,128]{2,1,0:T(8,128)(2,1)}, bf16[3,192,128]{2,1,0:T(8,128)(2,1)S(1)}, u32[]{:S(2)}) copy-start(bf16[3,192,128]{2,1,0:T(8,128)(2,1)S(1)} %get-tuple-element.36.pick_ref) | copy-start | bytes 442372
  100.6 1.3 copy-start.7
  104.4 29.1 %all-to-all-start.1 = ((bf16[4,48,4096]{2,1,0:T(8,128)(2,1)}), bf16[4,48,4096]{2,1,0:T(8,128)(2,1)}, u32[]{:S(2)}, u32[]{:S(2)}) async-start(bf16[4,48,4096]{2,1,0:T(8,128)(2,1)} %bitcast.17), calls=%async_computation.1 | async-start | bytes 3145728 | tf_op jit(solution)/shard_map/all_to_all | solution.py:196
  110.4 23.1 %collective-permute-start.7 = (bf16[64,4096]{1,0:T(8,128)(2,1)S(1)}, bf16[64,4096]{1,0:T(8,128)(2,1)S(1)}, u32[]{:S(2)}, u32[]{:S(2)}) collective-permute-start(bf16[64,4096]{1,0:T(8,128)(2,1)S(1)} %slice.13), channel_id=1, source_target_pairs={{0,192},{64,0},{128,64},{192,128},{1,193},{65,1},{129,65},{193,129... | collective-permute-start | bytes 1572872 | tf_op jit(solution)/shard_map/ppermute | solution.py:226
  112.3 21.2 %collective-permute-start.6 = (bf16[64,4096]{1,0:T(8,128)(2,1)S(1)}, bf16[64,4096]{1,0:T(8,128)(2,1)S(1)}, u32[]{:S(2)}, u32[]{:S(2)}) collective-permute-start(bf16[64,4096]{1,0:T(8,128)(2,1)S(1)} %slice.12), channel_id=1, source_target_pairs={{0,64},{64,128},{128,192},{192,0},{1,65},{65,129},{129,193},{193,1... | collective-permute-start | bytes 1572872 | tf_op jit(solution)/shard_map/ppermute | solution.py:226
  133.5 51.3 %collective-permute-start.8 = (bf16[4,9,256,256]{3,2,1,0:T(8,128)(2,1)}, bf16[4,9,256,256]{3,2,1,0:T(8,128)(2,1)}, u32[]{:S(2)}, u32[]{:S(2)}) collective-permute-start(bf16[4,9,256,256]{3,2,1,0:T(8,128)(2,1)} %bitcast.41), channel_id=1, source_target_pairs={{0,1},{1,0},{2,3},{3,2},{4,5},{5,4},{6,7},{7,6},{8,9},{9,8},{10,11... | collective-permute-start | bytes 14155784 | tf_op jit(solution)/shard_map/ppermute | solution.py:229
  136.0 25.0 %all-to-all-start.2 = ((bf16[4,48,4096]{2,1,0:T(8,128)(2,1)}), bf16[4,48,4096]{2,1,0:T(8,128)(2,1)}, u32[]{:S(2)}, u32[]{:S(2)}) async-start(bf16[4,48,4096]{2,1,0:T(8,128)(2,1)} %bitcast.20), calls=%async_computation.2 | async-start | bytes 3145728 | tf_op jit(solution)/shard_map/all_to_all | solution.py:196
  140.8 1.2 copy-start.5
  184.8 8.3 %collective-permute-start.9 = (bf16[4,9,256,256]{3,2,1,0:T(8,128)(2,1)}, bf16[4,9,256,256]{3,2,1,0:T(8,128)(2,1)}, u32[]{:S(2)}, u32[]{:S(2)}) collective-permute-start(bf16[4,9,256,256]{3,2,1,0:T(8,128)(2,1)} %bitcast.50), channel_id=1, source_target_pairs={{0,1},{1,0},{2,3},{3,2},{4,5},{5,4},{6,7},{7,6},{8,9},{9,8},{10,11... | collective-permute-start | bytes 14155784 | tf_op jit(solution)/shard_map/ppermute | solution.py:233
  206.7 24.8 %all-to-all-start.5 = ((bf16[4,48,4096]{2,1,0:T(8,128)(2,1)}), bf16[4,48,4096]{2,1,0:T(8,128)(2,1)S(1)}, u32[]{:S(2)}, u32[]{:S(2)}) async-start(bf16[4,48,4096]{2,1,0:T(8,128)(2,1)} %bitcast.26), calls=%async_computation.5 | async-start | bytes 3145728 | tf_op jit(solution)/shard_map/all_to_all | solution.py:196
  232.7 24.9 %all-to-all-start.4 = ((bf16[4,48,4096]{2,1,0:T(8,128)(2,1)}), bf16[4,48,4096]{2,1,0:T(8,128)(2,1)}, u32[]{:S(2)}, u32[]{:S(2)}) async-start(bf16[4,48,4096]{2,1,0:T(8,128)(2,1)} %bitcast.24), calls=%async_computation.4 | async-start | bytes 3145728 | tf_op jit(solution)/shard_map/all_to_all | solution.py:196
  238.4 3.1 copy-start
  238.4 1.5 copy-start.3
  252.9 1.2 copy-start.1
  257.6 48.0 %all-to-all-start.7 = ((bf16[4,48,4096]{2,1,0:T(8,128)(2,1)}), bf16[4,48,4096]{2,1,0:T(8,128)(2,1)}, u32[]{:S(2)}, u32[]{:S(2)}) async-start(bf16[4,48,4096]{2,1,0:T(8,128)(2,1)} %bitcast.37), calls=%async_computation.7 | async-start | bytes 3145728 | tf_op jit(solution)/shard_map/all_to_all | solution.py:196
  263.4 25.5 %collective-permute-start.10 = (bf16[64,4096]{1,0:T(8,128)(2,1)S(1)}, bf16[64,4096]{1,0:T(8,128)(2,1)S(1)}, u32[]{:S(2)}, u32[]{:S(2)}) collective-permute-start(bf16[64,4096]{1,0:T(8,128)(2,1)S(1)} %get-tuple-element.49), channel_id=1, source_target_pairs={{0,192},{64,0},{128,64},{192,128},{1,193},{65,1},{129,65},{193,129... | collective-permute-start | bytes 1572872 | tf_op jit(solution)/shard_map/ppermute | solution.py:242
  266.5 46.8 %collective-permute-start.12 = (bf16[64,4096]{1,0:T(8,128)(2,1)S(1)}, bf16[64,4096]{1,0:T(8,128)(2,1)S(1)}, u32[]{:S(2)}, u32[]{:S(2)}) collective-permute-start(bf16[64,4096]{1,0:T(8,128)(2,1)S(1)} %get-tuple-element.50), channel_id=1, source_target_pairs={{0,64},{64,128},{128,192},{192,0},{1,65},{65,129},{129,193},{193,1... | collective-permute-start | bytes 1572872 | tf_op jit(solution)/shard_map/ppermute | solution.py:242
  305.6 22.7 %all-to-all-start.6 = ((bf16[4,48,4096]{2,1,0:T(8,128)(2,1)}), bf16[4,48,4096]{2,1,0:T(8,128)(2,1)S(1)}, u32[]{:S(2)}, u32[]{:S(2)}) async-start(bf16[4,48,4096]{2,1,0:T(8,128)(2,1)} %bitcast.28), calls=%async_computation.6 | async-start | bytes 3145728 | tf_op jit(solution)/shard_map/all_to_all | solution.py:196
  310.4 42.1 %collective-permute-start.11 = (bf16[128,4096]{1,0:T(8,128)(2,1)}, bf16[128,4096]{1,0:T(8,128)(2,1)}, u32[]{:S(2)}, u32[]{:S(2)}) collective-permute-start(bf16[128,4096]{1,0:T(8,128)(2,1)} %combine.5.refs_8_), channel_id=1, source_target_pairs={{0,192},{64,0},{128,64},{192,128},{1,193},{65,1},{129,65},{193,129... | collective-permute-start | bytes 3145736 | tf_op jit(solution)/shard_map/ppermute | solution.py:249
  316.4 44.1 %collective-permute-start.13 = (bf16[128,4096]{1,0:T(8,128)(2,1)S(1)}, bf16[128,4096]{1,0:T(8,128)(2,1)}, u32[]{:S(2)}, u32[]{:S(2)}) collective-permute-start(bf16[128,4096]{1,0:T(8,128)(2,1)S(1)} %combine.7), channel_id=1, source_target_pairs={{0,64},{64,128},{128,192},{192,0},{1,65},{65,129},{129,193},{193,1... | collective-permute-start | bytes 3145736 | tf_op jit(solution)/shard_map/ppermute | solution.py:249
  (3 other events, 3.0 us)
Sparse Core Ops, SparseCore 0:
  12.8 57.4 all-gather.4
  100.5 53.2 all-gather.6

commit v3 on v2

v3 whole, which is shorter than its diff:
```python
import functools

import jax
import jax.numpy as jnp
from jax import lax
from jax.experimental import pallas as pl
from jax.experimental.pallas import tpu as pltpu
from jax.sharding import Mesh, PartitionSpec as P

BF, F32 = jnp.bfloat16, jnp.float32
ZH, YS, XS = 4, 4, 4
PARAMS = pltpu.CompilerParams(vmem_limit_bytes=56 << 20)
BLOCK = 256
TILE = 1024


def ring(step):
    return [(i, (i + step) % ZH) for i in range(ZH)]


def pack_kernel(up_ref, down_ref, out_ref):
    step = pl.program_id(0)

    @pl.when(step < 2)
    def _():
        for n in range(3):
            out_ref[n] = up_ref[:, n * BLOCK : (n + 1) * BLOCK]

    @pl.when(step == 2)
    def _():
        for n in range(3):
            out_ref[n] = down_ref[n * BLOCK : (n + 1) * BLOCK, :]


def pack_shards(up, down):
    return pl.pallas_call(
        pack_kernel,
        grid=(3,),
        out_shape=jax.ShapeDtypeStruct((9, BLOCK, BLOCK), BF),
        in_specs=[
            pl.BlockSpec((BLOCK, 3 * BLOCK), lambda s: (0, jnp.minimum(s, 1))),
            pl.BlockSpec((3 * BLOCK, BLOCK), lambda s: (0, 0)),
        ],
        out_specs=pl.BlockSpec((3, BLOCK, BLOCK), lambda s: (s, 0, 0)),
        compiler_params=PARAMS,
        name="pack",
    )(up, down)


def plan_kernel(group_ref, *refs):
    metas, (pick_ref, high_ref, low_ref) = refs[:-3], refs[-3:]
    rows = metas[0].shape[1]
    slots = pick_ref.shape[1] // YS
    group = group_ref[0]
    named, gates = [], []
    for meta_ref in metas:
        ids, weights = meta_ref[0:4, :], meta_ref[4:8, :]
        for y in range(YS):
            match = ids == (group * YS + y).astype(F32)
            named.append(jnp.sum(match.astype(F32), axis=0, keepdims=True))
            gates.append(jnp.sum(jnp.where(match, weights, 0.0), axis=0, keepdims=True))
    stacked = jnp.concatenate(named, axis=0)
    earlier = lax.broadcasted_iota(jnp.int32, (rows, rows), 0)
    later = lax.broadcasted_iota(jnp.int32, (rows, rows), 1)
    rank = jnp.dot(
        stacked.astype(BF), (earlier < later).astype(F32).astype(BF), preferred_element_type=F32
    )
    slot = lax.broadcasted_iota(jnp.int32, (slots, rows), 0).astype(F32)
    for k in range(len(metas)):
        for y in range(YS):
            i = k * YS + y
            here = (rank[i : i + 1, :] == slot) & (named[i] > 0.5)
            at = slice(y * slots, (y + 1) * slots)
            scaled = jnp.where(here, gates[i], 0.0)
            high = scaled.astype(BF)
            pick_ref[k, at, :] = here.astype(F32).astype(BF)
            high_ref[k, at, :] = high
            low_ref[k, at, :] = (scaled - high.astype(F32)).astype(BF)


def plan(group, slots, *metas):
    out = jax.ShapeDtypeStruct((len(metas), YS * slots, metas[0].shape[1]), BF)
    return pl.pallas_call(
        plan_kernel,
        out_shape=(out, out, out),
        in_specs=[pl.BlockSpec(memory_space=pltpu.SMEM)] + [pl.BlockSpec()] * len(metas),
        compiler_params=PARAMS,
        name="plan",
    )(group, *metas)


def gather_kernel(pieces, pick_ref, *refs):
    blocks, out_ref = refs[:-1], refs[-1]
    slots = out_ref.shape[2]
    for i in range(pick_ref.shape[0]):
        rows = jnp.concatenate([ref[...] for ref in blocks[i * pieces : (i + 1) * pieces]], axis=0)
        got = jnp.dot(pick_ref[i], rows, preferred_element_type=F32).astype(BF)
        for y in range(YS):
            out_ref[y, i] = got[y * slots : (y + 1) * slots]


def gather(pick, *blocks):
    sources, routes, _ = pick.shape
    width = blocks[0].shape[1]
    shape = (YS, sources, routes // YS)
    return pl.pallas_call(
        functools.partial(gather_kernel, len(blocks) // sources),
        grid=(width // TILE,),
        out_shape=jax.ShapeDtypeStruct(shape + (width,), BF),
        in_specs=[pl.BlockSpec(pick.shape, lambda j: (0, 0, 0))]
        + [pl.BlockSpec((b.shape[0], TILE), lambda j: (0, j)) for b in blocks],
        out_specs=pl.BlockSpec(shape + (TILE,), lambda j: (0, 0, 0, j)),
        compiler_params=PARAMS,
        name="gather",
    )(pick, *blocks)


def expert_kernel(place_ref, x_ref, *refs):
    ins, downs, outs = refs[0:4], refs[4:8], refs[8:-2]
    sums_ref, hidden_ref = refs[-2:]
    step = pl.program_id(0)
    parts = sums_ref.shape[0]
    half = parts // 2
    each = XS // len(outs)

    def columns(x, r):
        return pl.ds(pl.multiple_of((x * 4 + place_ref[r]) * BLOCK, BLOCK), BLOCK)

    @pl.when(step == 0)
    def _():
        sums_ref[...] = jnp.zeros_like(sums_ref)

    @pl.when(step < XS)
    def _():
        rows = [x_ref[:, columns(step, r)] for r in range(4)]
        for n in range(parts):
            sums_ref[n] += sum(
                jnp.dot(rows[r], ins[r][n], preferred_element_type=F32) for r in range(4)
            )

    @pl.when(step == XS)
    def _():
        for n in range(half):
            g, u = sums_ref[n], sums_ref[half + n]
            hidden_ref[n] = (g / (1.0 + jnp.exp(-g)) * u).astype(BF)

    for x in range(XS):

        @pl.when(step == XS + x)
        def _(x=x):
            for r in range(4):
                made = sum(
                    jnp.dot(hidden_ref[n], downs[r][n], preferred_element_type=F32)
                    for n in range(half)
                )
                outs[x // each][:, columns(x % each, r)] = made.astype(BF)


def expert(place, rows, packs, pieces):
    count, width = rows.shape
    half = packs[0].shape[1] // 3
    out = jax.ShapeDtypeStruct((count, width // pieces), BF)
    return pl.pallas_call(
        expert_kernel,
        grid_spec=pltpu.PrefetchScalarGridSpec(
            num_scalar_prefetch=1,
            grid=(2 * XS,),
            in_specs=[pl.BlockSpec((count, width), lambda s, p: (0, 0))]
            + [
                pl.BlockSpec(
                    (pl.Squeezed(), 2 * half, BLOCK, BLOCK),
                    lambda s, p: (jnp.minimum(s, XS - 1), 0, 0, 0),
                )
            ]
            * 4
            + [
                pl.BlockSpec(
                    (pl.Squeezed(), half, BLOCK, BLOCK),
                    lambda s, p: (jnp.maximum(s - XS, 0), 2, 0, 0),
                )
            ]
            * 4,
            out_specs=[pl.BlockSpec(out.shape, lambda s, p: (0, 0))] * pieces,
            scratch_shapes=[
                pltpu.VMEM((2 * half, count, BLOCK), F32),
                pltpu.VMEM((half, count, BLOCK), BF),
            ],
        ),
        out_shape=[out] * pieces,
        compiler_params=PARAMS,
        name="expert",
    )(place, rows, *packs, *packs)


def weighted(high_ref, low_ref, i, rows_ref):
    rows = jnp.concatenate([rows_ref[y, i] for y in range(YS)], axis=0)
    return sum(
        lax.dot_general(s[i], rows, (((0,), (0,)), ((), ())), preferred_element_type=F32)
        for s in (high_ref, low_ref)
    )


def split_kernel(high_ref, low_ref, rows_ref, top_ref, bottom_ref):
    total = weighted(high_ref, low_ref, 0, rows_ref).astype(BF)
    half = top_ref.shape[0]
    top_ref[...], bottom_ref[...] = total[:half], total[half:]


def add_kernel(high_ref, low_ref, rows_ref, top_ref, bottom_ref, below_ref, above_ref):
    half = top_ref.shape[0]
    below = weighted(high_ref, low_ref, 0, rows_ref)
    above = weighted(high_ref, low_ref, 1, rows_ref)
    below_ref[:half, :] = (below[:half] + top_ref[...].astype(F32)).astype(BF)
    below_ref[half:, :] = below[half:].astype(BF)
    above_ref[:half, :] = above[:half].astype(BF)
    above_ref[half:, :] = (above[half:] + bottom_ref[...].astype(F32)).astype(BF)


def last_kernel(high_ref, low_ref, rows_ref, *refs):
    left, right, out_ref = refs[0:2], refs[2:4], refs[4]
    total = weighted(high_ref, low_ref, 0, rows_ref)
    first = pl.program_id(0) < pl.num_programs(0) // 2

    @pl.when(first)
    def _():
        out_ref[...] = (total + left[0][...].astype(F32) + left[1][...].astype(F32)).astype(BF)

    @pl.when(jnp.logical_not(first))
    def _():
        out_ref[...] = (total + right[0][...].astype(F32) + right[1][...].astype(F32)).astype(BF)


def combine(kernel, plans, rows, more, counts):
    _, high, low = plans
    width = rows.shape[-1]
    table = pl.BlockSpec(high.shape, lambda j: (0, 0, 0))
    return pl.pallas_call(
        kernel,
        grid=(width // TILE,),
        out_shape=[jax.ShapeDtypeStruct((n, width), BF) for n in counts],
        in_specs=[table, table, pl.BlockSpec(rows.shape[:-1] + (TILE,), lambda j: (0, 0, 0, j))]
        + [pl.BlockSpec((a.shape[0], TILE), lambda j, at=at: (0, at(j))) for a, at in more],
        out_specs=[pl.BlockSpec((n, TILE), lambda j: (0, j)) for n in counts],
        compiler_params=PARAMS,
        name="combine",
    )(high, low, rows, *[a for a, _ in more])


def over_y(rows, shape):
    return lax.all_to_all(
        rows.reshape(YS, -1, rows.shape[-1]), "y", split_axis=0, concat_axis=0, tiled=True
    ).reshape(shape)


def on_device(tokens, route_ids, gate_values, w_gate_up, w_down):
    tok_rows, top = route_ids.shape
    model = tokens.shape[1]
    slots = 3 * tok_rows * top // (2 * ZH * YS)
    half = tok_rows // 2
    swap = [(0, 1), (1, 0)]
    group = lax.axis_index("zh").reshape(1)
    barrier = lax.optimization_barrier
    pack = pack_shards(w_gate_up[0], w_down[0])
    meta = jnp.concatenate([route_ids.astype(F32).T, gate_values.T], axis=0)

    near = [lax.ppermute(tokens, "zh", ring(k)) for k in (1, 3)]
    near_metas = [lax.ppermute(meta, "zh", ring(k)) for k in (1, 3)]
    swapped = lax.ppermute(pack, "zl", swap)
    mine = lax.all_gather(pack, "x")
    own = plan(group, slots, meta)
    arrived_own = over_y(gather(own[0], tokens), (-1, model))
    near, near_metas, swapped, arrived_own = barrier((near, near_metas, swapped, arrived_own))
    other = lax.all_gather(swapped, "x")

    sides = plan(group, slots, *near_metas)
    top, bottom, sent = barrier((near[0][:half], near[1][half:], gather(sides[0], *near)))
    arrived_sides = over_y(sent, (-1, model))
    far = [lax.ppermute(top, "zh", ring(1)), lax.ppermute(bottom, "zh", ring(3))]
    far_meta = lax.ppermute(near_metas[0], "zh", ring(1))
    far, far_meta, mine, arrived_sides = barrier((far, far_meta, mine, arrived_sides))
    mine_swapped = lax.ppermute(mine, "core", swap)
    across = plan(group, slots, far_meta)
    arrived_across = over_y(gather(across[0], *far), (-1, model))
    packs = [mine, mine_swapped, other, lax.ppermute(other, "core", swap)]
    zl, core = lax.axis_index("zl"), lax.axis_index("core")
    place = jnp.stack([zl * 2 + core, zl * 2 + 1 - core, (1 - zl) * 2 + core, (1 - zl) * 2 + 1 - core])

    made_sides = expert(place, arrived_sides, packs, 2)
    (made_own,) = expert(place, arrived_own, packs, 1)
    made_sides, made_own, arrived_across = barrier((made_sides, made_own, arrived_across))
    (made,) = expert(place, arrived_across, packs, 1)

    back = over_y(made, (YS, 1, slots, model))
    parts = combine(split_kernel, across, back, [], (half, half))
    passed = [lax.ppermute(parts[0], "zh", ring(3)), lax.ppermute(parts[1], "zh", ring(1))]
    home = []
    for piece in range(2):
        if piece == 0:
            rows, back = barrier((made_sides[0], back))
        else:
            rows, passed = barrier((made_sides[1], passed))
        back = over_y(rows, (YS, 2, slots, model // 2))
        shift = lambda j, at=piece * (model // 2 // TILE): j + at
        below, above = combine(
            add_kernel, sides, back, [(p, shift) for p in passed], (tok_rows, tok_rows)
        )
        if piece == 1:
            made_own, home, below = barrier((made_own, home, below))
        home = home + [lax.ppermute(below, "zh", ring(3)), lax.ppermute(above, "zh", ring(1))]
    back = over_y(made_own, (YS, 1, slots, model))
    steps = model // 2 // TILE
    left, right = lambda j: jnp.minimum(j, steps - 1), lambda j: jnp.maximum(j - steps, 0)
    more = [(home[0], left), (home[1], left), (home[2], right), (home[3], right)]
    return combine(last_kernel, own, back, more, (tok_rows,))[0]


def solution(mesh):
    split = Mesh(mesh.devices.reshape(ZH, YS, XS, 2, 2), ("zh", "y", "x", "zl", "core"))
    owner, shard = ("zh", "y"), ("x", "zl", "core")
    every = owner + shard
    in_specs = (P(every, None),) * 3 + (P(owner, shard, None), P(owner, None, shard))
    return jax.shard_map(
        on_device, mesh=split, in_specs=in_specs, out_specs=P(every, None), check_vma=False
    )
```

time: 373 us -> 340 us (0.912)
  waiting for transfers between devices: 179 us -> 154 us
  local copies, waits for them, and re-layouts: 17.2 us -> 9.03 us
  Pallas kernels: 71.9 us -> 79.2 us
  starting transfers between devices: 60.2 us -> 54.4 us
    all_to_all x7 -> x6, waiting for transfers between devices: 37.5 us -> 22.5 us  [over_y(): lax.all_to_all(rows.reshape(YS, -1, rows.shape[-1]), 'y', split_axis=0, c...]
    pallas_call x8, Pallas kernels: 20.3 us -> 30.2 us  [the longest x4 14.9 us: combine(): pl.pallas_call(kernel, grid=(width // TILE,), out_shape=[jax.ShapeDtypeSt...]
    ppermute x1, waiting for transfers between devices: 8.16 us -> 1.03 us  [on_device(): packs = [mine, mine_swapped, other, lax.ppermute(other, 'core', swap)]]
    pallas_call x4 -> x3, Pallas kernels: 51.2 us -> 44.4 us  [expert(): pl.pallas_call(expert_kernel, grid_spec=pltpu.PrefetchScalarGridSpec(num_...]
    ppermute x9 -> x11, waiting for transfers between devices: 134 us -> 127 us  [the longest x2 55.7 us: on_device(): near_metas = [lax.ppermute(meta, 'zh', ring(k)) for k in (1, 3)]]
    all_to_all x7 -> x6, starting transfers between devices: 35.9 us -> 29.4 us  [over_y(): lax.all_to_all(rows.reshape(YS, -1, rows.shape[-1]), 'y', split_axis=0, c...]
    pallas_call x2 -> x3, Pallas kernels: 0.37 us -> 4.56 us  [plan(): pl.pallas_call(plan_kernel, out_shape=(out, out, out), in_specs=[pl.Block...]
    unnamed x25 -> x40, local copies, waits for them, and re-layouts: 9.7 us -> 6.16 us
  transfers between devices with their start and end apart: 23 -> 24, of which waited for: 11 -> 11; matrix products, arithmetic and copies ran while one was open for 1% -> 1% of each run, Pallas kernels for 16% -> 17%
where the time goes in v3:
time: 340 us; the launch traced here: 337 us
  waiting for transfers between devices  154 us (45%)
  Pallas kernels  79.2 us (23%)
  starting transfers between devices  54.4 us (16%)
  blocking collectives  25.7 us (8%)
  between operations  13.5 us (4%)
  local copies, waits for them, and re-layouts  9.03 us (3%)
    ppermute x2, waiting for transfers between devices, on_device(): near_metas = [lax.ppermute(meta, 'zh', ring(k)) for k in (1, 3)]  55.7 us
    pallas_call x3, Pallas kernels, expert(): pl.pallas_call(expert_kernel, grid_spec=pltpu.PrefetchScalarGridSpec(num_...  44.4 us
    all_to_all x6, starting transfers between devices, over_y(): lax.all_to_all(rows.reshape(YS, -1, rows.shape[-1]), 'y', split_axis=0, c...  29.4 us
    all_to_all x1, blocking collectives, over_y(): lax.all_to_all(rows.reshape(YS, -1, rows.shape[-1]), 'y', split_axis=0, c...  25.7 us
    ppermute x2, waiting for transfers between devices, on_device(): lax.ppermute(below, 'zh', ring(3))  23.8 us
    all_to_all x6, waiting for transfers between devices, over_y(): lax.all_to_all(rows.reshape(YS, -1, rows.shape[-1]), 'y', split_axis=0, c...  22.5 us
    ppermute x1, waiting for transfers between devices, on_device(): lax.ppermute(parts[0], 'zh', ring(3))  21.8 us
    ppermute x1, waiting for transfers between devices, on_device(): far_meta = lax.ppermute(near_metas[0], 'zh', ring(1))  20.3 us
  transfers between devices with their start and end apart: 24, of which 11 were waited for; matrix products, arithmetic and copies ran while one was open for 1% of the time, Pallas kernels for 17%

profile of v3, /device:TPU:10, one launch (start us, length us, event | category | flops | bytes accessed | tf_op | source)
XLA Modules:
  0.0 336.9 jit_solution(15144810054882257498)
XLA Ops:
  6.5 2.7 pack.1
  13.4 4.0 %gather.3 = bf16[4,1,48,4096]{3,2,1,0:T(8,128)(2,1)} custom-call(bf16[1,192,128]{2,1,0:T(8,128)(2,1)} %get-tuple-element.50.pick_ref, bf16[128,4096]{1,0:T(8,128)(2,1)} %refs_0_.1), custom_call_target="tpu_custom_call" | custom-call | tf_op jit(solution)/shard_map/gather/pallas_call | solution.py:106
  17.3 5.0 %all-to-all-start = ((bf16[4,48,4096]{2,1,0:T(8,128)(2,1)}), bf16[4,48,4096]{2,1,0:T(8,128)(2,1)S(1)}, u32[]{:S(2)}, u32[]{:S(2)}) async-start(bf16[4,48,4096]{2,1,0:T(8,128)(2,1)} %bitcast.46), calls=%async_computation | async-start | bytes 3145728 | tf_op jit(solution)/shard_map/all_to_all | solution.py:250
  22.4 3.3 collective-permute-start
  29.2 2.7 collective-permute-start.3
  31.9 55.7 %collective-permute-done.2.refs_0_ = f32[8,128]{1,0:T(8,128)S(1)} collective-permute-done((f32[8,128]{1,0:T(8,128)S(1)}, f32[8,128]{1,0:T(8,128)S(1)}, u32[]{:S(2)}, u32[]{:S(2)}) %collective-permute-start.2) | collective-permute-done | bytes 4128 | tf_op jit(solution)/shard_map/ppermute | solution.py:267
  92.2 4.7 %gather.4 = bf16[4,2,48,4096]{3,2,1,0:T(8,128)(2,1)} custom-call(bf16[2,192,128]{2,1,0:T(8,128)(2,1)} %get-tuple-element.55.pick_ref, bf16[128,4096]{1,0:T(8,128)(2,1)} %copy-done.5, bf16[128,4096]{1,0:T(8,128)(2,1)} %collective-permute-done.1.refs_1_), custom_call_target="tpu_custom_call" | custom-call | tf_op jit(solution)/shard_map/gather/pallas_call | solution.py:106
  96.9 5.0 %all-to-all-start.1 = ((bf16[4,96,4096]{2,1,0:T(8,128)(2,1)}), bf16[4,96,4096]{2,1,0:T(8,128)(2,1)S(1)}, u32[]{:S(2)}, u32[]{:S(2)}) async-start(bf16[4,96,4096]{2,1,0:T(8,128)(2,1)} %bitcast.40), calls=%async_computation.1 | async-start | bytes 6291456 | tf_op jit(solution)/shard_map/all_to_all | solution.py:250
  102.0 4.1 %collective-permute-start.6 = (bf16[64,4096]{1,0:T(8,128)(2,1)}, bf16[64,4096]{1,0:T(8,128)(2,1)}, u32[]{:S(2)}, u32[]{:S(2)}) collective-permute-start(bf16[64,4096]{1,0:T(8,128)(2,1)} %slice.7), channel_id=1, source_target_pairs={{0,192},{64,0},{128,64},{192,128},{1,193},{65,1},{129,65},{193,129... | collective-permute-start | bytes 1572872 | tf_op jit(solution)/shard_map/ppermute | solution.py:278
  106.1 20.3 %collective-permute-done.7.refs_0_ = f32[8,128]{1,0:T(8,128)S(1)} collective-permute-done((f32[8,128]{1,0:T(8,128)S(1)}, f32[8,128]{1,0:T(8,128)S(1)}, u32[]{:S(2)}, u32[]{:S(2)}) %collective-permute-start.7) | collective-permute-done | bytes 4128 | tf_op jit(solution)/shard_map/ppermute | solution.py:279
  127.2 10.0 %all-to-all-done.1 = bf16[4,96,4096]{2,1,0:T(8,128)(2,1)S(1)} async-done(((bf16[4,96,4096]{2,1,0:T(8,128)(2,1)}), bf16[4,96,4096]{2,1,0:T(8,128)(2,1)S(1)}, u32[]{:S(2)}, u32[]{:S(2)}) %all-to-all-start.1) | async-done | bytes 3145760 | tf_op jit(solution)/shard_map/all_to_all | solution.py:250
  137.2 2.9 all-gather.7.cloned.1.call-done
  141.7 4.0 %gather.5 = bf16[4,1,48,4096]{3,2,1,0:T(8,128)(2,1)} custom-call(bf16[1,192,128]{2,1,0:T(8,128)(2,1)} %get-tuple-element.66.pick_ref, bf16[64,4096]{1,0:T(8,128)(2,1)} %copy-done.11, bf16[64,4096]{1,0:T(8,128)(2,1)} %collective-permute-done.6.refs_1_), custom_call_target="tpu_custom_call" | custom-call | tf_op jit(solution)/shard_map/gather/pallas_call | solution.py:106
  145.7 4.9 %all-to-all-start.2 = ((bf16[4,48,4096]{2,1,0:T(8,128)(2,1)}), bf16[4,48,4096]{2,1,0:T(8,128)(2,1)}, u32[]{:S(2)}, u32[]{:S(2)}) async-start(bf16[4,48,4096]{2,1,0:T(8,128)(2,1)} %bitcast.45), calls=%async_computation.2 | async-start | bytes 3145728 | tf_op jit(solution)/shard_map/all_to_all | solution.py:250
  152.2 17.1 %expert.3 = (bf16[384,2048]{1,0:T(8,128)(2,1)}, bf16[384,2048]{1,0:T(8,128)(2,1)}) custom-call(s32[4]{0:T(128)} %pad_add_fusion.place_ref, bf16[384,4096]{1,0:T(8,128)(2,1)} %bitcast.41, bf16[4,9,256,256]{3,2,1,0:T(8,128)(2,1)} %bitcast.27, bf16[4,9,256,256]{3,2,1,0:T(8,128)(2,1)} %collective-permute-done.8.refs_1_.refs_5_, ...), custom_call_target="tpu_custom_call" | custom-call | tf_op jit(solution)/shard_map/expert/pallas_call | solution.py:163
  169.3 13.7 %expert.4 = bf16[192,4096]{1,0:T(8,128)(2,1)} custom-call(s32[4]{0:T(128)} %pad_add_fusion.place_ref, bf16[192,4096]{1,0:T(8,128)(2,1)} %bitcast.42, bf16[4,9,256,256]{3,2,1,0:T(8,128)(2,1)} %bitcast.29, bf16[4,9,256,256]{3,2,1,0:T(8,128)(2,1)} %collective-permute-done.8.refs_1_.refs_5_, bf16[4,9,256,256]{3,2,1,0:T(8,128)(2,1)} %bitcast.36, ...), custom_call_target="tpu_custom_call" | custom-call | tf_op jit(solution)/shard_map/expert/pallas_call | solution.py:163
  182.9 13.7 %expert.5 = bf16[192,4096]{1,0:T(8,128)(2,1)} custom-call(s32[4]{0:T(128)} %pad_add_fusion.place_ref, bf16[192,4096]{1,0:T(8,128)(2,1)} %bitcast.16.x_ref, bf16[4,9,256,256]{3,2,1,0:T(8,128)(2,1)} %bitcast.31, bf16[4,9,256,256]{3,2,1,0:T(8,128)(2,1)} %collective-permute-done.8.refs_1_.refs_5_, bf16[4,9,256,256]{3,2,1,0:T(8,128)(2,1)} %bitcast.38, ...), custom_call_target="tpu_custom_call" | custom-call | tf_op jit(solution)/shard_map/expert/pallas_call | solution.py:163
  196.6 25.7 %all_to_all.35 = bf16[4,48,4096]{2,1,0:T(8,128)(2,1)} all-to-all(bf16[4,48,4096]{2,1,0:T(8,128)(2,1)} %bitcast.43), channel_id=1, replica_groups=mesh['zh'=4,'y'=4,'x'=4,'zl'=2,'core'=2] {'y'}, dimensions={0} | all-to-all | bytes 3145728 | tf_op jit(solution)/shard_map/all_to_all | solution.py:250
  222.3 5.0 %all-to-all-start.4 = ((bf16[4,96,2048]{2,1,0:T(8,128)(2,1)}), bf16[4,96,2048]{2,1,0:T(8,128)(2,1)S(1)}, u32[]{:S(2)}, u32[]{:S(2)}) async-start(bf16[4,96,2048]{2,1,0:T(8,128)(2,1)} %bitcast.19), calls=%async_computation.4 | async-start | bytes 3145728 | tf_op jit(solution)/shard_map/all_to_all | solution.py:250
  227.3 4.0 %combine.4 = (bf16[64,4096]{1,0:T(8,128)(2,1)}, bf16[64,4096]{1,0:T(8,128)(2,1)}) custom-call(bf16[1,192,128]{2,1,0:T(8,128)(2,1)} %get-tuple-element.75.high_ref, bf16[1,192,128]{2,1,0:T(8,128)(2,1)} %get-tuple-element.76.low_ref, bf16[4,1,48,4096]{3,2,1,0:T(8,128)(2,1)} %bitcast.44), custom_call_target="tpu_custom_call" | custom-call | tf_op jit(solution)/shard_map/combine/pallas_call | solution.py:237
  234.3 21.8 %collective-permute-done.10.top_ref = bf16[64,4096]{1,0:T(8,128)(2,1)S(1)} collective-permute-done((bf16[64,4096]{1,0:T(8,128)(2,1)}, bf16[64,4096]{1,0:T(8,128)(2,1)S(1)}, u32[]{:S(2)}, u32[]{:S(2)}) %collective-permute-start.10) | collective-permute-done | bytes 524320 | tf_op jit(solution)/shard_map/ppermute | solution.py:295
  258.1 4.7 %all-to-all-start.5 = ((bf16[4,96,2048]{2,1,0:T(8,128)(2,1)}), bf16[4,96,2048]{2,1,0:T(8,128)(2,1)S(1)}, u32[]{:S(2)}, u32[]{:S(2)}) async-start(bf16[4,96,2048]{2,1,0:T(8,128)(2,1)} %bitcast.50), calls=%async_computation.5 | async-start | bytes 3145728 | tf_op jit(solution)/shard_map/all_to_all | solution.py:250
  262.8 3.0 combine.5
  265.8 3.4 %collective-permute-start.12 = (bf16[128,2048]{1,0:T(8,128)(2,1)}, bf16[128,2048]{1,0:T(8,128)(2,1)S(1)}, u32[]{:S(2)}, u32[]{:S(2)}) collective-permute-start(bf16[128,2048]{1,0:T(8,128)(2,1)} %get-tuple-element.79), channel_id=1, source_target_pairs={{0,192},{64,0},{128,64},{192,128},{1,193},{65,1},{129,65},{193,129... | collective-permute-start | bytes 1572872 | tf_op jit(solution)/shard_map/ppermute | solution.py:309
  269.2 12.6 %all-to-all-done.5 = bf16[4,96,2048]{2,1,0:T(8,128)(2,1)S(1)} async-done(((bf16[4,96,2048]{2,1,0:T(8,128)(2,1)}), bf16[4,96,2048]{2,1,0:T(8,128)(2,1)S(1)}, u32[]{:S(2)}, u32[]{:S(2)}) %all-to-all-start.5) | async-done | bytes 1572896 | tf_op jit(solution)/shard_map/all_to_all | solution.py:250
  283.0 3.1 combine.6
  286.0 5.3 %collective-permute-done.12.refs_0_ = bf16[128,2048]{1,0:T(8,128)(2,1)S(1)} collective-permute-done((bf16[128,2048]{1,0:T(8,128)(2,1)}, bf16[128,2048]{1,0:T(8,128)(2,1)S(1)}, u32[]{:S(2)}, u32[]{:S(2)}) %collective-permute-start.12) | collective-permute-done | bytes 524320 | tf_op jit(solution)/shard_map/ppermute | solution.py:309
  291.4 4.2 %collective-permute-done.13.refs_1_ = bf16[128,2048]{1,0:T(8,128)(2,1)S(1)} collective-permute-done((bf16[128,2048]{1,0:T(8,128)(2,1)}, bf16[128,2048]{1,0:T(8,128)(2,1)S(1)}, u32[]{:S(2)}, u32[]{:S(2)}) %collective-permute-start.13) | collective-permute-done | bytes 524320 | tf_op jit(solution)/shard_map/ppermute | solution.py:309
  296.4 4.8 %all-to-all-start.6 = ((bf16[4,48,4096]{2,1,0:T(8,128)(2,1)}), bf16[4,48,4096]{2,1,0:T(8,128)(2,1)S(1)}, u32[]{:S(2)}, u32[]{:S(2)}) async-start(bf16[4,48,4096]{2,1,0:T(8,128)(2,1)} %bitcast.23), calls=%async_computation.6 | async-start | bytes 3145728 | tf_op jit(solution)/shard_map/all_to_all | solution.py:250
  301.6 2.5 collective-permute-start.15
  304.1 18.4 %collective-permute-done.14.refs_2_ = bf16[128,2048]{1,0:T(8,128)(2,1)S(1)} collective-permute-done((bf16[128,2048]{1,0:T(8,128)(2,1)}, bf16[128,2048]{1,0:T(8,128)(2,1)S(1)}, u32[]{:S(2)}, u32[]{:S(2)}) %collective-permute-start.14) | collective-permute-done | bytes 524320 | tf_op jit(solution)/shard_map/ppermute | solution.py:309
  325.3 4.8 %combine.7 = bf16[128,4096]{1,0:T(8,128)(2,1)} custom-call(bf16[1,192,128]{2,1,0:T(8,128)(2,1)} %get-tuple-element.48.high_ref, bf16[1,192,128]{2,1,0:T(8,128)(2,1)} %get-tuple-element.49.low_ref, bf16[4,1,48,4096]{3,2,1,0:T(8,128)(2,1)} %bitcast.48, bf16[128,2048]{1,0:T(8,128)(2,1)} %copy-done.7, bf16[128,2048]{1,0:T(8,128)(2,1)} %copy-done.8, ...), custom_call_target="tpu_custom_call" | custom-call | tf_op jit(solution)/shard_map/combine/pallas_call | solution.py:237
  (78 shorter events, 26.3 us)
Async XLA Ops:
  6.5 130.7 %all-gather.5.cloned.1.call-start = ((), (), s32[]{:S(2)}) async-start(), calls=%async_computation.7 | async-start | bytes 5898240 | tf_op jit(solution)/shard_map/all_gather | solution.py:269
  6.5 4.7 %copy-start.17 = (s32[128,4]{0,1:T(4,128)S(1)}, s32[128,4]{0,1:T(4,128)}, u32[]{:S(2)}) copy-start(s32[128,4]{0,1:T(4,128)} %param.6) | copy-start | bytes 6148
  6.5 4.7 %copy-start.18 = (f32[128,4]{0,1:T(4,128)S(1)}, f32[128,4]{0,1:T(4,128)}, u32[]{:S(2)}) copy-start(f32[128,4]{0,1:T(4,128)} %param.7) | copy-start | bytes 6148
  9.3 78.5 %collective-permute-start.4 = (bf16[9,256,256]{2,1,0:T(8,128)(2,1)}, bf16[9,256,256]{2,1,0:T(8,128)(2,1)}, u32[]{:S(2)}, u32[]{:S(2)}) collective-permute-start(bf16[9,256,256]{2,1,0:T(8,128)(2,1)} %pack.1), channel_id=1, source_target_pairs={{0,2},{2,0},{1,3},{3,1},{4,6},{6,4},{5,7},{7,5},{8,10},{10,8},{9,1... | collective-permute-start | bytes 3538952 | tf_op jit(solution)/shard_map/ppermute | solution.py:268
  17.3 10.5 %copy-start.12 = (f32[8,128]{1,0:T(8,128)S(1)}, f32[8,128]{1,0:T(8,128)}, u32[]{:S(2)}) copy-start(f32[8,128]{1,0:T(8,128)} %pad_maximum_fusion.refs_0_) | copy-start | bytes 12292
  17.3 70.4 %all-to-all-start = ((bf16[4,48,4096]{2,1,0:T(8,128)(2,1)}), bf16[4,48,4096]{2,1,0:T(8,128)(2,1)S(1)}, u32[]{:S(2)}, u32[]{:S(2)}) async-start(bf16[4,48,4096]{2,1,0:T(8,128)(2,1)} %bitcast.46), calls=%async_computation | async-start | bytes 3145728 | tf_op jit(solution)/shard_map/all_to_all | solution.py:250
  22.4 117.8 %all-gather.7.cloned.1.call-start = ((), (), s32[]{:S(2)}) async-start(), calls=%async_computation.8 | async-start | bytes 5898240 | tf_op jit(solution)/shard_map/all_gather | solution.py:273
  22.4 65.3 %collective-permute-start = (bf16[128,4096]{1,0:T(8,128)(2,1)}, bf16[128,4096]{1,0:T(8,128)(2,1)S(1)}, u32[]{:S(2)}, u32[]{:S(2)}) collective-permute-start(bf16[128,4096]{1,0:T(8,128)(2,1)} %refs_0_.1), channel_id=1, source_target_pairs={{0,64},{64,128},{128,192},{192,0},{1,65},{65,129},{129,193},{193,1... | collective-permute-start | bytes 3145736 | tf_op jit(solution)/shard_map/ppermute | solution.py:266
  25.7 62.1 %collective-permute-start.1 = (bf16[128,4096]{1,0:T(8,128)(2,1)}, bf16[128,4096]{1,0:T(8,128)(2,1)}, u32[]{:S(2)}, u32[]{:S(2)}) collective-permute-start(bf16[128,4096]{1,0:T(8,128)(2,1)} %refs_0_.1), channel_id=1, source_target_pairs={{0,192},{64,0},{128,64},{192,128},{1,193},{65,1},{129,65},{193,129... | collective-permute-start | bytes 3145736 | tf_op jit(solution)/shard_map/ppermute | solution.py:266
  27.8 59.9 %collective-permute-start.2 = (f32[8,128]{1,0:T(8,128)S(1)}, f32[8,128]{1,0:T(8,128)S(1)}, u32[]{:S(2)}, u32[]{:S(2)}) collective-permute-start(f32[8,128]{1,0:T(8,128)S(1)} %copy-done.12), channel_id=1, source_target_pairs={{0,64},{64,128},{128,192},{192,0},{1,65},{65,129},{129,193},{193,1... | collective-permute-start | bytes 12296 | tf_op jit(solution)/shard_map/ppermute | solution.py:267
  29.2 58.4 %collective-permute-start.3 = (f32[8,128]{1,0:T(8,128)S(1)}, f32[8,128]{1,0:T(8,128)S(1)}, u32[]{:S(2)}, u32[]{:S(2)}) collective-permute-start(f32[8,128]{1,0:T(8,128)S(1)} %copy-done.12), channel_id=1, source_target_pairs={{0,192},{64,0},{128,64},{192,128},{1,193},{65,1},{129,65},{193,129... | collective-permute-start | bytes 12296 | tf_op jit(solution)/shard_map/ppermute | solution.py:267
  96.9 9.2 %copy-start.15 = (f32[8,128]{1,0:T(8,128)S(1)}, f32[8,128]{1,0:T(8,128)}, u32[]{:S(2)}) copy-start(f32[8,128]{1,0:T(8,128)} %copy-done.14) | copy-start | bytes 12292
  96.9 40.3 %all-to-all-start.1 = ((bf16[4,96,4096]{2,1,0:T(8,128)(2,1)}), bf16[4,96,4096]{2,1,0:T(8,128)(2,1)S(1)}, u32[]{:S(2)}, u32[]{:S(2)}) async-start(bf16[4,96,4096]{2,1,0:T(8,128)(2,1)} %bitcast.40), calls=%async_computation.1 | async-start | bytes 6291456 | tf_op jit(solution)/shard_map/all_to_all | solution.py:250
  102.0 24.5 %collective-permute-start.5 = (bf16[64,4096]{1,0:T(8,128)(2,1)}, bf16[64,4096]{1,0:T(8,128)(2,1)S(1)}, u32[]{:S(2)}, u32[]{:S(2)}) collective-permute-start(bf16[64,4096]{1,0:T(8,128)(2,1)} %slice.6), channel_id=1, source_target_pairs={{0,64},{64,128},{128,192},{192,0},{1,65},{65,129},{129,193},{193,1... | collective-permute-start | bytes 1572872 | tf_op jit(solution)/shard_map/ppermute | solution.py:278
  102.0 25.3 %collective-permute-start.6 = (bf16[64,4096]{1,0:T(8,128)(2,1)}, bf16[64,4096]{1,0:T(8,128)(2,1)}, u32[]{:S(2)}, u32[]{:S(2)}) collective-permute-start(bf16[64,4096]{1,0:T(8,128)(2,1)} %slice.7), channel_id=1, source_target_pairs={{0,192},{64,0},{128,64},{192,128},{1,193},{65,1},{129,65},{193,129... | collective-permute-start | bytes 1572872 | tf_op jit(solution)/shard_map/ppermute | solution.py:278
  106.1 20.3 %collective-permute-start.7 = (f32[8,128]{1,0:T(8,128)S(1)}, f32[8,128]{1,0:T(8,128)S(1)}, u32[]{:S(2)}, u32[]{:S(2)}) collective-permute-start(f32[8,128]{1,0:T(8,128)S(1)} %copy-done.15), channel_id=1, source_target_pairs={{0,64},{64,128},{128,192},{192,0},{1,65},{65,129},{129,193},{193,1... | collective-permute-start | bytes 12296 | tf_op jit(solution)/shard_map/ppermute | solution.py:279
  126.4 13.7 %copy-start.13 = (f32[8,128]{1,0:T(8,128)}, f32[8,128]{1,0:T(8,128)S(1)}, u32[]{:S(2)}) copy-start(f32[8,128]{1,0:T(8,128)S(1)} %collective-permute-done.7.refs_0_) | copy-start | bytes 12292
  137.2 8.5 %copy-start = (bf16[4,96,4096]{2,1,0:T(8,128)(2,1)}, bf16[4,96,4096]{2,1,0:T(8,128)(2,1)S(1)}, u32[]{:S(2)}) copy-start(bf16[4,96,4096]{2,1,0:T(8,128)(2,1)S(1)} %all-to-all-done.1) | copy-start | bytes 9437188
  137.2 14.0 %collective-permute-start.8 = (bf16[4,9,256,256]{3,2,1,0:T(8,128)(2,1)}, bf16[4,9,256,256]{3,2,1,0:T(8,128)(2,1)}, u32[]{:S(2)}, u32[]{:S(2)}) collective-permute-start(bf16[4,9,256,256]{3,2,1,0:T(8,128)(2,1)} %bitcast.26), channel_id=1, source_target_pairs={{0,1},{1,0},{2,3},{3,2},{4,5},{5,4},{6,7},{7,6},{8,9},{9,8},{10,11... | collective-permute-start | bytes 14155784 | tf_op jit(solution)/shard_map/ppermute | solution.py:281
  140.2 12.1 %collective-permute-start.9 = (bf16[4,9,256,256]{3,2,1,0:T(8,128)(2,1)}, bf16[4,9,256,256]{3,2,1,0:T(8,128)(2,1)}, u32[]{:S(2)}, u32[]{:S(2)}) collective-permute-start(bf16[4,9,256,256]{3,2,1,0:T(8,128)(2,1)} %bitcast.33), channel_id=1, source_target_pairs={{0,1},{1,0},{2,3},{3,2},{4,5},{5,4},{6,7},{7,6},{8,9},{9,8},{10,11... | collective-permute-start | bytes 14155784 | tf_op jit(solution)/shard_map/ppermute | solution.py:284
  145.7 37.3 %all-to-all-start.2 = ((bf16[4,48,4096]{2,1,0:T(8,128)(2,1)}), bf16[4,48,4096]{2,1,0:T(8,128)(2,1)}, u32[]{:S(2)}, u32[]{:S(2)}) async-start(bf16[4,48,4096]{2,1,0:T(8,128)(2,1)} %bitcast.45), calls=%async_computation.2 | async-start | bytes 3145728 | tf_op jit(solution)/shard_map/all_to_all | solution.py:250
  222.3 34.6 %all-to-all-start.4 = ((bf16[4,96,2048]{2,1,0:T(8,128)(2,1)}), bf16[4,96,2048]{2,1,0:T(8,128)(2,1)S(1)}, u32[]{:S(2)}, u32[]{:S(2)}) async-start(bf16[4,96,2048]{2,1,0:T(8,128)(2,1)} %bitcast.19), calls=%async_computation.4 | async-start | bytes 3145728 | tf_op jit(solution)/shard_map/all_to_all | solution.py:250
  231.4 24.7 %collective-permute-start.10 = (bf16[64,4096]{1,0:T(8,128)(2,1)}, bf16[64,4096]{1,0:T(8,128)(2,1)S(1)}, u32[]{:S(2)}, u32[]{:S(2)}) collective-permute-start(bf16[64,4096]{1,0:T(8,128)(2,1)} %get-tuple-element.77), channel_id=1, source_target_pairs={{0,192},{64,0},{128,64},{192,128},{1,193},{65,1},{129,65},{193,129... | collective-permute-start | bytes 1572872 | tf_op jit(solution)/shard_map/ppermute | solution.py:295
  233.6 23.3 %collective-permute-start.11 = (bf16[64,4096]{1,0:T(8,128)(2,1)}, bf16[64,4096]{1,0:T(8,128)(2,1)}, u32[]{:S(2)}, u32[]{:S(2)}) collective-permute-start(bf16[64,4096]{1,0:T(8,128)(2,1)} %get-tuple-element.78), channel_id=1, source_target_pairs={{0,64},{64,128},{128,192},{192,0},{1,65},{65,129},{129,193},{193,1... | collective-permute-start | bytes 1572872 | tf_op jit(solution)/shard_map/ppermute | solution.py:295
  258.1 23.7 %all-to-all-start.5 = ((bf16[4,96,2048]{2,1,0:T(8,128)(2,1)}), bf16[4,96,2048]{2,1,0:T(8,128)(2,1)S(1)}, u32[]{:S(2)}, u32[]{:S(2)}) async-start(bf16[4,96,2048]{2,1,0:T(8,128)(2,1)} %bitcast.50), calls=%async_computation.5 | async-start | bytes 3145728 | tf_op jit(solution)/shard_map/all_to_all | solution.py:250
  265.8 25.6 %collective-permute-start.12 = (bf16[128,2048]{1,0:T(8,128)(2,1)}, bf16[128,2048]{1,0:T(8,128)(2,1)S(1)}, u32[]{:S(2)}, u32[]{:S(2)}) collective-permute-start(bf16[128,2048]{1,0:T(8,128)(2,1)} %get-tuple-element.79), channel_id=1, source_target_pairs={{0,192},{64,0},{128,64},{192,128},{1,193},{65,1},{129,65},{193,129... | collective-permute-start | bytes 1572872 | tf_op jit(solution)/shard_map/ppermute | solution.py:309
  269.2 26.3 %collective-permute-start.13 = (bf16[128,2048]{1,0:T(8,128)(2,1)}, bf16[128,2048]{1,0:T(8,128)(2,1)S(1)}, u32[]{:S(2)}, u32[]{:S(2)}) collective-permute-start(bf16[128,2048]{1,0:T(8,128)(2,1)} %get-tuple-element.80), channel_id=1, source_target_pairs={{0,64},{64,128},{128,192},{192,0},{1,65},{65,129},{129,193},{193,1... | collective-permute-start | bytes 1572872 | tf_op jit(solution)/shard_map/ppermute | solution.py:309
  291.4 4.2 %copy-start.7 = (bf16[128,2048]{1,0:T(8,128)(2,1)}, bf16[128,2048]{1,0:T(8,128)(2,1)S(1)}, u32[]{:S(2)}) copy-start(bf16[128,2048]{1,0:T(8,128)(2,1)S(1)} %collective-permute-done.12.refs_0_) | copy-start | bytes 1572868
  295.6 6.0 %copy-start.19 = (bf16[128,2048]{1,0:T(8,128)(2,1)S(1)}, bf16[128,2048]{1,0:T(8,128)(2,1)}, u32[]{:S(2)}) copy-start(bf16[128,2048]{1,0:T(8,128)(2,1)} %get-tuple-element.90) | copy-start | bytes 1572868
  296.4 27.5 %all-to-all-start.6 = ((bf16[4,48,4096]{2,1,0:T(8,128)(2,1)}), bf16[4,48,4096]{2,1,0:T(8,128)(2,1)S(1)}, u32[]{:S(2)}, u32[]{:S(2)}) async-start(bf16[4,48,4096]{2,1,0:T(8,128)(2,1)} %bitcast.23), calls=%async_computation.6 | async-start | bytes 3145728 | tf_op jit(solution)/shard_map/all_to_all | solution.py:250
  301.2 21.4 %collective-permute-start.14 = (bf16[128,2048]{1,0:T(8,128)(2,1)}, bf16[128,2048]{1,0:T(8,128)(2,1)S(1)}, u32[]{:S(2)}, u32[]{:S(2)}) collective-permute-start(bf16[128,2048]{1,0:T(8,128)(2,1)} %get-tuple-element.89), channel_id=1, source_target_pairs={{0,192},{64,0},{128,64},{192,128},{1,193},{65,1},{129,65},{193,129... | collective-permute-start | bytes 1572872 | tf_op jit(solution)/shard_map/ppermute | solution.py:309
  301.6 22.3 %collective-permute-start.15 = (bf16[128,2048]{1,0:T(8,128)(2,1)S(1)}, bf16[128,2048]{1,0:T(8,128)(2,1)S(1)}, u32[]{:S(2)}, u32[]{:S(2)}) collective-permute-start(bf16[128,2048]{1,0:T(8,128)(2,1)S(1)} %copy-done.19), channel_id=1, source_target_pairs={{0,64},{64,128},{128,192},{192,0},{1,65},{65,129},{129,193},{193,1... | collective-permute-start | bytes 1572872 | tf_op jit(solution)/shard_map/ppermute | solution.py:309
  (12 other events, 20.1 us)
Sparse Core Ops, SparseCore 0:
  9.4 57.4 all-gather.4
  87.9 52.2 all-gather.6

commit v4 on v3

--- a/solution.py
+++ b/solution.py
@@ -11,7 +11,7 @@
 ZH, YS, XS = 4, 4, 4
 PARAMS = pltpu.CompilerParams(vmem_limit_bytes=56 << 20)
 BLOCK = 256
-TILE = 1024
+TILE = 2048
 
 
 def ring(step):
@@ -230,20 +230,23 @@
         out_ref[...] = (total + right[0][...].astype(F32) + right[1][...].astype(F32)).astype(BF)
 
 
-def combine(kernel, plans, rows, more, counts):
+def combine(kernel, plans, rows, first, steps, more, counts):
     _, high, low = plans
-    width = rows.shape[-1]
     table = pl.BlockSpec(high.shape, lambda j: (0, 0, 0))
     return pl.pallas_call(
         kernel,
-        grid=(width // TILE,),
-        out_shape=[jax.ShapeDtypeStruct((n, width), BF) for n in counts],
-        in_specs=[table, table, pl.BlockSpec(rows.shape[:-1] + (TILE,), lambda j: (0, 0, 0, j))]
-        + [pl.BlockSpec((a.shape[0], TILE), lambda j, at=at: (0, at(j))) for a, at in more],
+        grid=(steps,),
+        out_shape=[jax.ShapeDtypeStruct((n, steps * TILE), BF) for n in counts],
+        in_specs=[
+            table,
+            table,
+            pl.BlockSpec(rows.shape[:-1] + (TILE,), lambda j: (0, 0, 0, first + j)),
+        ]
+        + [pl.BlockSpec(a.shape, lambda j: (0, 0)) for a in more],
         out_specs=[pl.BlockSpec((n, TILE), lambda j: (0, j)) for n in counts],
         compiler_params=PARAMS,
         name="combine",
-    )(high, low, rows, *[a for a, _ in more])
+    )(high, low, rows, *more)
 
 
 def over_y(rows, shape):
@@ -273,45 +276,42 @@
     other = lax.all_gather(swapped, "x")
 
     sides = plan(group, slots, *near_metas)
-    top, bottom, sent = barrier((near[0][:half], near[1][half:], gather(sides[0], *near)))
-    arrived_sides = over_y(sent, (-1, model))
-    far = [lax.ppermute(top, "zh", ring(1)), lax.ppermute(bottom, "zh", ring(3))]
+    arrived_sides = over_y(gather(sides[0], *near), (-1, model))
+    far = [lax.ppermute(near[0][:half], "zh", ring(1)), lax.ppermute(near[1][half:], "zh", ring(3))]
     far_meta = lax.ppermute(near_metas[0], "zh", ring(1))
-    far, far_meta, mine, arrived_sides = barrier((far, far_meta, mine, arrived_sides))
+    across = plan(group, slots, far_meta)
+    sent, mine, arrived_sides = barrier((gather(across[0], *far), mine, arrived_sides))
     mine_swapped = lax.ppermute(mine, "core", swap)
-    across = plan(group, slots, far_meta)
-    arrived_across = over_y(gather(across[0], *far), (-1, model))
+    arrived_across = over_y(sent, (-1, model))
     packs = [mine, mine_swapped, other, lax.ppermute(other, "core", swap)]
     zl, core = lax.axis_index("zl"), lax.axis_index("core")
     place = jnp.stack([zl * 2 + core, zl * 2 + 1 - core, (1 - zl) * 2 + core, (1 - zl) * 2 + 1 - core])
 
     made_sides = expert(place, arrived_sides, packs, 2)
+    made_sides, arrived_across = barrier((made_sides, arrived_across))
+    (made,) = expert(place, arrived_across, packs, 1)
+
+    back = over_y(made, (YS, 1, slots, model))
+    pieces = range(model // TILE)
+    parts = [combine(split_kernel, across, back, p, 1, [], (half, half)) for p in pieces]
+    passed = [
+        [lax.ppermute(top, "zh", ring(3)), lax.ppermute(bottom, "zh", ring(1))] for top, bottom in parts
+    ]
+    arrived_own, parts = barrier((arrived_own, parts))
     (made_own,) = expert(place, arrived_own, packs, 1)
-    made_sides, made_own, arrived_across = barrier((made_sides, made_own, arrived_across))
-    (made,) = expert(place, arrived_across, packs, 1)
-
-    back = over_y(made, (YS, 1, slots, model))
-    parts = combine(split_kernel, across, back, [], (half, half))
-    passed = [lax.ppermute(parts[0], "zh", ring(3)), lax.ppermute(parts[1], "zh", ring(1))]
-    home = []
-    for piece in range(2):
-        if piece == 0:
-            rows, back = barrier((made_sides[0], back))
-        else:
-            rows, passed = barrier((made_sides[1], passed))
-        back = over_y(rows, (YS, 2, slots, model // 2))
-        shift = lambda j, at=piece * (model // 2 // TILE): j + at
-        below, above = combine(
-            add_kernel, sides, back, [(p, shift) for p in passed], (tok_rows, tok_rows)
-        )
-        if piece == 1:
-            made_own, home, below = barrier((made_own, home, below))
+    home, rows = [], made_sides[0]
+    for p in pieces:
+        rows, back = barrier((rows, back))
+        back = over_y(rows, (YS, 2, slots, TILE))
+        if p == 0:
+            rows, passed[0], made_own = barrier((made_sides[1], passed[0], made_own))
+            back, passed[1] = barrier((back, passed[1]))
+        below, above = combine(add_kernel, sides, back, 0, 1, passed[p], (tok_rows, tok_rows))
+        if p == 1:
+            made_own, home, below, above = barrier((made_own, home, below, above))
         home = home + [lax.ppermute(below, "zh", ring(3)), lax.ppermute(above, "zh", ring(1))]
     back = over_y(made_own, (YS, 1, slots, model))
-    steps = model // 2 // TILE
-    left, right = lambda j: jnp.minimum(j, steps - 1), lambda j: jnp.maximum(j - steps, 0)
-    more = [(home[0], left), (home[1], left), (home[2], right), (home[3], right)]
-    return combine(last_kernel, own, back, more, (tok_rows,))[0]
+    return combine(last_kernel, own, back, 0, len(pieces), home, (tok_rows,))[0]
 
 
 def solution(mesh):

time: 340 us -> 317 us (0.932)
  waiting for transfers between devices: 154 us -> 127 us
  starting transfers between devices: 54.4 us -> 62.6 us
  Pallas kernels: 79.2 us -> 75.7 us
    ppermute x4 -> x6, waiting for transfers between devices: 21.8 us -> 1.2 us  [the longest x2 1.19 us: on_device(): lax.ppermute(top, 'zh', ring(3))]
    all_to_all x6, waiting for transfers between devices: 22.5 us -> 12.9 us  [over_y(): lax.all_to_all(rows.reshape(YS, -1, rows.shape[-1]), 'y', split_axis=0, c...]
    ppermute x2, starting transfers between devices: 3.86 us -> 12.2 us  [on_device(): lax.ppermute(below, 'zh', ring(3))]
    ppermute x2, waiting for transfers between devices: 23.8 us -> 18.2 us  [on_device(): lax.ppermute(below, 'zh', ring(3))]
    pallas_call x3, Pallas kernels: 12.6 us -> 8.98 us  [gather(): pl.pallas_call(functools.partial(gather_kernel, len(blocks) // sources),...]
    ppermute x1, waiting for transfers between devices: 20.3 us -> 23.9 us  [on_device(): far_meta = lax.ppermute(near_metas[0], 'zh', ring(1))]
    all_gather x1, waiting for transfers between devices: 2.94 us -> 6.48 us  [on_device(): other = lax.all_gather(swapped, 'x')]
    ppermute x4 -> x6, starting transfers between devices: 7.06 us -> 10.4 us  [the longest x2 7.39 us: on_device(): lax.ppermute(top, 'zh', ring(3))]
  transfers between devices with their start and end apart: 24 -> 26, of which waited for: 11 -> 10; matrix products, arithmetic and copies ran while one was open for 1% -> 1% of each run, Pallas kernels for 17% -> 18%
where the time goes in v4:
time: 317 us; the launch traced here: 315 us
  waiting for transfers between devices  127 us (40%)
  Pallas kernels  75.7 us (24%)
  starting transfers between devices  62.6 us (20%)
  blocking collectives  25.7 us (8%)
  between operations  13.6 us (4%)
  local copies, waits for them, and re-layouts  9.15 us (3%)
    ppermute x2, waiting for transfers between devices, on_device(): near_metas = [lax.ppermute(meta, 'zh', ring(k)) for k in (1, 3)]  58.3 us
    pallas_call x3, Pallas kernels, expert(): pl.pallas_call(expert_kernel, grid_spec=pltpu.PrefetchScalarGridSpec(num_...  44.4 us
    all_to_all x6, starting transfers between devices, over_y(): lax.all_to_all(rows.reshape(YS, -1, rows.shape[-1]), 'y', split_axis=0, c...  29.6 us
    all_to_all x1, blocking collectives, over_y(): lax.all_to_all(rows.reshape(YS, -1, rows.shape[-1]), 'y', split_axis=0, c...  25.7 us
    ppermute x1, waiting for transfers between devices, on_device(): far_meta = lax.ppermute(near_metas[0], 'zh', ring(1))  23.9 us
    ppermute x2, waiting for transfers between devices, on_device(): lax.ppermute(below, 'zh', ring(3))  18.2 us
    pallas_call x5, Pallas kernels, combine(): pl.pallas_call(kernel, grid=(steps,), out_shape=[jax.ShapeDtypeStruct((n,...  15 us
    all_to_all x6, waiting for transfers between devices, over_y(): lax.all_to_all(rows.reshape(YS, -1, rows.shape[-1]), 'y', split_axis=0, c...  12.9 us
  transfers between devices with their start and end apart: 26, of which 10 were waited for; matrix products, arithmetic and copies ran while one was open for 1% of the time, Pallas kernels for 18%

profile of v4, /device:TPU:10, one launch (start us, length us, event | category | flops | bytes accessed | tf_op | source)
XLA Modules:
  0.0 315.1 jit_solution(2418940777952963634)
XLA Ops:
  6.5 2.7 pack.1
  13.4 2.7 gather.3
  16.0 5.0 %all-to-all-start = ((bf16[4,48,4096]{2,1,0:T(8,128)(2,1)}), bf16[4,48,4096]{2,1,0:T(8,128)(2,1)S(1)}, u32[]{:S(2)}, u32[]{:S(2)}) async-start(bf16[4,48,4096]{2,1,0:T(8,128)(2,1)} %bitcast.49), calls=%async_computation | async-start | bytes 3145728 | tf_op jit(solution)/shard_map/all_to_all | solution.py:253
  21.1 3.3 %collective-permute-start = (bf16[128,4096]{1,0:T(8,128)(2,1)}, bf16[128,4096]{1,0:T(8,128)(2,1)S(1)}, u32[]{:S(2)}, u32[]{:S(2)}) collective-permute-start(bf16[128,4096]{1,0:T(8,128)(2,1)} %refs_0_.1), channel_id=1, source_target_pairs={{0,64},{64,128},{128,192},{192,0},{1,65},{65,129},{129,193},{193,1... | collective-permute-start | bytes 3145736 | tf_op jit(solution)/shard_map/ppermute | solution.py:269
  26.5 2.9 collective-permute-start.3
  29.4 21.0 %collective-permute-done.3.refs_1_ = f32[8,128]{1,0:T(8,128)S(1)} collective-permute-done((f32[8,128]{1,0:T(8,128)S(1)}, f32[8,128]{1,0:T(8,128)S(1)}, u32[]{:S(2)}, u32[]{:S(2)}) %collective-permute-start.3) | collective-permute-done | bytes 4128 | tf_op jit(solution)/shard_map/ppermute | solution.py:270
  50.5 37.2 %collective-permute-done.2.refs_0_ = f32[8,128]{1,0:T(8,128)S(1)} collective-permute-done((f32[8,128]{1,0:T(8,128)S(1)}, f32[8,128]{1,0:T(8,128)S(1)}, u32[]{:S(2)}, u32[]{:S(2)}) %collective-permute-start.2) | collective-permute-done | bytes 4128 | tf_op jit(solution)/shard_map/ppermute | solution.py:270
  89.9 3.7 %gather.5 = bf16[4,2,48,4096]{3,2,1,0:T(8,128)(2,1)} custom-call(bf16[2,192,128]{2,1,0:T(8,128)(2,1)} %get-tuple-element.59.pick_ref, bf16[128,4096]{1,0:T(8,128)(2,1)} %copy-done.5, bf16[128,4096]{1,0:T(8,128)(2,1)} %collective-permute-done.1.refs_1_), custom_call_target="tpu_custom_call" | custom-call | tf_op jit(solution)/shard_map/gather/pallas_call | solution.py:106
  93.6 4.9 %all-to-all-start.1 = ((bf16[4,96,4096]{2,1,0:T(8,128)(2,1)}), bf16[4,96,4096]{2,1,0:T(8,128)(2,1)S(1)}, u32[]{:S(2)}, u32[]{:S(2)}) async-start(bf16[4,96,4096]{2,1,0:T(8,128)(2,1)} %bitcast.42), calls=%async_computation.1 | async-start | bytes 6291456 | tf_op jit(solution)/shard_map/all_to_all | solution.py:253
  103.8 23.9 %collective-permute-done.5.refs_0_ = f32[8,128]{1,0:T(8,128)S(1)} collective-permute-done((f32[8,128]{1,0:T(8,128)S(1)}, f32[8,128]{1,0:T(8,128)S(1)}, u32[]{:S(2)}, u32[]{:S(2)}) %collective-permute-start.5) | collective-permute-done | bytes 4128 | tf_op jit(solution)/shard_map/ppermute | solution.py:281
  130.8 2.7 gather.4
  133.7 6.5 %all-gather.7.cloned.1.call-done = bf16[36,256,256]{2,1,0:T(8,128)(2,1)} async-done(((bf16[9,256,256]{2,1,0:T(8,128)(2,1)}), bf16[36,256,256]{2,1,0:T(8,128)(2,1)}) %all-gather.7.cloned.1.call-update) | async-done | bytes 4718608 | tf_op jit(solution)/shard_map/all_gather | solution.py:276
  140.2 4.9 %all-to-all-start.2 = ((bf16[4,48,4096]{2,1,0:T(8,128)(2,1)}), bf16[4,48,4096]{2,1,0:T(8,128)(2,1)}, u32[]{:S(2)}, u32[]{:S(2)}) async-start(bf16[4,48,4096]{2,1,0:T(8,128)(2,1)} %bitcast.48), calls=%async_computation.2 | async-start | bytes 3145728 | tf_op jit(solution)/shard_map/all_to_all | solution.py:253
  145.7 3.0 collective-permute-done.9.refs_3_.refs_7_
  148.7 17.1 %expert.3 = (bf16[384,2048]{1,0:T(8,128)(2,1)}, bf16[384,2048]{1,0:T(8,128)(2,1)}) custom-call(s32[4]{0:T(128)} %pad_add_fusion.place_ref, bf16[384,4096]{1,0:T(8,128)(2,1)} %bitcast.43, bf16[4,9,256,256]{3,2,1,0:T(8,128)(2,1)} %bitcast.27, bf16[4,9,256,256]{3,2,1,0:T(8,128)(2,1)} %collective-permute-done.8.refs_1_.refs_5_, ...), custom_call_target="tpu_custom_call" | custom-call | tf_op jit(solution)/shard_map/expert/pallas_call | solution.py:163
  165.8 13.7 %expert.4 = bf16[192,4096]{1,0:T(8,128)(2,1)} custom-call(s32[4]{0:T(128)} %pad_add_fusion.place_ref, bf16[192,4096]{1,0:T(8,128)(2,1)} %bitcast.16.x_ref, bf16[4,9,256,256]{3,2,1,0:T(8,128)(2,1)} %bitcast.29, bf16[4,9,256,256]{3,2,1,0:T(8,128)(2,1)} %collective-permute-done.8.refs_1_.refs_5_, bf16[4,9,256,256]{3,2,1,0:T(8,128)(2,1)} %bitcast.36, ...), custom_call_target="tpu_custom_call" | custom-call | tf_op jit(solution)/shard_map/expert/pallas_call | solution.py:163
  179.5 25.7 %all_to_all.35 = bf16[4,48,4096]{2,1,0:T(8,128)(2,1)} all-to-all(bf16[4,48,4096]{2,1,0:T(8,128)(2,1)} %bitcast.45), channel_id=1, replica_groups=mesh['zh'=4,'y'=4,'x'=4,'zl'=2,'core'=2] {'y'}, dimensions={0} | all-to-all | bytes 3145728 | tf_op jit(solution)/shard_map/all_to_all | solution.py:253
  205.2 5.0 %all-to-all-start.4 = ((bf16[4,96,2048]{2,1,0:T(8,128)(2,1)}), bf16[4,96,2048]{2,1,0:T(8,128)(2,1)S(1)}, u32[]{:S(2)}, u32[]{:S(2)}) async-start(bf16[4,96,2048]{2,1,0:T(8,128)(2,1)} %bitcast.19), calls=%async_computation.4 | async-start | bytes 3145728 | tf_op jit(solution)/shard_map/all_to_all | solution.py:253
  212.6 3.3 %collective-permute-start.10 = (bf16[64,2048]{1,0:T(8,128)(2,1)}, bf16[64,2048]{1,0:T(8,128)(2,1)S(1)}, u32[]{:S(2)}, u32[]{:S(2)}) collective-permute-start(bf16[64,2048]{1,0:T(8,128)(2,1)} %get-tuple-element.70), channel_id=1, source_target_pairs={{0,192},{64,0},{128,64},{192,128},{1,193},{65,1},{129,65},{193,129... | collective-permute-start | bytes 786440 | tf_op jit(solution)/shard_map/ppermute | solution.py:298
  215.8 2.5 combine.6
  218.3 4.1 %collective-permute-start.12 = (bf16[64,2048]{1,0:T(8,128)(2,1)}, bf16[64,2048]{1,0:T(8,128)(2,1)S(1)}, u32[]{:S(2)}, u32[]{:S(2)}) collective-permute-start(bf16[64,2048]{1,0:T(8,128)(2,1)} %get-tuple-element.73), channel_id=1, source_target_pairs={{0,192},{64,0},{128,64},{192,128},{1,193},{65,1},{129,65},{193,129... | collective-permute-start | bytes 786440 | tf_op jit(solution)/shard_map/ppermute | solution.py:298
  222.4 13.7 %expert.5 = bf16[192,4096]{1,0:T(8,128)(2,1)} custom-call(s32[4]{0:T(128)} %pad_add_fusion.place_ref, bf16[192,4096]{1,0:T(8,128)(2,1)} %bitcast.44, bf16[4,9,256,256]{3,2,1,0:T(8,128)(2,1)} %bitcast.31, bf16[4,9,256,256]{3,2,1,0:T(8,128)(2,1)} %collective-permute-done.8.refs_1_.refs_5_, bf16[4,9,256,256]{3,2,1,0:T(8,128)(2,1)} %bitcast.38, ...), custom_call_target="tpu_custom_call" | custom-call | tf_op jit(solution)/shard_map/expert/pallas_call | solution.py:163
  238.6 4.8 %all-to-all-start.5 = ((bf16[4,96,2048]{2,1,0:T(8,128)(2,1)}), bf16[4,96,2048]{2,1,0:T(8,128)(2,1)S(1)}, u32[]{:S(2)}, u32[]{:S(2)}) async-start(bf16[4,96,2048]{2,1,0:T(8,128)(2,1)} %bitcast.51), calls=%async_computation.5 | async-start | bytes 3145728 | tf_op jit(solution)/shard_map/all_to_all | solution.py:253
  243.4 3.1 combine.7
  246.6 3.5 %collective-permute-start.14 = (bf16[128,2048]{1,0:T(8,128)(2,1)}, bf16[128,2048]{1,0:T(8,128)(2,1)S(1)}, u32[]{:S(2)}, u32[]{:S(2)}) collective-permute-start(bf16[128,2048]{1,0:T(8,128)(2,1)} %get-tuple-element.84), channel_id=1, source_target_pairs={{0,192},{64,0},{128,64},{192,128},{1,193},{65,1},{129,65},{193,129... | collective-permute-start | bytes 1572872 | tf_op jit(solution)/shard_map/ppermute | solution.py:312
  250.1 12.6 %all-to-all-done.5 = bf16[4,96,2048]{2,1,0:T(8,128)(2,1)S(1)} async-done(((bf16[4,96,2048]{2,1,0:T(8,128)(2,1)}), bf16[4,96,2048]{2,1,0:T(8,128)(2,1)S(1)}, u32[]{:S(2)}, u32[]{:S(2)}) %all-to-all-start.5) | async-done | bytes 1572896 | tf_op jit(solution)/shard_map/all_to_all | solution.py:253
  263.9 3.1 combine.8
  268.0 5.0 %all-to-all-start.6 = ((bf16[4,48,4096]{2,1,0:T(8,128)(2,1)}), bf16[4,48,4096]{2,1,0:T(8,128)(2,1)S(1)}, u32[]{:S(2)}, u32[]{:S(2)}) async-start(bf16[4,48,4096]{2,1,0:T(8,128)(2,1)} %bitcast.23), calls=%async_computation.6 | async-start | bytes 3145728 | tf_op jit(solution)/shard_map/all_to_all | solution.py:253
  273.0 8.7 %collective-permute-start.16 = (bf16[128,2048]{1,0:T(8,128)(2,1)}, bf16[128,2048]{1,0:T(8,128)(2,1)S(1)}, u32[]{:S(2)}, u32[]{:S(2)}) collective-permute-start(bf16[128,2048]{1,0:T(8,128)(2,1)} %get-tuple-element.95), channel_id=1, source_target_pairs={{0,192},{64,0},{128,64},{192,128},{1,193},{65,1},{129,65},{193,129... | collective-permute-start | bytes 1572872 | tf_op jit(solution)/shard_map/ppermute | solution.py:312
  281.7 18.2 %collective-permute-done.16.refs_2_ = bf16[128,2048]{1,0:T(8,128)(2,1)S(1)} collective-permute-done((bf16[128,2048]{1,0:T(8,128)(2,1)}, bf16[128,2048]{1,0:T(8,128)(2,1)S(1)}, u32[]{:S(2)}, u32[]{:S(2)}) %collective-permute-start.16) | collective-permute-done | bytes 524320 | tf_op jit(solution)/shard_map/ppermute | solution.py:312
  299.9 3.1 collective-permute-done.17.refs_3_
  304.4 3.8 %combine.9 = bf16[128,4096]{1,0:T(8,128)(2,1)} custom-call(bf16[1,192,128]{2,1,0:T(8,128)(2,1)} %get-tuple-element.51.high_ref, bf16[1,192,128]{2,1,0:T(8,128)(2,1)} %get-tuple-element.52.low_ref, bf16[4,1,48,4096]{3,2,1,0:T(8,128)(2,1)} %bitcast.50, bf16[128,2048]{1,0:T(8,128)(2,1)} %copy-done.6, bf16[128,2048]{1,0:T(8,128)(2,1)} %copy-done.7, ...), custom_call_target="tpu_custom_call" | custom-call | tf_op jit(solution)/shard_map/combine/pallas_call | solution.py:236
  (91 shorter events, 26.2 us)
Async XLA Ops:
  6.5 127.2 %all-gather.5.cloned.1.call-start = ((), (), s32[]{:S(2)}) async-start(), calls=%async_computation.7 | async-start | bytes 5898240 | tf_op jit(solution)/shard_map/all_gather | solution.py:272
  9.3 78.4 %collective-permute-start.4 = (bf16[9,256,256]{2,1,0:T(8,128)(2,1)}, bf16[9,256,256]{2,1,0:T(8,128)(2,1)}, u32[]{:S(2)}, u32[]{:S(2)}) collective-permute-start(bf16[9,256,256]{2,1,0:T(8,128)(2,1)} %pack.1), channel_id=1, source_target_pairs={{0,2},{2,0},{1,3},{3,1},{4,6},{6,4},{5,7},{7,5},{8,10},{10,8},{9,1... | collective-permute-start | bytes 3538952 | tf_op jit(solution)/shard_map/ppermute | solution.py:271
  16.0 10.5 %copy-start.16 = (f32[8,128]{1,0:T(8,128)S(1)}, f32[8,128]{1,0:T(8,128)}, u32[]{:S(2)}) copy-start(f32[8,128]{1,0:T(8,128)} %pad_maximum_fusion.refs_0_) | copy-start | bytes 12292
  16.0 71.7 %all-to-all-start = ((bf16[4,48,4096]{2,1,0:T(8,128)(2,1)}), bf16[4,48,4096]{2,1,0:T(8,128)(2,1)S(1)}, u32[]{:S(2)}, u32[]{:S(2)}) async-start(bf16[4,48,4096]{2,1,0:T(8,128)(2,1)} %bitcast.49), calls=%async_computation | async-start | bytes 3145728 | tf_op jit(solution)/shard_map/all_to_all | solution.py:253
  21.1 119.1 %all-gather.7.cloned.1.call-start = ((), (), s32[]{:S(2)}) async-start(), calls=%async_computation.8 | async-start | bytes 5898240 | tf_op jit(solution)/shard_map/all_gather | solution.py:276
  21.1 66.6 %collective-permute-start = (bf16[128,4096]{1,0:T(8,128)(2,1)}, bf16[128,4096]{1,0:T(8,128)(2,1)S(1)}, u32[]{:S(2)}, u32[]{:S(2)}) collective-permute-start(bf16[128,4096]{1,0:T(8,128)(2,1)} %refs_0_.1), channel_id=1, source_target_pairs={{0,64},{64,128},{128,192},{192,0},{1,65},{65,129},{129,193},{193,1... | collective-permute-start | bytes 3145736 | tf_op jit(solution)/shard_map/ppermute | solution.py:269
  24.4 63.4 %collective-permute-start.1 = (bf16[128,4096]{1,0:T(8,128)(2,1)}, bf16[128,4096]{1,0:T(8,128)(2,1)}, u32[]{:S(2)}, u32[]{:S(2)}) collective-permute-start(bf16[128,4096]{1,0:T(8,128)(2,1)} %refs_0_.1), channel_id=1, source_target_pairs={{0,192},{64,0},{128,64},{192,128},{1,193},{65,1},{129,65},{193,129... | collective-permute-start | bytes 3145736 | tf_op jit(solution)/shard_map/ppermute | solution.py:269
  26.5 24.0 %collective-permute-start.3 = (f32[8,128]{1,0:T(8,128)S(1)}, f32[8,128]{1,0:T(8,128)S(1)}, u32[]{:S(2)}, u32[]{:S(2)}) collective-permute-start(f32[8,128]{1,0:T(8,128)S(1)} %copy-done.16), channel_id=1, source_target_pairs={{0,192},{64,0},{128,64},{192,128},{1,193},{65,1},{129,65},{193,129... | collective-permute-start | bytes 12296 | tf_op jit(solution)/shard_map/ppermute | solution.py:270
  29.4 58.3 %collective-permute-start.2 = (f32[8,128]{1,0:T(8,128)S(1)}, f32[8,128]{1,0:T(8,128)S(1)}, u32[]{:S(2)}, u32[]{:S(2)}) collective-permute-start(f32[8,128]{1,0:T(8,128)S(1)} %copy-done.16), channel_id=1, source_target_pairs={{0,64},{64,128},{128,192},{192,0},{1,65},{65,129},{129,193},{193,1... | collective-permute-start | bytes 12296 | tf_op jit(solution)/shard_map/ppermute | solution.py:270
  50.5 37.3 %copy-start.20 = (f32[8,128]{1,0:T(8,128)}, f32[8,128]{1,0:T(8,128)S(1)}, u32[]{:S(2)}) copy-start(f32[8,128]{1,0:T(8,128)S(1)} %collective-permute-done.3.refs_1_) | copy-start | bytes 12292
  87.7 5.8 %copy-start.1 = (bf16[4,48,4096]{2,1,0:T(8,128)(2,1)}, bf16[4,48,4096]{2,1,0:T(8,128)(2,1)S(1)}, u32[]{:S(2)}) copy-start(bf16[4,48,4096]{2,1,0:T(8,128)(2,1)S(1)} %all-to-all-done) | copy-start | bytes 4718596
  93.6 40.1 %all-to-all-start.1 = ((bf16[4,96,4096]{2,1,0:T(8,128)(2,1)}), bf16[4,96,4096]{2,1,0:T(8,128)(2,1)S(1)}, u32[]{:S(2)}, u32[]{:S(2)}) async-start(bf16[4,96,4096]{2,1,0:T(8,128)(2,1)} %bitcast.42), calls=%async_computation.1 | async-start | bytes 6291456 | tf_op jit(solution)/shard_map/all_to_all | solution.py:253
  98.5 5.3 %copy-start.19 = (f32[8,128]{1,0:T(8,128)S(1)}, f32[8,128]{1,0:T(8,128)}, u32[]{:S(2)}) copy-start(f32[8,128]{1,0:T(8,128)} %copy-done.18) | copy-start | bytes 12292
  100.7 29.0 %collective-permute-start.7 = (bf16[64,4096]{1,0:T(8,128)(2,1)S(1)}, bf16[64,4096]{1,0:T(8,128)(2,1)S(1)}, u32[]{:S(2)}, u32[]{:S(2)}) collective-permute-start(bf16[64,4096]{1,0:T(8,128)(2,1)S(1)} %slice.7), channel_id=1, source_target_pairs={{0,192},{64,0},{128,64},{192,128},{1,193},{65,1},{129,65},{193,129... | collective-permute-start | bytes 1572872 | tf_op jit(solution)/shard_map/ppermute | solution.py:280
  102.3 27.5 %collective-permute-start.6 = (bf16[64,4096]{1,0:T(8,128)(2,1)S(1)}, bf16[64,4096]{1,0:T(8,128)(2,1)S(1)}, u32[]{:S(2)}, u32[]{:S(2)}) collective-permute-start(bf16[64,4096]{1,0:T(8,128)(2,1)S(1)} %slice.6), channel_id=1, source_target_pairs={{0,64},{64,128},{128,192},{192,0},{1,65},{65,129},{129,193},{193,1... | collective-permute-start | bytes 1572872 | tf_op jit(solution)/shard_map/ppermute | solution.py:280
  103.7 23.9 %collective-permute-start.5 = (f32[8,128]{1,0:T(8,128)S(1)}, f32[8,128]{1,0:T(8,128)S(1)}, u32[]{:S(2)}, u32[]{:S(2)}) collective-permute-start(f32[8,128]{1,0:T(8,128)S(1)} %copy-done.19), channel_id=1, source_target_pairs={{0,64},{64,128},{128,192},{192,0},{1,65},{65,129},{129,193},{193,1... | collective-permute-start | bytes 12296 | tf_op jit(solution)/shard_map/ppermute | solution.py:281
  133.7 6.5 %copy-start = (bf16[4,96,4096]{2,1,0:T(8,128)(2,1)}, bf16[4,96,4096]{2,1,0:T(8,128)(2,1)S(1)}, u32[]{:S(2)}) copy-start(bf16[4,96,4096]{2,1,0:T(8,128)(2,1)S(1)} %all-to-all-done.1) | copy-start | bytes 9437188
  133.7 12.0 %collective-permute-start.8 = (bf16[4,9,256,256]{3,2,1,0:T(8,128)(2,1)}, bf16[4,9,256,256]{3,2,1,0:T(8,128)(2,1)}, u32[]{:S(2)}, u32[]{:S(2)}) collective-permute-start(bf16[4,9,256,256]{3,2,1,0:T(8,128)(2,1)} %bitcast.26), channel_id=1, source_target_pairs={{0,1},{1,0},{2,3},{3,2},{4,5},{5,4},{6,7},{7,6},{8,9},{9,8},{10,11... | collective-permute-start | bytes 14155784 | tf_op jit(solution)/shard_map/ppermute | solution.py:284
  140.2 8.5 %collective-permute-start.9 = (bf16[4,9,256,256]{3,2,1,0:T(8,128)(2,1)}, bf16[4,9,256,256]{3,2,1,0:T(8,128)(2,1)}, u32[]{:S(2)}, u32[]{:S(2)}) collective-permute-start(bf16[4,9,256,256]{3,2,1,0:T(8,128)(2,1)} %bitcast.33), channel_id=1, source_target_pairs={{0,1},{1,0},{2,3},{3,2},{4,5},{5,4},{6,7},{7,6},{8,9},{9,8},{10,11... | collective-permute-start | bytes 14155784 | tf_op jit(solution)/shard_map/ppermute | solution.py:286
  140.2 25.6 %all-to-all-start.2 = ((bf16[4,48,4096]{2,1,0:T(8,128)(2,1)}), bf16[4,48,4096]{2,1,0:T(8,128)(2,1)}, u32[]{:S(2)}, u32[]{:S(2)}) async-start(bf16[4,48,4096]{2,1,0:T(8,128)(2,1)} %bitcast.48), calls=%async_computation.2 | async-start | bytes 3145728 | tf_op jit(solution)/shard_map/all_to_all | solution.py:253
  205.2 32.2 %all-to-all-start.4 = ((bf16[4,96,2048]{2,1,0:T(8,128)(2,1)}), bf16[4,96,2048]{2,1,0:T(8,128)(2,1)S(1)}, u32[]{:S(2)}, u32[]{:S(2)}) async-start(bf16[4,96,2048]{2,1,0:T(8,128)(2,1)} %bitcast.19), calls=%async_computation.4 | async-start | bytes 3145728 | tf_op jit(solution)/shard_map/all_to_all | solution.py:253
  212.6 23.5 %collective-permute-start.10 = (bf16[64,2048]{1,0:T(8,128)(2,1)}, bf16[64,2048]{1,0:T(8,128)(2,1)S(1)}, u32[]{:S(2)}, u32[]{:S(2)}) collective-permute-start(bf16[64,2048]{1,0:T(8,128)(2,1)} %get-tuple-element.70), channel_id=1, source_target_pairs={{0,192},{64,0},{128,64},{192,128},{1,193},{65,1},{129,65},{193,129... | collective-permute-start | bytes 786440 | tf_op jit(solution)/shard_map/ppermute | solution.py:298
  215.8 20.3 %collective-permute-start.11 = (bf16[64,2048]{1,0:T(8,128)(2,1)}, bf16[64,2048]{1,0:T(8,128)(2,1)S(1)}, u32[]{:S(2)}, u32[]{:S(2)}) collective-permute-start(bf16[64,2048]{1,0:T(8,128)(2,1)} %get-tuple-element.71), channel_id=1, source_target_pairs={{0,64},{64,128},{128,192},{192,0},{1,65},{65,129},{129,193},{193,1... | collective-permute-start | bytes 786440 | tf_op jit(solution)/shard_map/ppermute | solution.py:298
  218.3 19.0 %collective-permute-start.12 = (bf16[64,2048]{1,0:T(8,128)(2,1)}, bf16[64,2048]{1,0:T(8,128)(2,1)S(1)}, u32[]{:S(2)}, u32[]{:S(2)}) collective-permute-start(bf16[64,2048]{1,0:T(8,128)(2,1)} %get-tuple-element.73), channel_id=1, source_target_pairs={{0,192},{64,0},{128,64},{192,128},{1,193},{65,1},{129,65},{193,129... | collective-permute-start | bytes 786440 | tf_op jit(solution)/shard_map/ppermute | solution.py:298
  222.4 14.9 %collective-permute-start.13 = (bf16[64,2048]{1,0:T(8,128)(2,1)}, bf16[64,2048]{1,0:T(8,128)(2,1)S(1)}, u32[]{:S(2)}, u32[]{:S(2)}) collective-permute-start(bf16[64,2048]{1,0:T(8,128)(2,1)} %get-tuple-element.74), channel_id=1, source_target_pairs={{0,64},{64,128},{128,192},{192,0},{1,65},{65,129},{129,193},{193,1... | collective-permute-start | bytes 786440 | tf_op jit(solution)/shard_map/ppermute | solution.py:298
  238.6 24.0 %all-to-all-start.5 = ((bf16[4,96,2048]{2,1,0:T(8,128)(2,1)}), bf16[4,96,2048]{2,1,0:T(8,128)(2,1)S(1)}, u32[]{:S(2)}, u32[]{:S(2)}) async-start(bf16[4,96,2048]{2,1,0:T(8,128)(2,1)} %bitcast.51), calls=%async_computation.5 | async-start | bytes 3145728 | tf_op jit(solution)/shard_map/all_to_all | solution.py:253
  246.6 20.4 %collective-permute-start.14 = (bf16[128,2048]{1,0:T(8,128)(2,1)}, bf16[128,2048]{1,0:T(8,128)(2,1)S(1)}, u32[]{:S(2)}, u32[]{:S(2)}) collective-permute-start(bf16[128,2048]{1,0:T(8,128)(2,1)} %get-tuple-element.84), channel_id=1, source_target_pairs={{0,192},{64,0},{128,64},{192,128},{1,193},{65,1},{129,65},{193,129... | collective-permute-start | bytes 1572872 | tf_op jit(solution)/shard_map/ppermute | solution.py:312
  250.1 16.9 %collective-permute-start.15 = (bf16[128,2048]{1,0:T(8,128)(2,1)}, bf16[128,2048]{1,0:T(8,128)(2,1)S(1)}, u32[]{:S(2)}, u32[]{:S(2)}) collective-permute-start(bf16[128,2048]{1,0:T(8,128)(2,1)} %get-tuple-element.85), channel_id=1, source_target_pairs={{0,64},{64,128},{128,192},{192,0},{1,65},{65,129},{129,193},{193,1... | collective-permute-start | bytes 1572872 | tf_op jit(solution)/shard_map/ppermute | solution.py:312
  267.0 14.7 %copy-start.23 = (bf16[128,2048]{1,0:T(8,128)(2,1)S(1)}, bf16[128,2048]{1,0:T(8,128)(2,1)}, u32[]{:S(2)}) copy-start(bf16[128,2048]{1,0:T(8,128)(2,1)} %get-tuple-element.96) | copy-start | bytes 1572868
  268.0 35.0 %all-to-all-start.6 = ((bf16[4,48,4096]{2,1,0:T(8,128)(2,1)}), bf16[4,48,4096]{2,1,0:T(8,128)(2,1)S(1)}, u32[]{:S(2)}, u32[]{:S(2)}) async-start(bf16[4,48,4096]{2,1,0:T(8,128)(2,1)} %bitcast.23), calls=%async_computation.6 | async-start | bytes 3145728 | tf_op jit(solution)/shard_map/all_to_all | solution.py:253
  273.0 26.9 %collective-permute-start.16 = (bf16[128,2048]{1,0:T(8,128)(2,1)}, bf16[128,2048]{1,0:T(8,128)(2,1)S(1)}, u32[]{:S(2)}, u32[]{:S(2)}) collective-permute-start(bf16[128,2048]{1,0:T(8,128)(2,1)} %get-tuple-element.95), channel_id=1, source_target_pairs={{0,192},{64,0},{128,64},{192,128},{1,193},{65,1},{129,65},{193,129... | collective-permute-start | bytes 1572872 | tf_op jit(solution)/shard_map/ppermute | solution.py:312
  281.7 21.4 %collective-permute-start.17 = (bf16[128,2048]{1,0:T(8,128)(2,1)S(1)}, bf16[128,2048]{1,0:T(8,128)(2,1)S(1)}, u32[]{:S(2)}, u32[]{:S(2)}) collective-permute-start(bf16[128,2048]{1,0:T(8,128)(2,1)S(1)} %copy-done.23), channel_id=1, source_target_pairs={{0,64},{64,128},{128,192},{192,0},{1,65},{65,129},{129,193},{193,1... | collective-permute-start | bytes 1572872 | tf_op jit(solution)/shard_map/ppermute | solution.py:312
  (18 other events, 28.3 us)
Sparse Core Ops, SparseCore 0:
  9.4 57.4 all-gather.4
  87.9 52.2 all-gather.6

commit v5 on v4

--- a/solution.py
+++ b/solution.py
@@ -89,39 +89,42 @@
     )(group, *metas)
 
 
-def gather_kernel(pieces, pick_ref, *refs):
+def gather_kernel(counts, pick_ref, *refs):
     blocks, out_ref = refs[:-1], refs[-1]
+    sources = pick_ref.shape[0]
     slots = out_ref.shape[2]
-    for i in range(pick_ref.shape[0]):
-        rows = jnp.concatenate([ref[...] for ref in blocks[i * pieces : (i + 1) * pieces]], axis=0)
-        got = jnp.dot(pick_ref[i], rows, preferred_element_type=F32).astype(BF)
-        for y in range(YS):
-            out_ref[y, i] = got[y * slots : (y + 1) * slots]
-
-
-def gather(pick, *blocks):
+    halves, per_source = counts
+    width = out_ref.shape[3] // halves
+    for h in range(halves):
+        for i in range(sources):
+            first = (h * sources + i) * per_source
+            rows = jnp.concatenate([ref[...] for ref in blocks[first : first + per_source]], axis=0)
+            got = jnp.dot(pick_ref[i], rows, preferred_element_type=F32).astype(BF)
+            for y in range(YS):
+                out_ref[y, i, :, h * width : (h + 1) * width] = got[y * slots : (y + 1) * slots]
+
+
+def gather(pick, blocks):
     sources, routes, _ = pick.shape
-    width = blocks[0].shape[1]
-    shape = (YS, sources, routes // YS)
-    return pl.pallas_call(
-        functools.partial(gather_kernel, len(blocks) // sources),
-        grid=(width // TILE,),
-        out_shape=jax.ShapeDtypeStruct(shape + (width,), BF),
-        in_specs=[pl.BlockSpec(pick.shape, lambda j: (0, 0, 0))]
-        + [pl.BlockSpec((b.shape[0], TILE), lambda j: (0, j)) for b in blocks],
-        out_specs=pl.BlockSpec(shape + (TILE,), lambda j: (0, 0, 0, j)),
+    counts = len(blocks), len(blocks[0][0])
+    flat = [piece for part in blocks for source in part for piece in source]
+    width = sum(part[0][0].shape[1] for part in blocks)
+    return pl.pallas_call(
+        functools.partial(gather_kernel, counts),
+        out_shape=jax.ShapeDtypeStruct((YS, sources, routes // YS, width), BF),
         compiler_params=PARAMS,
         name="gather",
-    )(pick, *blocks)
-
-
-def expert_kernel(place_ref, x_ref, *refs):
+    )(pick, *flat)
+
+
+def expert_kernel(given, place_ref, *refs):
+    rows, refs = refs[:given], refs[given:]
     ins, downs, outs = refs[0:4], refs[4:8], refs[8:-2]
     sums_ref, hidden_ref = refs[-2:]
     step = pl.program_id(0)
     parts = sums_ref.shape[0]
     half = parts // 2
-    each = XS // len(outs)
+    taken, each = XS // given, XS // len(outs)
 
     def columns(x, r):
         return pl.ds(pl.multiple_of((x * 4 + place_ref[r]) * BLOCK, BLOCK), BLOCK)
@@ -130,13 +133,15 @@
     def _():
         sums_ref[...] = jnp.zeros_like(sums_ref)
 
-    @pl.when(step < XS)
-    def _():
-        rows = [x_ref[:, columns(step, r)] for r in range(4)]
-        for n in range(parts):
-            sums_ref[n] += sum(
-                jnp.dot(rows[r], ins[r][n], preferred_element_type=F32) for r in range(4)
-            )
+    for piece in range(given):
+
+        @pl.when((step >= piece * taken) & (step < (piece + 1) * taken))
+        def _(piece=piece):
+            x = [rows[piece][:, columns(step - piece * taken, r)] for r in range(4)]
+            for n in range(parts):
+                sums_ref[n] += sum(
+                    jnp.dot(x[r], ins[r][n], preferred_element_type=F32) for r in range(4)
+                )
 
     @pl.when(step == XS)
     def _():
@@ -157,15 +162,16 @@
 
 
 def expert(place, rows, packs, pieces):
-    count, width = rows.shape
+    count = rows[0].shape[0]
+    width = sum(r.shape[1] for r in rows)
     half = packs[0].shape[1] // 3
     out = jax.ShapeDtypeStruct((count, width // pieces), BF)
     return pl.pallas_call(
-        expert_kernel,
+        functools.partial(expert_kernel, len(rows)),
         grid_spec=pltpu.PrefetchScalarGridSpec(
             num_scalar_prefetch=1,
             grid=(2 * XS,),
-            in_specs=[pl.BlockSpec((count, width), lambda s, p: (0, 0))]
+            in_specs=[pl.BlockSpec(r.shape, lambda s, p: (0, 0)) for r in rows]
             + [
                 pl.BlockSpec(
                     (pl.Squeezed(), 2 * half, BLOCK, BLOCK),
@@ -189,7 +195,7 @@
         out_shape=[out] * pieces,
         compiler_params=PARAMS,
         name="expert",
-    )(place, rows, *packs, *packs)
+    )(place, *rows, *packs, *packs)
 
 
 def weighted(high_ref, low_ref, i, rows_ref):
@@ -266,21 +272,30 @@
     pack = pack_shards(w_gate_up[0], w_down[0])
     meta = jnp.concatenate([route_ids.astype(F32).T, gate_values.T], axis=0)
 
-    near = [lax.ppermute(tokens, "zh", ring(k)) for k in (1, 3)]
+    pieces = range(model // TILE)
+    token_parts = [tokens[:, p * TILE : (p + 1) * TILE] for p in pieces]
     near_metas = [lax.ppermute(meta, "zh", ring(k)) for k in (1, 3)]
+    near = [[lax.ppermute(t, "zh", ring(k)) for k in (1, 3)] for t in token_parts]
     swapped = lax.ppermute(pack, "zl", swap)
     mine = lax.all_gather(pack, "x")
     own = plan(group, slots, meta)
-    arrived_own = over_y(gather(own[0], tokens), (-1, model))
-    near, near_metas, swapped, arrived_own = barrier((near, near_metas, swapped, arrived_own))
+    arrived_own = over_y(gather(own[0], [[[tokens]]]), (-1, model))
+    sides = plan(group, slots, *near_metas)
+    near[0], sides, swapped, arrived_own = barrier((near[0], sides, swapped, arrived_own))
     other = lax.all_gather(swapped, "x")
-
-    sides = plan(group, slots, *near_metas)
-    arrived_sides = over_y(gather(sides[0], *near), (-1, model))
-    far = [lax.ppermute(near[0][:half], "zh", ring(1)), lax.ppermute(near[1][half:], "zh", ring(3))]
     far_meta = lax.ppermute(near_metas[0], "zh", ring(1))
+
+    arrived_sides, far = [], []
+    for p in pieces:
+        arrived_sides.append(over_y(gather(sides[0], [[[t] for t in near[p]]]), (-1, TILE)))
+        below, above = near[p]
+        far.append(
+            [lax.ppermute(below[:half], "zh", ring(1)), lax.ppermute(above[half:], "zh", ring(3))]
+        )
+        if p == 0:
+            near[1], arrived_sides, far = barrier((near[1], arrived_sides, far))
     across = plan(group, slots, far_meta)
-    sent, mine, arrived_sides = barrier((gather(across[0], *far), mine, arrived_sides))
+    sent, mine, arrived_sides = barrier((gather(across[0], [[f] for f in far]), mine, arrived_sides))
     mine_swapped = lax.ppermute(mine, "core", swap)
     arrived_across = over_y(sent, (-1, model))
     packs = [mine, mine_swapped, other, lax.ppermute(other, "core", swap)]
@@ -289,22 +304,21 @@
 
     made_sides = expert(place, arrived_sides, packs, 2)
     made_sides, arrived_across = barrier((made_sides, arrived_across))
-    (made,) = expert(place, arrived_across, packs, 1)
-
-    back = over_y(made, (YS, 1, slots, model))
-    pieces = range(model // TILE)
+    (made,) = expert(place, [arrived_across], packs, 1)
+    made, arrived_own = barrier((made, arrived_own))
+    (made_own,) = expert(place, [arrived_own], packs, 1)
+
+    back, made_own = barrier((over_y(made, (YS, 1, slots, model)), made_own))
     parts = [combine(split_kernel, across, back, p, 1, [], (half, half)) for p in pieces]
     passed = [
         [lax.ppermute(top, "zh", ring(3)), lax.ppermute(bottom, "zh", ring(1))] for top, bottom in parts
     ]
-    arrived_own, parts = barrier((arrived_own, parts))
-    (made_own,) = expert(place, arrived_own, packs, 1)
     home, rows = [], made_sides[0]
     for p in pieces:
         rows, back = barrier((rows, back))
         back = over_y(rows, (YS, 2, slots, TILE))
         if p == 0:
-            rows, passed[0], made_own = barrier((made_sides[1], passed[0], made_own))
+            rows, passed[0] = barrier((made_sides[1], passed[0]))
             back, passed[1] = barrier((back, passed[1]))
         below, above = combine(add_kernel, sides, back, 0, 1, passed[p], (tok_rows, tok_rows))
         if p == 1:

time: 317 us -> 325 us (1.025)
  blocking collectives: 25.7 us -> 0 us
  waiting for transfers between devices: 127 us -> 141 us
  starting transfers between devices: 62.6 us -> 74.2 us
  local copies, waits for them, and re-layouts: 9.15 us -> 13 us
  Pallas kernels: 75.7 us -> 79.1 us
    ppermute x4 -> x8, waiting for transfers between devices: 0.01 us -> 32.3 us  [the longest x4 20.9 us: on_device(): lax.ppermute(t, 'zh', ring(k))]
    all_to_all x1 -> x0, blocking collectives: 25.7 us -> none  [over_y(): lax.all_to_all(rows.reshape(YS, -1, rows.shape[-1]), 'y', split_axis=0, c...]
    ppermute x2, waiting for transfers between devices: 58.3 us -> 33.4 us  [on_device(): near_metas = [lax.ppermute(meta, 'zh', ring(k)) for k in (1, 3)]]
    ppermute x1, waiting for transfers between devices: 23.9 us -> 8.27 us  [on_device(): far_meta = lax.ppermute(near_metas[0], 'zh', ring(1))]
    ppermute x2, waiting for transfers between devices: 1.19 us -> 13.5 us  [on_device(): lax.ppermute(top, 'zh', ring(3))]
    all_to_all x6 -> x8, starting transfers between devices: 29.6 us -> 39.1 us  [over_y(): lax.all_to_all(rows.reshape(YS, -1, rows.shape[-1]), 'y', split_axis=0, c...]
    ppermute x2, starting transfers between devices: 12.2 us -> 3.38 us  [on_device(): lax.ppermute(below, 'zh', ring(3))]
    all_gather x1, waiting for transfers between devices: 6.48 us -> 0.02 us  [on_device(): other = lax.all_gather(swapped, 'x')]
  transfers between devices with their start and end apart: 26 -> 32, of which waited for: 10 -> 18; matrix products, arithmetic and copies ran while one was open for 1% -> 1% of each run, Pallas kernels for 18% -> 18%
where the time goes in v5:
time: 325 us; the launch traced here: 322 us
  waiting for transfers between devices  141 us (43%)
  Pallas kernels  79.1 us (24%)
  starting transfers between devices  74.2 us (23%)
  between operations  13.6 us (4%)
  local copies, waits for them, and re-layouts  13 us (4%)
    pallas_call x3, Pallas kernels, expert(): pl.pallas_call(functools.partial(expert_kernel, len(rows)), grid_spec=plt...  44.4 us
    all_to_all x8, starting transfers between devices, over_y(): lax.all_to_all(rows.reshape(YS, -1, rows.shape[-1]), 'y', split_axis=0, c...  39.1 us
    ppermute x2, waiting for transfers between devices, on_device(): near_metas = [lax.ppermute(meta, 'zh', ring(k)) for k in (1, 3)]  33.4 us
    ppermute x4, waiting for transfers between devices, on_device(): lax.ppermute(t, 'zh', ring(k))  20.9 us
    all_to_all x8, waiting for transfers between devices, over_y(): lax.all_to_all(rows.reshape(YS, -1, rows.shape[-1]), 'y', split_axis=0, c...  18.7 us
    pallas_call x5, Pallas kernels, combine(): pl.pallas_call(kernel, grid=(steps,), out_shape=[jax.ShapeDtypeStruct((n,...  15 us
    ppermute x2, waiting for transfers between devices, on_device(): lax.ppermute(top, 'zh', ring(3))  13.5 us
    ppermute x2, waiting for transfers between devices, on_device(): lax.ppermute(below, 'zh', ring(3))  13 us
  transfers between devices with their start and end apart: 32, of which 18 were waited for; matrix products, arithmetic and copies ran while one was open for 1% of the time, Pallas kernels for 18%

profile of v5, /device:TPU:10, one launch (start us, length us, event | category | flops | bytes accessed | tf_op | source)
XLA Modules:
  0.0 322.1 jit_solution(2455147285963598488)
XLA Ops:
  13.4 3.0 gather.4
  16.4 5.0 %all-to-all-start = ((bf16[4,48,4096]{2,1,0:T(8,128)(2,1)}), bf16[4,48,4096]{2,1,0:T(8,128)(2,1)S(1)}, u32[]{:S(2)}, u32[]{:S(2)}) async-start(bf16[4,48,4096]{2,1,0:T(8,128)(2,1)} %bitcast.52), calls=%async_computation | async-start | bytes 3145728 | tf_op jit(solution)/shard_map/all_to_all | solution.py:259
  22.3 5.4 %collective-permute-start.5 = (bf16[128,2048]{1,0:T(8,128)(2,1)S(1)}, bf16[128,2048]{1,0:T(8,128)(2,1)S(1)}, u32[]{:S(2)}, u32[]{:S(2)}) collective-permute-start(bf16[128,2048]{1,0:T(8,128)(2,1)S(1)} %get-tuple-element.115), channel_id=1, source_target_pairs={{0,192},{64,0},{128,64},{192,128},{1,193},{65,1},{129,65},{193,129... | collective-permute-start | bytes 1572872 | tf_op jit(solution)/shard_map/ppermute | solution.py:278
  27.7 4.1 %collective-permute-start.6 = (f32[8,128]{1,0:T(8,128)S(1)}, f32[8,128]{1,0:T(8,128)S(1)}, u32[]{:S(2)}, u32[]{:S(2)}) collective-permute-start(f32[8,128]{1,0:T(8,128)S(1)} %copy-done.27), channel_id=1, source_target_pairs={{0,192},{64,0},{128,64},{192,128},{1,193},{65,1},{129,65},{193,129... | collective-permute-start | bytes 12296 | tf_op jit(solution)/shard_map/ppermute | solution.py:277
  31.9 6.3 %collective-permute-done.6.refs_1_ = f32[8,128]{1,0:T(8,128)S(1)} collective-permute-done((f32[8,128]{1,0:T(8,128)S(1)}, f32[8,128]{1,0:T(8,128)S(1)}, u32[]{:S(2)}, u32[]{:S(2)}) %collective-permute-start.6) | collective-permute-done | bytes 4128 | tf_op jit(solution)/shard_map/ppermute | solution.py:277
  38.2 27.1 %collective-permute-done.refs_0_ = f32[8,128]{1,0:T(8,128)S(1)} collective-permute-done((f32[8,128]{1,0:T(8,128)S(1)}, f32[8,128]{1,0:T(8,128)S(1)}, u32[]{:S(2)}, u32[]{:S(2)}) %collective-permute-start) | collective-permute-done | bytes 4128 | tf_op jit(solution)/shard_map/ppermute | solution.py:277
  71.5 5.0 %all-to-all-start.1 = ((bf16[4,96,2048]{2,1,0:T(8,128)(2,1)}), bf16[4,96,2048]{2,1,0:T(8,128)(2,1)S(1)}, u32[]{:S(2)}, u32[]{:S(2)}) async-start(bf16[4,96,2048]{2,1,0:T(8,128)(2,1)} %bitcast.54), calls=%async_computation.1 | async-start | bytes 3145728 | tf_op jit(solution)/shard_map/all_to_all | solution.py:259
  82.5 18.0 %collective-permute-done.3.refs_1_ = bf16[128,2048]{1,0:T(8,128)(2,1)S(1)} collective-permute-done((bf16[128,2048]{1,0:T(8,128)(2,1)}, bf16[128,2048]{1,0:T(8,128)(2,1)S(1)}, u32[]{:S(2)}, u32[]{:S(2)}) %collective-permute-start.3) | collective-permute-done | bytes 524320 | tf_op jit(solution)/shard_map/ppermute | solution.py:278
  103.4 9.0 %collective-permute-done.9.refs_1_ = bf16[64,2048]{1,0:T(8,128)(2,1)S(1)} collective-permute-done((bf16[64,2048]{1,0:T(8,128)(2,1)S(1)}, bf16[64,2048]{1,0:T(8,128)(2,1)S(1)}, u32[]{:S(2)}, u32[]{:S(2)}) %collective-permute-start.9) | collective-permute-done | bytes 262176 | tf_op jit(solution)/shard_map/ppermute | solution.py:293
  114.8 3.6 %gather.7 = bf16[4,2,48,2048]{3,2,1,0:T(8,128)(2,1)} custom-call(bf16[2,192,128]{2,1,0:T(8,128)(2,1)} %get-tuple-element.67.pick_ref, bf16[128,2048]{1,0:T(8,128)(2,1)} %copy-done.14, bf16[128,2048]{1,0:T(8,128)(2,1)} %copy-done.13), custom_call_target="tpu_custom_call" | custom-call | tf_op jit(solution)/shard_map/gather/pallas_call | solution.py:112
  118.5 4.8 %all-to-all-start.2 = ((bf16[4,96,2048]{2,1,0:T(8,128)(2,1)}), bf16[4,96,2048]{2,1,0:T(8,128)(2,1)S(1)}, u32[]{:S(2)}, u32[]{:S(2)}) async-start(bf16[4,96,2048]{2,1,0:T(8,128)(2,1)} %bitcast.53), calls=%async_computation.2 | async-start | bytes 3145728 | tf_op jit(solution)/shard_map/all_to_all | solution.py:259
  129.8 8.3 %collective-permute-done.1.refs_0_ = f32[8,128]{1,0:T(8,128)S(1)} collective-permute-done((f32[8,128]{1,0:T(8,128)S(1)}, f32[8,128]{1,0:T(8,128)S(1)}, u32[]{:S(2)}, u32[]{:S(2)}) %collective-permute-start.1) | collective-permute-done | bytes 4128 | tf_op jit(solution)/shard_map/ppermute | solution.py:286
  145.0 4.8 %all-to-all-start.3 = ((bf16[4,48,4096]{2,1,0:T(8,128)(2,1)}), bf16[4,48,4096]{2,1,0:T(8,128)(2,1)S(1)}, u32[]{:S(2)}, u32[]{:S(2)}) async-start(bf16[4,48,4096]{2,1,0:T(8,128)(2,1)} %bitcast.51), calls=%async_computation.3 | async-start | bytes 3145728 | tf_op jit(solution)/shard_map/all_to_all | solution.py:259
  152.4 6.7 %collective-permute-done.13.refs_5_.refs_9_.refs_4_.refs_8_ = bf16[4,9,256,256]{3,2,1,0:T(8,128)(2,1)} collective-permute-done((bf16[4,9,256,256]{3,2,1,0:T(8,128)(2,1)}, bf16[4,9,256,256]{3,2,1,0:T(8,128)(2,1)}, u32[]{:S(2)}, u32[]{:S(2)}) %collective-permute-start.13) | collective-permute-done | bytes 4718624 | tf_op jit(solution)/shard_map/ppermute | solution.py:301
  159.1 17.1 %expert.3 = (bf16[384,2048]{1,0:T(8,128)(2,1)}, bf16[384,2048]{1,0:T(8,128)(2,1)}) custom-call(s32[4]{0:T(128)} %pad_add_fusion.place_ref, bf16[384,2048]{1,0:T(8,128)(2,1)} %bitcast.45, bf16[384,2048]{1,0:T(8,128)(2,1)} %bitcast.46, bf16[4,9,256,256]{3,2,1,0:T(8,128)(2,1)} %bitcast.29, ...), custom_call_target="tpu_custom_call" | custom-call | tf_op jit(solution)/shard_map/expert/pallas_call | solution.py:169
  177.4 13.6 %expert.4 = bf16[192,4096]{1,0:T(8,128)(2,1)} custom-call(s32[4]{0:T(128)} %pad_add_fusion.place_ref, bf16[192,4096]{1,0:T(8,128)(2,1)} %bitcast.47, bf16[4,9,256,256]{3,2,1,0:T(8,128)(2,1)} %bitcast.31, bf16[4,9,256,256]{3,2,1,0:T(8,128)(2,1)} %collective-permute-done.12.refs_3_.refs_7_.refs_2_.refs_6_, bf16[4,9,256,256]{3,2,1,0:T(8,128)(2,1)} %bitcast.38, ...), custom_call_target="tpu_custom_call" | custom-call | tf_op jit(solution)/shard_map/expert/pallas_call | solution.py:169
  191.0 4.8 %all-to-all-start.4 = ((bf16[4,48,4096]{2,1,0:T(8,128)(2,1)}), bf16[4,48,4096]{2,1,0:T(8,128)(2,1)S(1)}, u32[]{:S(2)}, u32[]{:S(2)}) async-start(bf16[4,48,4096]{2,1,0:T(8,128)(2,1)} %bitcast.48), calls=%async_computation.4 | async-start | bytes 3145728 | tf_op jit(solution)/shard_map/all_to_all | solution.py:259
  195.8 13.7 %expert.5 = bf16[192,4096]{1,0:T(8,128)(2,1)} custom-call(s32[4]{0:T(128)} %pad_add_fusion.place_ref, bf16[192,4096]{1,0:T(8,128)(2,1)} %bitcast.44, bf16[4,9,256,256]{3,2,1,0:T(8,128)(2,1)} %bitcast.33, bf16[4,9,256,256]{3,2,1,0:T(8,128)(2,1)} %collective-permute-done.12.refs_3_.refs_7_.refs_2_.refs_6_, bf16[4,9,256,256]{3,2,1,0:T(8,128)(2,1)} %bitcast.40, ...), custom_call_target="tpu_custom_call" | custom-call | tf_op jit(solution)/shard_map/expert/pallas_call | solution.py:169
  209.5 5.9 %all-to-all-done.4 = bf16[4,48,4096]{2,1,0:T(8,128)(2,1)S(1)} async-done(((bf16[4,48,4096]{2,1,0:T(8,128)(2,1)}), bf16[4,48,4096]{2,1,0:T(8,128)(2,1)S(1)}, u32[]{:S(2)}, u32[]{:S(2)}) %all-to-all-start.4) | async-done | bytes 1572896 | tf_op jit(solution)/shard_map/all_to_all | solution.py:259
  216.5 5.0 %all-to-all-start.5 = ((bf16[4,96,2048]{2,1,0:T(8,128)(2,1)}), bf16[4,96,2048]{2,1,0:T(8,128)(2,1)S(1)}, u32[]{:S(2)}, u32[]{:S(2)}) async-start(bf16[4,96,2048]{2,1,0:T(8,128)(2,1)} %bitcast.57), calls=%async_computation.5 | async-start | bytes 3145728 | tf_op jit(solution)/shard_map/all_to_all | solution.py:259
  229.3 3.1 collective-permute-start.14
  232.4 9.8 %collective-permute-done.16.top_ref = bf16[64,2048]{1,0:T(8,128)(2,1)S(1)} collective-permute-done((bf16[64,2048]{1,0:T(8,128)(2,1)}, bf16[64,2048]{1,0:T(8,128)(2,1)S(1)}, u32[]{:S(2)}, u32[]{:S(2)}) %collective-permute-start.16) | collective-permute-done | bytes 262176 | tf_op jit(solution)/shard_map/ppermute | solution.py:314
  244.0 3.7 %collective-permute-done.14.top_ref = bf16[64,2048]{1,0:T(8,128)(2,1)S(1)} collective-permute-done((bf16[64,2048]{1,0:T(8,128)(2,1)}, bf16[64,2048]{1,0:T(8,128)(2,1)S(1)}, u32[]{:S(2)}, u32[]{:S(2)}) %collective-permute-start.14) | collective-permute-done | bytes 262176 | tf_op jit(solution)/shard_map/ppermute | solution.py:314
  250.8 4.8 %all-to-all-start.6 = ((bf16[4,96,2048]{2,1,0:T(8,128)(2,1)}), bf16[4,96,2048]{2,1,0:T(8,128)(2,1)S(1)}, u32[]{:S(2)}, u32[]{:S(2)}) async-start(bf16[4,96,2048]{2,1,0:T(8,128)(2,1)} %bitcast.56), calls=%async_computation.6 | async-start | bytes 3145728 | tf_op jit(solution)/shard_map/all_to_all | solution.py:259
  255.6 3.1 combine.7
  258.7 3.4 %collective-permute-start.18 = (bf16[128,2048]{1,0:T(8,128)(2,1)}, bf16[128,2048]{1,0:T(8,128)(2,1)S(1)}, u32[]{:S(2)}, u32[]{:S(2)}) collective-permute-start(bf16[128,2048]{1,0:T(8,128)(2,1)} %get-tuple-element.102), channel_id=1, source_target_pairs={{0,192},{64,0},{128,64},{192,128},{1,193},{65,1},{129,65},{193,129... | collective-permute-start | bytes 1572872 | tf_op jit(solution)/shard_map/ppermute | solution.py:326
  262.1 12.9 %all-to-all-done.6 = bf16[4,96,2048]{2,1,0:T(8,128)(2,1)S(1)} async-done(((bf16[4,96,2048]{2,1,0:T(8,128)(2,1)}), bf16[4,96,2048]{2,1,0:T(8,128)(2,1)S(1)}, u32[]{:S(2)}, u32[]{:S(2)}) %all-to-all-start.6) | async-done | bytes 1572896 | tf_op jit(solution)/shard_map/all_to_all | solution.py:259
  276.1 3.1 combine.8
  279.2 8.3 %collective-permute-done.19.refs_1_ = bf16[128,2048]{1,0:T(8,128)(2,1)S(1)} collective-permute-done((bf16[128,2048]{1,0:T(8,128)(2,1)}, bf16[128,2048]{1,0:T(8,128)(2,1)S(1)}, u32[]{:S(2)}, u32[]{:S(2)}) %collective-permute-start.19) | collective-permute-done | bytes 524320 | tf_op jit(solution)/shard_map/ppermute | solution.py:326
  288.3 4.8 %all-to-all-start.7 = ((bf16[4,48,4096]{2,1,0:T(8,128)(2,1)}), bf16[4,48,4096]{2,1,0:T(8,128)(2,1)S(1)}, u32[]{:S(2)}, u32[]{:S(2)}) async-start(bf16[4,48,4096]{2,1,0:T(8,128)(2,1)} %bitcast.25), calls=%async_computation.7 | async-start | bytes 3145728 | tf_op jit(solution)/shard_map/all_to_all | solution.py:259
  296.1 13.0 %collective-permute-done.20.refs_2_ = bf16[128,2048]{1,0:T(8,128)(2,1)S(1)} collective-permute-done((bf16[128,2048]{1,0:T(8,128)(2,1)}, bf16[128,2048]{1,0:T(8,128)(2,1)S(1)}, u32[]{:S(2)}, u32[]{:S(2)}) %collective-permute-start.20) | collective-permute-done | bytes 524320 | tf_op jit(solution)/shard_map/ppermute | solution.py:326
  311.4 3.8 %combine.9 = bf16[128,4096]{1,0:T(8,128)(2,1)} custom-call(bf16[1,192,128]{2,1,0:T(8,128)(2,1)} %get-tuple-element.60.high_ref, bf16[1,192,128]{2,1,0:T(8,128)(2,1)} %get-tuple-element.61.low_ref, bf16[4,1,48,4096]{3,2,1,0:T(8,128)(2,1)} %bitcast.55, bf16[128,2048]{1,0:T(8,128)(2,1)} %copy-done.15, bf16[128,2048]{1,0:T(8,128)(2,1)} %copy-done.16, ...), custom_call_target="tpu_custom_call" | custom-call | tf_op jit(solution)/shard_map/combine/pallas_call | solution.py:242
  (128 shorter events, 63.3 us)
Async XLA Ops:
  6.5 137.3 %all-gather.5.cloned.1.call-start = ((), (), s32[]{:S(2)}) async-start(), calls=%async_computation.8 | async-start | bytes 5898240 | tf_op jit(solution)/shard_map/all_gather | solution.py:280
  9.4 58.2 %collective-permute-start.7 = (bf16[9,256,256]{2,1,0:T(8,128)(2,1)}, bf16[9,256,256]{2,1,0:T(8,128)(2,1)}, u32[]{:S(2)}, u32[]{:S(2)}) collective-permute-start(bf16[9,256,256]{2,1,0:T(8,128)(2,1)} %pack.1), channel_id=1, source_target_pairs={{0,2},{2,0},{1,3},{3,1},{4,6},{6,4},{5,7},{7,5},{8,10},{10,8},{9,1... | collective-permute-start | bytes 3538952 | tf_op jit(solution)/shard_map/ppermute | solution.py:279
  16.4 51.1 %all-to-all-start = ((bf16[4,48,4096]{2,1,0:T(8,128)(2,1)}), bf16[4,48,4096]{2,1,0:T(8,128)(2,1)S(1)}, u32[]{:S(2)}, u32[]{:S(2)}) async-start(bf16[4,48,4096]{2,1,0:T(8,128)(2,1)} %bitcast.52), calls=%async_computation | async-start | bytes 3145728 | tf_op jit(solution)/shard_map/all_to_all | solution.py:259
  21.5 122.7 %all-gather.7.cloned.1.call-start = ((), (), s32[]{:S(2)}) async-start(), calls=%async_computation.9 | async-start | bytes 5898240 | tf_op jit(solution)/shard_map/all_gather | solution.py:285
  22.3 45.2 %collective-permute-start.5 = (bf16[128,2048]{1,0:T(8,128)(2,1)S(1)}, bf16[128,2048]{1,0:T(8,128)(2,1)S(1)}, u32[]{:S(2)}, u32[]{:S(2)}) collective-permute-start(bf16[128,2048]{1,0:T(8,128)(2,1)S(1)} %get-tuple-element.115), channel_id=1, source_target_pairs={{0,192},{64,0},{128,64},{192,128},{1,193},{65,1},{129,65},{193,129... | collective-permute-start | bytes 1572872 | tf_op jit(solution)/shard_map/ppermute | solution.py:278
  27.7 39.8 %collective-permute-start.4 = (bf16[128,2048]{1,0:T(8,128)(2,1)S(1)}, bf16[128,2048]{1,0:T(8,128)(2,1)S(1)}, u32[]{:S(2)}, u32[]{:S(2)}) collective-permute-start(bf16[128,2048]{1,0:T(8,128)(2,1)S(1)} %get-tuple-element.115), channel_id=1, source_target_pairs={{0,64},{64,128},{128,192},{192,0},{1,65},{65,129},{129,193},{193,1... | collective-permute-start | bytes 1572872 | tf_op jit(solution)/shard_map/ppermute | solution.py:278
  27.7 10.5 %collective-permute-start.6 = (f32[8,128]{1,0:T(8,128)S(1)}, f32[8,128]{1,0:T(8,128)S(1)}, u32[]{:S(2)}, u32[]{:S(2)}) collective-permute-start(f32[8,128]{1,0:T(8,128)S(1)} %copy-done.27), channel_id=1, source_target_pairs={{0,192},{64,0},{128,64},{192,128},{1,193},{65,1},{129,65},{193,129... | collective-permute-start | bytes 12296 | tf_op jit(solution)/shard_map/ppermute | solution.py:277
  31.9 33.4 %collective-permute-start = (f32[8,128]{1,0:T(8,128)S(1)}, f32[8,128]{1,0:T(8,128)S(1)}, u32[]{:S(2)}, u32[]{:S(2)}) collective-permute-start(f32[8,128]{1,0:T(8,128)S(1)} %copy-done.27), channel_id=1, source_target_pairs={{0,64},{64,128},{128,192},{192,0},{1,65},{65,129},{129,193},{193,1... | collective-permute-start | bytes 12296 | tf_op jit(solution)/shard_map/ppermute | solution.py:277
  71.5 43.4 %all-to-all-start.1 = ((bf16[4,96,2048]{2,1,0:T(8,128)(2,1)}), bf16[4,96,2048]{2,1,0:T(8,128)(2,1)S(1)}, u32[]{:S(2)}, u32[]{:S(2)}) async-start(bf16[4,96,2048]{2,1,0:T(8,128)(2,1)} %bitcast.54), calls=%async_computation.1 | async-start | bytes 3145728 | tf_op jit(solution)/shard_map/all_to_all | solution.py:259
  76.5 24.0 %collective-permute-start.3 = (bf16[128,2048]{1,0:T(8,128)(2,1)}, bf16[128,2048]{1,0:T(8,128)(2,1)S(1)}, u32[]{:S(2)}, u32[]{:S(2)}) collective-permute-start(bf16[128,2048]{1,0:T(8,128)(2,1)} %get-tuple-element.116), channel_id=1, source_target_pairs={{0,192},{64,0},{128,64},{192,128},{1,193},{65,1},{129,65},{193,129... | collective-permute-start | bytes 1572872 | tf_op jit(solution)/shard_map/ppermute | solution.py:278
  78.0 25.5 %collective-permute-start.2 = (bf16[128,2048]{1,0:T(8,128)(2,1)}, bf16[128,2048]{1,0:T(8,128)(2,1)S(1)}, u32[]{:S(2)}, u32[]{:S(2)}) collective-permute-start(bf16[128,2048]{1,0:T(8,128)(2,1)} %get-tuple-element.116), channel_id=1, source_target_pairs={{0,64},{64,128},{128,192},{192,0},{1,65},{65,129},{129,193},{193,1... | collective-permute-start | bytes 1572872 | tf_op jit(solution)/shard_map/ppermute | solution.py:278
  79.5 33.0 %collective-permute-start.9 = (bf16[64,2048]{1,0:T(8,128)(2,1)S(1)}, bf16[64,2048]{1,0:T(8,128)(2,1)S(1)}, u32[]{:S(2)}, u32[]{:S(2)}) collective-permute-start(bf16[64,2048]{1,0:T(8,128)(2,1)S(1)} %slice.21), channel_id=1, source_target_pairs={{0,192},{64,0},{128,64},{192,128},{1,193},{65,1},{129,65},{193,129... | collective-permute-start | bytes 786440 | tf_op jit(solution)/shard_map/ppermute | solution.py:293
  82.2 32.6 %collective-permute-start.8 = (bf16[64,2048]{1,0:T(8,128)(2,1)S(1)}, bf16[64,2048]{1,0:T(8,128)(2,1)S(1)}, u32[]{:S(2)}, u32[]{:S(2)}) collective-permute-start(bf16[64,2048]{1,0:T(8,128)(2,1)S(1)} %slice.20), channel_id=1, source_target_pairs={{0,64},{64,128},{128,192},{192,0},{1,65},{65,129},{129,193},{193,1... | collective-permute-start | bytes 786440 | tf_op jit(solution)/shard_map/ppermute | solution.py:293
  118.5 25.4 %all-to-all-start.2 = ((bf16[4,96,2048]{2,1,0:T(8,128)(2,1)}), bf16[4,96,2048]{2,1,0:T(8,128)(2,1)S(1)}, u32[]{:S(2)}, u32[]{:S(2)}) async-start(bf16[4,96,2048]{2,1,0:T(8,128)(2,1)} %bitcast.53), calls=%async_computation.2 | async-start | bytes 3145728 | tf_op jit(solution)/shard_map/all_to_all | solution.py:259
  125.2 14.9 %collective-permute-start.11 = (bf16[64,2048]{1,0:T(8,128)(2,1)S(1)}, bf16[64,2048]{1,0:T(8,128)(2,1)S(1)}, u32[]{:S(2)}, u32[]{:S(2)}) collective-permute-start(bf16[64,2048]{1,0:T(8,128)(2,1)S(1)} %slice.23), channel_id=1, source_target_pairs={{0,192},{64,0},{128,64},{192,128},{1,193},{65,1},{129,65},{193,129... | collective-permute-start | bytes 786440 | tf_op jit(solution)/shard_map/ppermute | solution.py:293
  125.3 14.8 %collective-permute-start.10 = (bf16[64,2048]{1,0:T(8,128)(2,1)S(1)}, bf16[64,2048]{1,0:T(8,128)(2,1)S(1)}, u32[]{:S(2)}, u32[]{:S(2)}) collective-permute-start(bf16[64,2048]{1,0:T(8,128)(2,1)S(1)} %slice.22), channel_id=1, source_target_pairs={{0,64},{64,128},{128,192},{192,0},{1,65},{65,129},{129,193},{193,1... | collective-permute-start | bytes 786440 | tf_op jit(solution)/shard_map/ppermute | solution.py:293
  128.2 9.8 %collective-permute-start.1 = (f32[8,128]{1,0:T(8,128)S(1)}, f32[8,128]{1,0:T(8,128)S(1)}, u32[]{:S(2)}, u32[]{:S(2)}) collective-permute-start(f32[8,128]{1,0:T(8,128)S(1)} %copy-done.30), channel_id=1, source_target_pairs={{0,64},{64,128},{128,192},{192,0},{1,65},{65,129},{129,193},{193,1... | collective-permute-start | bytes 12296 | tf_op jit(solution)/shard_map/ppermute | solution.py:286
  143.8 8.5 %collective-permute-start.12 = (bf16[4,9,256,256]{3,2,1,0:T(8,128)(2,1)}, bf16[4,9,256,256]{3,2,1,0:T(8,128)(2,1)}, u32[]{:S(2)}, u32[]{:S(2)}) collective-permute-start(bf16[4,9,256,256]{3,2,1,0:T(8,128)(2,1)} %bitcast.28), channel_id=1, source_target_pairs={{0,1},{1,0},{2,3},{3,2},{4,5},{5,4},{6,7},{7,6},{8,9},{9,8},{10,11... | collective-permute-start | bytes 14155784 | tf_op jit(solution)/shard_map/ppermute | solution.py:299
  144.1 15.0 %collective-permute-start.13 = (bf16[4,9,256,256]{3,2,1,0:T(8,128)(2,1)}, bf16[4,9,256,256]{3,2,1,0:T(8,128)(2,1)}, u32[]{:S(2)}, u32[]{:S(2)}) collective-permute-start(bf16[4,9,256,256]{3,2,1,0:T(8,128)(2,1)} %bitcast.35), channel_id=1, source_target_pairs={{0,1},{1,0},{2,3},{3,2},{4,5},{5,4},{6,7},{7,6},{8,9},{9,8},{10,11... | collective-permute-start | bytes 14155784 | tf_op jit(solution)/shard_map/ppermute | solution.py:301
  145.0 31.2 %all-to-all-start.3 = ((bf16[4,48,4096]{2,1,0:T(8,128)(2,1)}), bf16[4,48,4096]{2,1,0:T(8,128)(2,1)S(1)}, u32[]{:S(2)}, u32[]{:S(2)}) async-start(bf16[4,48,4096]{2,1,0:T(8,128)(2,1)} %bitcast.51), calls=%async_computation.3 | async-start | bytes 3145728 | tf_op jit(solution)/shard_map/all_to_all | solution.py:259
  191.0 24.3 %all-to-all-start.4 = ((bf16[4,48,4096]{2,1,0:T(8,128)(2,1)}), bf16[4,48,4096]{2,1,0:T(8,128)(2,1)S(1)}, u32[]{:S(2)}, u32[]{:S(2)}) async-start(bf16[4,48,4096]{2,1,0:T(8,128)(2,1)} %bitcast.48), calls=%async_computation.4 | async-start | bytes 3145728 | tf_op jit(solution)/shard_map/all_to_all | solution.py:259
  216.5 33.1 %all-to-all-start.5 = ((bf16[4,96,2048]{2,1,0:T(8,128)(2,1)}), bf16[4,96,2048]{2,1,0:T(8,128)(2,1)S(1)}, u32[]{:S(2)}, u32[]{:S(2)}) async-start(bf16[4,96,2048]{2,1,0:T(8,128)(2,1)} %bitcast.57), calls=%async_computation.5 | async-start | bytes 3145728 | tf_op jit(solution)/shard_map/all_to_all | solution.py:259
  223.9 18.3 %collective-permute-start.16 = (bf16[64,2048]{1,0:T(8,128)(2,1)}, bf16[64,2048]{1,0:T(8,128)(2,1)S(1)}, u32[]{:S(2)}, u32[]{:S(2)}) collective-permute-start(bf16[64,2048]{1,0:T(8,128)(2,1)} %get-tuple-element.98), channel_id=1, source_target_pairs={{0,192},{64,0},{128,64},{192,128},{1,193},{65,1},{129,65},{193,129... | collective-permute-start | bytes 786440 | tf_op jit(solution)/shard_map/ppermute | solution.py:314
  225.8 18.2 %collective-permute-start.17 = (bf16[64,2048]{1,0:T(8,128)(2,1)}, bf16[64,2048]{1,0:T(8,128)(2,1)S(1)}, u32[]{:S(2)}, u32[]{:S(2)}) collective-permute-start(bf16[64,2048]{1,0:T(8,128)(2,1)} %get-tuple-element.99), channel_id=1, source_target_pairs={{0,64},{64,128},{128,192},{192,0},{1,65},{65,129},{129,193},{193,1... | collective-permute-start | bytes 786440 | tf_op jit(solution)/shard_map/ppermute | solution.py:314
  229.3 18.5 %collective-permute-start.14 = (bf16[64,2048]{1,0:T(8,128)(2,1)}, bf16[64,2048]{1,0:T(8,128)(2,1)S(1)}, u32[]{:S(2)}, u32[]{:S(2)}) collective-permute-start(bf16[64,2048]{1,0:T(8,128)(2,1)} %get-tuple-element.94), channel_id=1, source_target_pairs={{0,192},{64,0},{128,64},{192,128},{1,193},{65,1},{129,65},{193,129... | collective-permute-start | bytes 786440 | tf_op jit(solution)/shard_map/ppermute | solution.py:314
  232.4 17.2 %collective-permute-start.15 = (bf16[64,2048]{1,0:T(8,128)(2,1)}, bf16[64,2048]{1,0:T(8,128)(2,1)S(1)}, u32[]{:S(2)}, u32[]{:S(2)}) collective-permute-start(bf16[64,2048]{1,0:T(8,128)(2,1)} %get-tuple-element.95), channel_id=1, source_target_pairs={{0,64},{64,128},{128,192},{192,0},{1,65},{65,129},{129,193},{193,1... | collective-permute-start | bytes 786440 | tf_op jit(solution)/shard_map/ppermute | solution.py:314
  250.8 24.2 %all-to-all-start.6 = ((bf16[4,96,2048]{2,1,0:T(8,128)(2,1)}), bf16[4,96,2048]{2,1,0:T(8,128)(2,1)S(1)}, u32[]{:S(2)}, u32[]{:S(2)}) async-start(bf16[4,96,2048]{2,1,0:T(8,128)(2,1)} %bitcast.56), calls=%async_computation.6 | async-start | bytes 3145728 | tf_op jit(solution)/shard_map/all_to_all | solution.py:259
  258.7 20.5 %collective-permute-start.18 = (bf16[128,2048]{1,0:T(8,128)(2,1)}, bf16[128,2048]{1,0:T(8,128)(2,1)S(1)}, u32[]{:S(2)}, u32[]{:S(2)}) collective-permute-start(bf16[128,2048]{1,0:T(8,128)(2,1)} %get-tuple-element.102), channel_id=1, source_target_pairs={{0,192},{64,0},{128,64},{192,128},{1,193},{65,1},{129,65},{193,129... | collective-permute-start | bytes 1572872 | tf_op jit(solution)/shard_map/ppermute | solution.py:326
  262.1 25.5 %collective-permute-start.19 = (bf16[128,2048]{1,0:T(8,128)(2,1)}, bf16[128,2048]{1,0:T(8,128)(2,1)S(1)}, u32[]{:S(2)}, u32[]{:S(2)}) collective-permute-start(bf16[128,2048]{1,0:T(8,128)(2,1)} %get-tuple-element.103), channel_id=1, source_target_pairs={{0,64},{64,128},{128,192},{192,0},{1,65},{65,129},{129,193},{193,1... | collective-permute-start | bytes 1572872 | tf_op jit(solution)/shard_map/ppermute | solution.py:326
  288.3 21.7 %all-to-all-start.7 = ((bf16[4,48,4096]{2,1,0:T(8,128)(2,1)}), bf16[4,48,4096]{2,1,0:T(8,128)(2,1)S(1)}, u32[]{:S(2)}, u32[]{:S(2)}) async-start(bf16[4,48,4096]{2,1,0:T(8,128)(2,1)} %bitcast.25), calls=%async_computation.7 | async-start | bytes 3145728 | tf_op jit(solution)/shard_map/all_to_all | solution.py:259
  293.1 15.9 %collective-permute-start.20 = (bf16[128,2048]{1,0:T(8,128)(2,1)}, bf16[128,2048]{1,0:T(8,128)(2,1)S(1)}, u32[]{:S(2)}, u32[]{:S(2)}) collective-permute-start(bf16[128,2048]{1,0:T(8,128)(2,1)} %get-tuple-element.113), channel_id=1, source_target_pairs={{0,192},{64,0},{128,64},{192,128},{1,193},{65,1},{129,65},{193,129... | collective-permute-start | bytes 1572872 | tf_op jit(solution)/shard_map/ppermute | solution.py:326
  293.1 16.9 %collective-permute-start.21 = (bf16[128,2048]{1,0:T(8,128)(2,1)S(1)}, bf16[128,2048]{1,0:T(8,128)(2,1)S(1)}, u32[]{:S(2)}, u32[]{:S(2)}) collective-permute-start(bf16[128,2048]{1,0:T(8,128)(2,1)S(1)} %copy-done.34), channel_id=1, source_target_pairs={{0,64},{64,128},{128,192},{192,0},{1,65},{65,129},{129,193},{193,1... | collective-permute-start | bytes 1572872 | tf_op jit(solution)/shard_map/ppermute | solution.py:326
  (35 other events, 158.7 us)
Sparse Core Ops, SparseCore 0:
  9.5 57.4 all-gather.4
  68.8 55.5 all-gather.6

commit v6 on v5

--- a/solution.py
+++ b/solution.py
@@ -206,25 +206,18 @@
     )
 
 
-def split_kernel(high_ref, low_ref, rows_ref, top_ref, bottom_ref):
-    total = weighted(high_ref, low_ref, 0, rows_ref).astype(BF)
-    half = top_ref.shape[0]
-    top_ref[...], bottom_ref[...] = total[:half], total[half:]
-
-
-def add_kernel(high_ref, low_ref, rows_ref, top_ref, bottom_ref, below_ref, above_ref):
-    half = top_ref.shape[0]
-    below = weighted(high_ref, low_ref, 0, rows_ref)
-    above = weighted(high_ref, low_ref, 1, rows_ref)
-    below_ref[:half, :] = (below[:half] + top_ref[...].astype(F32)).astype(BF)
-    below_ref[half:, :] = below[half:].astype(BF)
-    above_ref[:half, :] = above[:half].astype(BF)
-    above_ref[half:, :] = (above[half:] + bottom_ref[...].astype(F32)).astype(BF)
+def pair_kernel(high_ref, low_ref, rows_ref, below_ref, above_ref):
+    below_ref[...] = weighted(high_ref, low_ref, 0, rows_ref).astype(BF)
+    above_ref[...] = weighted(high_ref, low_ref, 1, rows_ref).astype(BF)
+
+
+def single_kernel(high_ref, low_ref, rows_ref, out_ref):
+    out_ref[...] = weighted(high_ref, low_ref, 0, rows_ref).astype(BF)
 
 
 def last_kernel(high_ref, low_ref, rows_ref, *refs):
-    left, right, out_ref = refs[0:2], refs[2:4], refs[4]
-    total = weighted(high_ref, low_ref, 0, rows_ref)
+    left, right, far_ref, out_ref = refs[0:2], refs[2:4], refs[4], refs[5]
+    total = weighted(high_ref, low_ref, 0, rows_ref) + far_ref[...].astype(F32)
     first = pl.program_id(0) < pl.num_programs(0) // 2
 
     @pl.when(first)
@@ -248,7 +241,10 @@
             table,
             pl.BlockSpec(rows.shape[:-1] + (TILE,), lambda j: (0, 0, 0, first + j)),
         ]
-        + [pl.BlockSpec(a.shape, lambda j: (0, 0)) for a in more],
+        + [
+            pl.BlockSpec((a.shape[0], TILE), lambda j, n=a.shape[1] // TILE: (0, jnp.minimum(j, n - 1)))
+            for a in more
+        ],
         out_specs=[pl.BlockSpec((n, TILE), lambda j: (0, j)) for n in counts],
         compiler_params=PARAMS,
         name="combine",
@@ -293,38 +289,39 @@
             [lax.ppermute(below[:half], "zh", ring(1)), lax.ppermute(above[half:], "zh", ring(3))]
         )
         if p == 0:
-            near[1], arrived_sides, far = barrier((near[1], arrived_sides, far))
+            near[1], arrived_sides, mine = barrier((near[1], arrived_sides, mine))
+            mine_swapped = lax.ppermute(mine, "core", swap)
     across = plan(group, slots, far_meta)
-    sent, mine, arrived_sides = barrier((gather(across[0], [[f] for f in far]), mine, arrived_sides))
-    mine_swapped = lax.ppermute(mine, "core", swap)
+    sent, mine_swapped, arrived_sides, other = barrier(
+        (gather(across[0], [[f] for f in far]), mine_swapped, arrived_sides, other)
+    )
     arrived_across = over_y(sent, (-1, model))
     packs = [mine, mine_swapped, other, lax.ppermute(other, "core", swap)]
     zl, core = lax.axis_index("zl"), lax.axis_index("core")
     place = jnp.stack([zl * 2 + core, zl * 2 + 1 - core, (1 - zl) * 2 + core, (1 - zl) * 2 + 1 - core])
 
-    made_sides = expert(place, arrived_sides, packs, 2)
+    made_sides = expert(place, arrived_sides, packs, len(pieces))
     made_sides, arrived_across = barrier((made_sides, arrived_across))
-    (made,) = expert(place, [arrived_across], packs, 1)
-    made, arrived_own = barrier((made, arrived_own))
+    (made_across,) = expert(place, [arrived_across], packs, 1)
+    made_across, arrived_own = barrier((made_across, arrived_own))
     (made_own,) = expert(place, [arrived_own], packs, 1)
 
-    back, made_own = barrier((over_y(made, (YS, 1, slots, model)), made_own))
-    parts = [combine(split_kernel, across, back, p, 1, [], (half, half)) for p in pieces]
-    passed = [
-        [lax.ppermute(top, "zh", ring(3)), lax.ppermute(bottom, "zh", ring(1))] for top, bottom in parts
-    ]
-    home, rows = [], made_sides[0]
-    for p in pieces:
-        rows, back = barrier((rows, back))
-        back = over_y(rows, (YS, 2, slots, TILE))
-        if p == 0:
-            rows, passed[0] = barrier((made_sides[1], passed[0]))
-            back, passed[1] = barrier((back, passed[1]))
-        below, above = combine(add_kernel, sides, back, 0, 1, passed[p], (tok_rows, tok_rows))
-        if p == 1:
-            made_own, home, below, above = barrier((made_own, home, below, above))
-        home = home + [lax.ppermute(below, "zh", ring(3)), lax.ppermute(above, "zh", ring(1))]
+    def sums_of_sides(rows):
+        below, above = combine(pair_kernel, sides, rows, 0, 1, [], (tok_rows, tok_rows))
+        return [lax.ppermute(below, "zh", ring(3)), lax.ppermute(above, "zh", ring(1))]
+
+    left = over_y(made_sides[0], (YS, 2, slots, TILE))
+    left, made_across, rows = barrier((left, made_across, made_sides[1]))
+    right = over_y(rows, (YS, 2, slots, TILE))
+    left_sums = sums_of_sides(left)
+    right, made_own, left_sums, made_across = barrier((right, made_own, left_sums, made_across))
+    back = over_y(made_across, (YS, 1, slots, model))
+    right_sums = sums_of_sides(right)
+    (part,) = combine(single_kernel, across, back, 0, len(pieces), [], (tok_rows,))
+    made_own, right_sums, part = barrier((made_own, right_sums, part))
+    far_sum = lax.ppermute(part, "zh", ring(2))
     back = over_y(made_own, (YS, 1, slots, model))
+    home = left_sums + right_sums + [far_sum]
     return combine(last_kernel, own, back, 0, len(pieces), home, (tok_rows,))[0]
 
 

time: 325 us -> 337 us (1.037)
  waiting for transfers between devices: 141 us -> 158 us
    ppermute x8 -> x5, waiting for transfers between devices: 39.5 us -> 64 us  [the longest x1 47.7 us: on_device(): far_sum = lax.ppermute(part, 'zh', ring(2))]
    ppermute x2, waiting for transfers between devices: 2.37 us -> 13.2 us  [on_device(): lax.ppermute(below[:half], 'zh', ring(1))]
    ppermute x1, waiting for transfers between devices: 8.27 us -> 0.01 us  [on_device(): far_meta = lax.ppermute(near_metas[0], 'zh', ring(1))]
    ppermute x2, starting transfers between devices: 2.82 us -> 8.1 us  [on_device(): lax.ppermute(above[half:], 'zh', ring(3))]
    ppermute x1, waiting for transfers between devices: 6.75 us -> 1.74 us  [on_device(): packs = [mine, mine_swapped, other, lax.ppermute(other, 'core', swap)]]
    ppermute x2, waiting for transfers between devices: 9.02 us -> 5.07 us  [on_device(): lax.ppermute(above[half:], 'zh', ring(3))]
    ppermute x8 -> x5, starting transfers between devices: 12.3 us -> 9.47 us  [the longest x2 5.1 us: sums_of_sides(): lax.ppermute(above, 'zh', ring(1))]
    pallas_call x5 -> x4, Pallas kernels: 15 us -> 13 us  [combine(): pl.pallas_call(kernel, grid=(steps,), out_shape=[jax.ShapeDtypeStruct((n,...]
  transfers between devices with their start and end apart: 32 -> 29, of which waited for: 18 -> 16; matrix products, arithmetic and copies ran while one was open for 1% -> 1% of each run, Pallas kernels for 18% -> 21%
where the time goes in v6:
time: 337 us; the launch traced here: 336 us
  waiting for transfers between devices  158 us (47%)
  Pallas kernels  76.5 us (23%)
  starting transfers between devices  71.6 us (21%)
  local copies, waits for them, and re-layouts  14.9 us (4%)
  between operations  13.6 us (4%)
    ppermute x1, waiting for transfers between devices, on_device(): far_sum = lax.ppermute(part, 'zh', ring(2))  47.7 us
    pallas_call x3, Pallas kernels, expert(): pl.pallas_call(functools.partial(expert_kernel, len(rows)), grid_spec=plt...  44.4 us
    all_to_all x8, starting transfers between devices, over_y(): lax.all_to_all(rows.reshape(YS, -1, rows.shape[-1]), 'y', split_axis=0, c...  38.9 us
    ppermute x2, waiting for transfers between devices, on_device(): near_metas = [lax.ppermute(meta, 'zh', ring(k)) for k in (1, 3)]  34.1 us
    ppermute x4, waiting for transfers between devices, on_device(): lax.ppermute(t, 'zh', ring(k))  23.9 us
    all_to_all x8, waiting for transfers between devices, over_y(): lax.all_to_all(rows.reshape(YS, -1, rows.shape[-1]), 'y', split_axis=0, c...  15.8 us
    ppermute x2, waiting for transfers between devices, on_device(): lax.ppermute(below[:half], 'zh', ring(1))  13.2 us
    pallas_call x4, Pallas kernels, combine(): pl.pallas_call(kernel, grid=(steps,), out_shape=[jax.ShapeDtypeStruct((n,...  13 us
  transfers between devices with their start and end apart: 29, of which 16 were waited for; matrix products, arithmetic and copies ran while one was open for 1% of the time, Pallas kernels for 21%

profile of v6, /device:TPU:10, one launch (start us, length us, event | category | flops | bytes accessed | tf_op | source)
XLA Modules:
  0.0 335.7 jit_solution(6367056733411693189)
XLA Ops:
  13.4 3.0 gather.4
  16.3 5.0 %all-to-all-start = ((bf16[4,48,4096]{2,1,0:T(8,128)(2,1)}), bf16[4,48,4096]{2,1,0:T(8,128)(2,1)S(1)}, u32[]{:S(2)}, u32[]{:S(2)}) async-start(bf16[4,48,4096]{2,1,0:T(8,128)(2,1)} %bitcast.50), calls=%async_computation | async-start | bytes 3145728 | tf_op jit(solution)/shard_map/all_to_all | solution.py:255
  21.5 5.5 %collective-permute-start.3 = (bf16[128,2048]{1,0:T(8,128)(2,1)S(1)}, bf16[128,2048]{1,0:T(8,128)(2,1)S(1)}, u32[]{:S(2)}, u32[]{:S(2)}) collective-permute-start(bf16[128,2048]{1,0:T(8,128)(2,1)S(1)} %get-tuple-element.102), channel_id=1, source_target_pairs={{0,192},{64,0},{128,64},{192,128},{1,193},{65,1},{129,65},{193,129... | collective-permute-start | bytes 1572872 | tf_op jit(solution)/shard_map/ppermute | solution.py:274
  27.0 4.1 %collective-permute-start.4 = (f32[8,128]{1,0:T(8,128)S(1)}, f32[8,128]{1,0:T(8,128)S(1)}, u32[]{:S(2)}, u32[]{:S(2)}) collective-permute-start(f32[8,128]{1,0:T(8,128)S(1)} %copy-done.22), channel_id=1, source_target_pairs={{0,192},{64,0},{128,64},{192,128},{1,193},{65,1},{129,65},{193,129... | collective-permute-start | bytes 12296 | tf_op jit(solution)/shard_map/ppermute | solution.py:273
  31.1 6.3 %collective-permute-done.4.refs_1_ = f32[8,128]{1,0:T(8,128)S(1)} collective-permute-done((f32[8,128]{1,0:T(8,128)S(1)}, f32[8,128]{1,0:T(8,128)S(1)}, u32[]{:S(2)}, u32[]{:S(2)}) %collective-permute-start.4) | collective-permute-done | bytes 4128 | tf_op jit(solution)/shard_map/ppermute | solution.py:273
  37.4 27.8 %collective-permute-done.refs_0_ = f32[8,128]{1,0:T(8,128)S(1)} collective-permute-done((f32[8,128]{1,0:T(8,128)S(1)}, f32[8,128]{1,0:T(8,128)S(1)}, u32[]{:S(2)}, u32[]{:S(2)}) %collective-permute-start) | collective-permute-done | bytes 4128 | tf_op jit(solution)/shard_map/ppermute | solution.py:273
  68.4 2.9 gather.5
  71.3 4.9 %all-to-all-start.1 = ((bf16[4,96,2048]{2,1,0:T(8,128)(2,1)}), bf16[4,96,2048]{2,1,0:T(8,128)(2,1)S(1)}, u32[]{:S(2)}, u32[]{:S(2)}) async-start(bf16[4,96,2048]{2,1,0:T(8,128)(2,1)} %bitcast.53), calls=%async_computation.1 | async-start | bytes 3145728 | tf_op jit(solution)/shard_map/all_to_all | solution.py:255
  79.2 21.5 %collective-permute-done.9.refs_1_ = bf16[128,2048]{1,0:T(8,128)(2,1)S(1)} collective-permute-done((bf16[128,2048]{1,0:T(8,128)(2,1)S(1)}, bf16[128,2048]{1,0:T(8,128)(2,1)S(1)}, u32[]{:S(2)}, u32[]{:S(2)}) %collective-permute-start.9) | collective-permute-done | bytes 524320 | tf_op jit(solution)/shard_map/ppermute | solution.py:274
  106.8 4.8 %all-to-all-start.2 = ((bf16[4,96,2048]{2,1,0:T(8,128)(2,1)}), bf16[4,96,2048]{2,1,0:T(8,128)(2,1)S(1)}, u32[]{:S(2)}, u32[]{:S(2)}) async-start(bf16[4,96,2048]{2,1,0:T(8,128)(2,1)} %bitcast.48), calls=%async_computation.2 | async-start | bytes 3145728 | tf_op jit(solution)/shard_map/all_to_all | solution.py:255
  113.9 3.9 %collective-permute-start.7 = (bf16[64,2048]{1,0:T(8,128)(2,1)S(1)}, bf16[64,2048]{1,0:T(8,128)(2,1)S(1)}, u32[]{:S(2)}, u32[]{:S(2)}) collective-permute-start(bf16[64,2048]{1,0:T(8,128)(2,1)S(1)} %slice.20), channel_id=1, source_target_pairs={{0,192},{64,0},{128,64},{192,128},{1,193},{65,1},{129,65},{193,129... | collective-permute-start | bytes 786440 | tf_op jit(solution)/shard_map/ppermute | solution.py:289
  118.8 4.2 %collective-permute-start.11 = (bf16[64,2048]{1,0:T(8,128)(2,1)S(1)}, bf16[64,2048]{1,0:T(8,128)(2,1)S(1)}, u32[]{:S(2)}, u32[]{:S(2)}) collective-permute-start(bf16[64,2048]{1,0:T(8,128)(2,1)S(1)} %slice.23), channel_id=1, source_target_pairs={{0,192},{64,0},{128,64},{192,128},{1,193},{65,1},{129,65},{193,129... | collective-permute-start | bytes 786440 | tf_op jit(solution)/shard_map/ppermute | solution.py:289
  125.1 4.5 %collective-permute-done.7.refs_1_ = bf16[64,2048]{1,0:T(8,128)(2,1)S(1)} collective-permute-done((bf16[64,2048]{1,0:T(8,128)(2,1)S(1)}, bf16[64,2048]{1,0:T(8,128)(2,1)S(1)}, u32[]{:S(2)}, u32[]{:S(2)}) %collective-permute-start.7) | collective-permute-done | bytes 262176 | tf_op jit(solution)/shard_map/ppermute | solution.py:289
  129.6 8.3 %collective-permute-done.6.refs_0_ = bf16[64,2048]{1,0:T(8,128)(2,1)S(1)} collective-permute-done((bf16[64,2048]{1,0:T(8,128)(2,1)S(1)}, bf16[64,2048]{1,0:T(8,128)(2,1)S(1)}, u32[]{:S(2)}, u32[]{:S(2)}) %collective-permute-start.6) | collective-permute-done | bytes 262176 | tf_op jit(solution)/shard_map/ppermute | solution.py:289
  138.4 5.0 %collective-permute-done.10.refs_2_ = bf16[64,2048]{1,0:T(8,128)(2,1)S(1)} collective-permute-done((bf16[64,2048]{1,0:T(8,128)(2,1)S(1)}, bf16[64,2048]{1,0:T(8,128)(2,1)S(1)}, u32[]{:S(2)}, u32[]{:S(2)}) %collective-permute-start.10) | collective-permute-done | bytes 262176 | tf_op jit(solution)/shard_map/ppermute | solution.py:289
  148.2 4.8 %all-to-all-start.3 = ((bf16[4,48,4096]{2,1,0:T(8,128)(2,1)}), bf16[4,48,4096]{2,1,0:T(8,128)(2,1)S(1)}, u32[]{:S(2)}, u32[]{:S(2)}) async-start(bf16[4,48,4096]{2,1,0:T(8,128)(2,1)} %bitcast.49), calls=%async_computation.3 | async-start | bytes 3145728 | tf_op jit(solution)/shard_map/all_to_all | solution.py:255
  155.4 17.1 %expert.3 = (bf16[384,2048]{1,0:T(8,128)(2,1)}, bf16[384,2048]{1,0:T(8,128)(2,1)}) custom-call(s32[4]{0:T(128)} %pad_add_fusion.place_ref, bf16[384,2048]{1,0:T(8,128)(2,1)} %bitcast.43, bf16[384,2048]{1,0:T(8,128)(2,1)} %bitcast.44, bf16[4,9,256,256]{3,2,1,0:T(8,128)(2,1)} %bitcast.29, ...), custom_call_target="tpu_custom_call" | custom-call | tf_op jit(solution)/shard_map/expert/pallas_call | solution.py:169
  173.6 4.8 %all-to-all-start.4 = ((bf16[4,96,2048]{2,1,0:T(8,128)(2,1)}), bf16[4,96,2048]{2,1,0:T(8,128)(2,1)S(1)}, u32[]{:S(2)}, u32[]{:S(2)}) async-start(bf16[4,96,2048]{2,1,0:T(8,128)(2,1)} %bitcast.55), calls=%async_computation.4 | async-start | bytes 3145728 | tf_op jit(solution)/shard_map/all_to_all | solution.py:255
  178.4 13.6 %expert.4 = bf16[192,4096]{1,0:T(8,128)(2,1)} custom-call(s32[4]{0:T(128)} %pad_add_fusion.place_ref, bf16[192,4096]{1,0:T(8,128)(2,1)} %bitcast.45, bf16[4,9,256,256]{3,2,1,0:T(8,128)(2,1)} %bitcast.31, bf16[4,9,256,256]{3,2,1,0:T(8,128)(2,1)} %collective-permute-done.12.refs_3_.refs_7_.refs_2_.refs_6_, bf16[4,9,256,256]{3,2,1,0:T(8,128)(2,1)} %bitcast.38, ...), custom_call_target="tpu_custom_call" | custom-call | tf_op jit(solution)/shard_map/expert/pallas_call | solution.py:169
  192.1 5.9 %all-to-all-done.4 = bf16[4,96,2048]{2,1,0:T(8,128)(2,1)S(1)} async-done(((bf16[4,96,2048]{2,1,0:T(8,128)(2,1)}), bf16[4,96,2048]{2,1,0:T(8,128)(2,1)S(1)}, u32[]{:S(2)}, u32[]{:S(2)}) %all-to-all-start.4) | async-done | bytes 1572896 | tf_op jit(solution)/shard_map/all_to_all | solution.py:255
  199.2 5.0 %all-to-all-start.5 = ((bf16[4,96,2048]{2,1,0:T(8,128)(2,1)}), bf16[4,96,2048]{2,1,0:T(8,128)(2,1)S(1)}, u32[]{:S(2)}, u32[]{:S(2)}) async-start(bf16[4,96,2048]{2,1,0:T(8,128)(2,1)} %bitcast.54), calls=%async_computation.5 | async-start | bytes 3145728 | tf_op jit(solution)/shard_map/all_to_all | solution.py:255
  204.1 3.1 combine.4
  210.1 13.7 %expert.5 = bf16[192,4096]{1,0:T(8,128)(2,1)} custom-call(s32[4]{0:T(128)} %pad_add_fusion.place_ref, bf16[192,4096]{1,0:T(8,128)(2,1)} %bitcast.42, bf16[4,9,256,256]{3,2,1,0:T(8,128)(2,1)} %bitcast.33, bf16[4,9,256,256]{3,2,1,0:T(8,128)(2,1)} %collective-permute-done.12.refs_3_.refs_7_.refs_2_.refs_6_, bf16[4,9,256,256]{3,2,1,0:T(8,128)(2,1)} %bitcast.40, ...), custom_call_target="tpu_custom_call" | custom-call | tf_op jit(solution)/shard_map/expert/pallas_call | solution.py:169
  223.8 6.1 %collective-permute-done.14.refs_0_ = bf16[128,2048]{1,0:T(8,128)(2,1)S(1)} collective-permute-done((bf16[128,2048]{1,0:T(8,128)(2,1)}, bf16[128,2048]{1,0:T(8,128)(2,1)S(1)}, u32[]{:S(2)}, u32[]{:S(2)}) %collective-permute-start.14) | collective-permute-done | bytes 524320 | tf_op jit(solution)/shard_map/ppermute | solution.py:311
  234.6 4.8 %all-to-all-start.6 = ((bf16[4,48,4096]{2,1,0:T(8,128)(2,1)}), bf16[4,48,4096]{2,1,0:T(8,128)(2,1)S(1)}, u32[]{:S(2)}, u32[]{:S(2)}) async-start(bf16[4,48,4096]{2,1,0:T(8,128)(2,1)} %bitcast.23), calls=%async_computation.6 | async-start | bytes 3145728 | tf_op jit(solution)/shard_map/all_to_all | solution.py:255
  239.4 3.1 combine.5
  245.4 9.9 %all-to-all-done.6 = bf16[4,48,4096]{2,1,0:T(8,128)(2,1)S(1)} async-done(((bf16[4,48,4096]{2,1,0:T(8,128)(2,1)}), bf16[4,48,4096]{2,1,0:T(8,128)(2,1)S(1)}, u32[]{:S(2)}, u32[]{:S(2)}) %all-to-all-start.6) | async-done | bytes 1572896 | tf_op jit(solution)/shard_map/all_to_all | solution.py:255
  259.3 5.6 %collective-permute-done.16.refs_2_ = bf16[128,2048]{1,0:T(8,128)(2,1)S(1)} collective-permute-done((bf16[128,2048]{1,0:T(8,128)(2,1)}, bf16[128,2048]{1,0:T(8,128)(2,1)S(1)}, u32[]{:S(2)}, u32[]{:S(2)}) %collective-permute-start.16) | collective-permute-done | bytes 524320 | tf_op jit(solution)/shard_map/ppermute | solution.py:311
  267.6 4.8 %all-to-all-start.7 = ((bf16[4,48,4096]{2,1,0:T(8,128)(2,1)}), bf16[4,48,4096]{2,1,0:T(8,128)(2,1)S(1)}, u32[]{:S(2)}, u32[]{:S(2)}) async-start(bf16[4,48,4096]{2,1,0:T(8,128)(2,1)} %bitcast.25), calls=%async_computation.7 | async-start | bytes 3145728 | tf_op jit(solution)/shard_map/all_to_all | solution.py:255
  272.4 3.6 %collective-permute-start.18 = (bf16[128,4096]{1,0:T(8,128)(2,1)S(1)}, bf16[128,4096]{1,0:T(8,128)(2,1)}, u32[]{:S(2)}, u32[]{:S(2)}) collective-permute-start(bf16[128,4096]{1,0:T(8,128)(2,1)S(1)} %copy-done.14), channel_id=1, source_target_pairs={{0,128},{64,192},{128,0},{192,64},{1,129},{65,193},{129,1},{193,65... | collective-permute-start | bytes 3145736 | tf_op jit(solution)/shard_map/ppermute | solution.py:322
  276.0 47.7 %collective-permute-done.18.refs_4_ = bf16[128,4096]{1,0:T(8,128)(2,1)} collective-permute-done((bf16[128,4096]{1,0:T(8,128)(2,1)S(1)}, bf16[128,4096]{1,0:T(8,128)(2,1)}, u32[]{:S(2)}, u32[]{:S(2)}) %collective-permute-start.18) | collective-permute-done | bytes 1048608 | tf_op jit(solution)/shard_map/ppermute | solution.py:322
  324.8 4.0 %combine.7 = bf16[128,4096]{1,0:T(8,128)(2,1)} custom-call(bf16[1,192,128]{2,1,0:T(8,128)(2,1)} %get-tuple-element.53.high_ref, bf16[1,192,128]{2,1,0:T(8,128)(2,1)} %get-tuple-element.54.low_ref, bf16[4,1,48,4096]{3,2,1,0:T(8,128)(2,1)} %bitcast.52, bf16[128,2048]{1,0:T(8,128)(2,1)} %copy-done.15, bf16[128,2048]{1,0:T(8,128)(2,1)} %collective-permute-done.15.refs_1_, ...), custom_call_target="tpu_custom_call" | custom-call | tf_op jit(solution)/shard_map/combine/pallas_call | solution.py:235
  (109 shorter events, 52.9 us)
Async XLA Ops:
  6.5 96.6 %all-gather.5.cloned.1.call-start = ((), (), s32[]{:S(2)}) async-start(), calls=%async_computation.8 | async-start | bytes 5898240 | tf_op jit(solution)/shard_map/all_gather | solution.py:276
  9.3 58.2 %collective-permute-start.5 = (bf16[9,256,256]{2,1,0:T(8,128)(2,1)}, bf16[9,256,256]{2,1,0:T(8,128)(2,1)}, u32[]{:S(2)}, u32[]{:S(2)}) collective-permute-start(bf16[9,256,256]{2,1,0:T(8,128)(2,1)} %pack.1), channel_id=1, source_target_pairs={{0,2},{2,0},{1,3},{3,1},{4,6},{6,4},{5,7},{7,5},{8,10},{10,8},{9,1... | collective-permute-start | bytes 3538952 | tf_op jit(solution)/shard_map/ppermute | solution.py:275
  16.3 51.1 %all-to-all-start = ((bf16[4,48,4096]{2,1,0:T(8,128)(2,1)}), bf16[4,48,4096]{2,1,0:T(8,128)(2,1)S(1)}, u32[]{:S(2)}, u32[]{:S(2)}) async-start(bf16[4,48,4096]{2,1,0:T(8,128)(2,1)} %bitcast.50), calls=%async_computation | async-start | bytes 3145728 | tf_op jit(solution)/shard_map/all_to_all | solution.py:255
  21.4 125.6 %all-gather.7.cloned.1.call-start = ((), (), s32[]{:S(2)}) async-start(), calls=%async_computation.9 | async-start | bytes 5898240 | tf_op jit(solution)/shard_map/all_gather | solution.py:281
  21.5 46.0 %collective-permute-start.3 = (bf16[128,2048]{1,0:T(8,128)(2,1)S(1)}, bf16[128,2048]{1,0:T(8,128)(2,1)S(1)}, u32[]{:S(2)}, u32[]{:S(2)}) collective-permute-start(bf16[128,2048]{1,0:T(8,128)(2,1)S(1)} %get-tuple-element.102), channel_id=1, source_target_pairs={{0,192},{64,0},{128,64},{192,128},{1,193},{65,1},{129,65},{193,129... | collective-permute-start | bytes 1572872 | tf_op jit(solution)/shard_map/ppermute | solution.py:274
  27.0 40.5 %collective-permute-start.2 = (bf16[128,2048]{1,0:T(8,128)(2,1)S(1)}, bf16[128,2048]{1,0:T(8,128)(2,1)S(1)}, u32[]{:S(2)}, u32[]{:S(2)}) collective-permute-start(bf16[128,2048]{1,0:T(8,128)(2,1)S(1)} %get-tuple-element.102), channel_id=1, source_target_pairs={{0,64},{64,128},{128,192},{192,0},{1,65},{65,129},{129,193},{193,1... | collective-permute-start | bytes 1572872 | tf_op jit(solution)/shard_map/ppermute | solution.py:274
  27.0 10.5 %collective-permute-start.4 = (f32[8,128]{1,0:T(8,128)S(1)}, f32[8,128]{1,0:T(8,128)S(1)}, u32[]{:S(2)}, u32[]{:S(2)}) collective-permute-start(f32[8,128]{1,0:T(8,128)S(1)} %copy-done.22), channel_id=1, source_target_pairs={{0,192},{64,0},{128,64},{192,128},{1,193},{65,1},{129,65},{193,129... | collective-permute-start | bytes 12296 | tf_op jit(solution)/shard_map/ppermute | solution.py:273
  31.1 34.1 %collective-permute-start = (f32[8,128]{1,0:T(8,128)S(1)}, f32[8,128]{1,0:T(8,128)S(1)}, u32[]{:S(2)}, u32[]{:S(2)}) collective-permute-start(f32[8,128]{1,0:T(8,128)S(1)} %copy-done.22), channel_id=1, source_target_pairs={{0,64},{64,128},{128,192},{192,0},{1,65},{65,129},{129,193},{193,1... | collective-permute-start | bytes 12296 | tf_op jit(solution)/shard_map/ppermute | solution.py:273
  37.4 27.8 %copy-start.26 = (f32[8,128]{1,0:T(8,128)}, f32[8,128]{1,0:T(8,128)S(1)}, u32[]{:S(2)}) copy-start(f32[8,128]{1,0:T(8,128)S(1)} %collective-permute-done.4.refs_1_) | copy-start | bytes 12292
  71.3 31.7 %all-to-all-start.1 = ((bf16[4,96,2048]{2,1,0:T(8,128)(2,1)}), bf16[4,96,2048]{2,1,0:T(8,128)(2,1)S(1)}, u32[]{:S(2)}, u32[]{:S(2)}) async-start(bf16[4,96,2048]{2,1,0:T(8,128)(2,1)} %bitcast.53), calls=%async_computation.1 | async-start | bytes 3145728 | tf_op jit(solution)/shard_map/all_to_all | solution.py:255
  76.3 24.4 %collective-permute-start.9 = (bf16[128,2048]{1,0:T(8,128)(2,1)S(1)}, bf16[128,2048]{1,0:T(8,128)(2,1)S(1)}, u32[]{:S(2)}, u32[]{:S(2)}) collective-permute-start(bf16[128,2048]{1,0:T(8,128)(2,1)S(1)} %get-tuple-element.101), channel_id=1, source_target_pairs={{0,192},{64,0},{128,64},{192,128},{1,193},{65,1},{129,65},{193,129... | collective-permute-start | bytes 1572872 | tf_op jit(solution)/shard_map/ppermute | solution.py:274
  77.7 25.4 %collective-permute-start.8 = (bf16[128,2048]{1,0:T(8,128)(2,1)S(1)}, bf16[128,2048]{1,0:T(8,128)(2,1)S(1)}, u32[]{:S(2)}, u32[]{:S(2)}) collective-permute-start(bf16[128,2048]{1,0:T(8,128)(2,1)S(1)} %get-tuple-element.101), channel_id=1, source_target_pairs={{0,64},{64,128},{128,192},{192,0},{1,65},{65,129},{129,193},{193,1... | collective-permute-start | bytes 1572872 | tf_op jit(solution)/shard_map/ppermute | solution.py:274
  103.1 43.9 %collective-permute-start.12 = (bf16[4,9,256,256]{3,2,1,0:T(8,128)(2,1)}, bf16[4,9,256,256]{3,2,1,0:T(8,128)(2,1)}, u32[]{:S(2)}, u32[]{:S(2)}) collective-permute-start(bf16[4,9,256,256]{3,2,1,0:T(8,128)(2,1)} %bitcast.28), channel_id=1, source_target_pairs={{0,1},{1,0},{2,3},{3,2},{4,5},{5,4},{6,7},{7,6},{8,9},{9,8},{10,11... | collective-permute-start | bytes 14155784 | tf_op jit(solution)/shard_map/ppermute | solution.py:293
  106.8 40.2 %all-to-all-start.2 = ((bf16[4,96,2048]{2,1,0:T(8,128)(2,1)}), bf16[4,96,2048]{2,1,0:T(8,128)(2,1)S(1)}, u32[]{:S(2)}, u32[]{:S(2)}) async-start(bf16[4,96,2048]{2,1,0:T(8,128)(2,1)} %bitcast.48), calls=%async_computation.2 | async-start | bytes 3145728 | tf_op jit(solution)/shard_map/all_to_all | solution.py:255
  111.6 7.1 %copy-start.12 = (bf16[128,2048]{1,0:T(8,128)(2,1)S(1)}, bf16[128,2048]{1,0:T(8,128)(2,1)}, u32[]{:S(2)}) copy-start(bf16[128,2048]{1,0:T(8,128)(2,1)} %copy-done.11) | copy-start | bytes 1572868
  111.6 11.4 %collective-permute-start.1 = (f32[8,128]{1,0:T(8,128)S(1)}, f32[8,128]{1,0:T(8,128)S(1)}, u32[]{:S(2)}, u32[]{:S(2)}) collective-permute-start(f32[8,128]{1,0:T(8,128)S(1)} %copy-done.25), channel_id=1, source_target_pairs={{0,64},{64,128},{128,192},{192,0},{1,65},{65,129},{129,193},{193,1... | collective-permute-start | bytes 12296 | tf_op jit(solution)/shard_map/ppermute | solution.py:282
  113.9 15.7 %collective-permute-start.7 = (bf16[64,2048]{1,0:T(8,128)(2,1)S(1)}, bf16[64,2048]{1,0:T(8,128)(2,1)S(1)}, u32[]{:S(2)}, u32[]{:S(2)}) collective-permute-start(bf16[64,2048]{1,0:T(8,128)(2,1)S(1)} %slice.20), channel_id=1, source_target_pairs={{0,192},{64,0},{128,64},{192,128},{1,193},{65,1},{129,65},{193,129... | collective-permute-start | bytes 786440 | tf_op jit(solution)/shard_map/ppermute | solution.py:289
  117.8 20.1 %collective-permute-start.6 = (bf16[64,2048]{1,0:T(8,128)(2,1)S(1)}, bf16[64,2048]{1,0:T(8,128)(2,1)S(1)}, u32[]{:S(2)}, u32[]{:S(2)}) collective-permute-start(bf16[64,2048]{1,0:T(8,128)(2,1)S(1)} %slice.19), channel_id=1, source_target_pairs={{0,64},{64,128},{128,192},{192,0},{1,65},{65,129},{129,193},{193,1... | collective-permute-start | bytes 786440 | tf_op jit(solution)/shard_map/ppermute | solution.py:289
  118.8 19.6 %collective-permute-start.11 = (bf16[64,2048]{1,0:T(8,128)(2,1)S(1)}, bf16[64,2048]{1,0:T(8,128)(2,1)S(1)}, u32[]{:S(2)}, u32[]{:S(2)}) collective-permute-start(bf16[64,2048]{1,0:T(8,128)(2,1)S(1)} %slice.23), channel_id=1, source_target_pairs={{0,192},{64,0},{128,64},{192,128},{1,193},{65,1},{129,65},{193,129... | collective-permute-start | bytes 786440 | tf_op jit(solution)/shard_map/ppermute | solution.py:289
  123.0 20.4 %collective-permute-start.10 = (bf16[64,2048]{1,0:T(8,128)(2,1)S(1)}, bf16[64,2048]{1,0:T(8,128)(2,1)S(1)}, u32[]{:S(2)}, u32[]{:S(2)}) collective-permute-start(bf16[64,2048]{1,0:T(8,128)(2,1)S(1)} %slice.22), channel_id=1, source_target_pairs={{0,64},{64,128},{128,192},{192,0},{1,65},{65,129},{129,193},{193,1... | collective-permute-start | bytes 786440 | tf_op jit(solution)/shard_map/ppermute | solution.py:289
  129.6 13.8 %copy-start.18 = (bf16[64,2048]{1,0:T(8,128)(2,1)}, bf16[64,2048]{1,0:T(8,128)(2,1)S(1)}, u32[]{:S(2)}) copy-start(bf16[64,2048]{1,0:T(8,128)(2,1)S(1)} %collective-permute-done.7.refs_1_) | copy-start | bytes 786436
  147.0 8.3 %collective-permute-start.13 = (bf16[4,9,256,256]{3,2,1,0:T(8,128)(2,1)}, bf16[4,9,256,256]{3,2,1,0:T(8,128)(2,1)}, u32[]{:S(2)}, u32[]{:S(2)}) collective-permute-start(bf16[4,9,256,256]{3,2,1,0:T(8,128)(2,1)} %bitcast.35), channel_id=1, source_target_pairs={{0,1},{1,0},{2,3},{3,2},{4,5},{5,4},{6,7},{7,6},{8,9},{9,8},{10,11... | collective-permute-start | bytes 14155784 | tf_op jit(solution)/shard_map/ppermute | solution.py:299
  148.2 24.3 %all-to-all-start.3 = ((bf16[4,48,4096]{2,1,0:T(8,128)(2,1)}), bf16[4,48,4096]{2,1,0:T(8,128)(2,1)S(1)}, u32[]{:S(2)}, u32[]{:S(2)}) async-start(bf16[4,48,4096]{2,1,0:T(8,128)(2,1)} %bitcast.49), calls=%async_computation.3 | async-start | bytes 3145728 | tf_op jit(solution)/shard_map/all_to_all | solution.py:255
  173.6 24.3 %all-to-all-start.4 = ((bf16[4,96,2048]{2,1,0:T(8,128)(2,1)}), bf16[4,96,2048]{2,1,0:T(8,128)(2,1)S(1)}, u32[]{:S(2)}, u32[]{:S(2)}) async-start(bf16[4,96,2048]{2,1,0:T(8,128)(2,1)} %bitcast.55), calls=%async_computation.4 | async-start | bytes 3145728 | tf_op jit(solution)/shard_map/all_to_all | solution.py:255
  199.2 34.3 %all-to-all-start.5 = ((bf16[4,96,2048]{2,1,0:T(8,128)(2,1)}), bf16[4,96,2048]{2,1,0:T(8,128)(2,1)S(1)}, u32[]{:S(2)}, u32[]{:S(2)}) async-start(bf16[4,96,2048]{2,1,0:T(8,128)(2,1)} %bitcast.54), calls=%async_computation.5 | async-start | bytes 3145728 | tf_op jit(solution)/shard_map/all_to_all | solution.py:255
  207.2 22.6 %collective-permute-start.14 = (bf16[128,2048]{1,0:T(8,128)(2,1)}, bf16[128,2048]{1,0:T(8,128)(2,1)S(1)}, u32[]{:S(2)}, u32[]{:S(2)}) collective-permute-start(bf16[128,2048]{1,0:T(8,128)(2,1)} %get-tuple-element.85), channel_id=1, source_target_pairs={{0,192},{64,0},{128,64},{192,128},{1,193},{65,1},{129,65},{193,129... | collective-permute-start | bytes 1572872 | tf_op jit(solution)/shard_map/ppermute | solution.py:311
  207.2 26.2 %collective-permute-start.15 = (bf16[128,2048]{1,0:T(8,128)(2,1)}, bf16[128,2048]{1,0:T(8,128)(2,1)}, u32[]{:S(2)}, u32[]{:S(2)}) collective-permute-start(bf16[128,2048]{1,0:T(8,128)(2,1)} %get-tuple-element.86), channel_id=1, source_target_pairs={{0,64},{64,128},{128,192},{192,0},{1,65},{65,129},{129,193},{193,1... | collective-permute-start | bytes 1572872 | tf_op jit(solution)/shard_map/ppermute | solution.py:311
  234.6 20.7 %all-to-all-start.6 = ((bf16[4,48,4096]{2,1,0:T(8,128)(2,1)}), bf16[4,48,4096]{2,1,0:T(8,128)(2,1)S(1)}, u32[]{:S(2)}, u32[]{:S(2)}) async-start(bf16[4,48,4096]{2,1,0:T(8,128)(2,1)} %bitcast.23), calls=%async_computation.6 | async-start | bytes 3145728 | tf_op jit(solution)/shard_map/all_to_all | solution.py:255
  242.5 22.4 %collective-permute-start.16 = (bf16[128,2048]{1,0:T(8,128)(2,1)}, bf16[128,2048]{1,0:T(8,128)(2,1)S(1)}, u32[]{:S(2)}, u32[]{:S(2)}) collective-permute-start(bf16[128,2048]{1,0:T(8,128)(2,1)} %get-tuple-element.90), channel_id=1, source_target_pairs={{0,192},{64,0},{128,64},{192,128},{1,193},{65,1},{129,65},{193,129... | collective-permute-start | bytes 1572872 | tf_op jit(solution)/shard_map/ppermute | solution.py:311
  243.3 23.5 %collective-permute-start.17 = (bf16[128,2048]{1,0:T(8,128)(2,1)}, bf16[128,2048]{1,0:T(8,128)(2,1)S(1)}, u32[]{:S(2)}, u32[]{:S(2)}) collective-permute-start(bf16[128,2048]{1,0:T(8,128)(2,1)} %get-tuple-element.91), channel_id=1, source_target_pairs={{0,64},{64,128},{128,192},{192,0},{1,65},{65,129},{129,193},{193,1... | collective-permute-start | bytes 1572872 | tf_op jit(solution)/shard_map/ppermute | solution.py:311
  267.6 56.1 %all-to-all-start.7 = ((bf16[4,48,4096]{2,1,0:T(8,128)(2,1)}), bf16[4,48,4096]{2,1,0:T(8,128)(2,1)S(1)}, u32[]{:S(2)}, u32[]{:S(2)}) async-start(bf16[4,48,4096]{2,1,0:T(8,128)(2,1)} %bitcast.25), calls=%async_computation.7 | async-start | bytes 3145728 | tf_op jit(solution)/shard_map/all_to_all | solution.py:255
  272.4 51.3 %collective-permute-start.18 = (bf16[128,4096]{1,0:T(8,128)(2,1)S(1)}, bf16[128,4096]{1,0:T(8,128)(2,1)}, u32[]{:S(2)}, u32[]{:S(2)}) collective-permute-start(bf16[128,4096]{1,0:T(8,128)(2,1)S(1)} %copy-done.14), channel_id=1, source_target_pairs={{0,128},{64,192},{128,0},{192,64},{1,129},{65,193},{129,1},{193,65... | collective-permute-start | bytes 3145736 | tf_op jit(solution)/shard_map/ppermute | solution.py:322
  (26 other events, 66.0 us)
Sparse Core Ops, SparseCore 0:
  9.4 57.4 all-gather.4
  68.7 55.5 all-gather.6

commit v7 on v4

--- a/solution.py
+++ b/solution.py
@@ -216,18 +216,27 @@
     above_ref[half:, :] = (above[half:] + bottom_ref[...].astype(F32)).astype(BF)
 
 
+def pair_kernel(high_ref, low_ref, rows_ref, below_ref, above_ref):
+    below_ref[...] = weighted(high_ref, low_ref, 0, rows_ref).astype(BF)
+    above_ref[...] = weighted(high_ref, low_ref, 1, rows_ref).astype(BF)
+
+
+def single_kernel(high_ref, low_ref, rows_ref, out_ref):
+    out_ref[...] = weighted(high_ref, low_ref, 0, rows_ref).astype(BF)
+
+
 def last_kernel(high_ref, low_ref, rows_ref, *refs):
-    left, right, out_ref = refs[0:2], refs[2:4], refs[4]
+    left, right, out_ref = refs[0:3], refs[3:5], refs[5]
     total = weighted(high_ref, low_ref, 0, rows_ref)
-    first = pl.program_id(0) < pl.num_programs(0) // 2
+    first = pl.program_id(0) == 0
 
     @pl.when(first)
     def _():
-        out_ref[...] = (total + left[0][...].astype(F32) + left[1][...].astype(F32)).astype(BF)
+        out_ref[...] = sum([ref[...].astype(F32) for ref in left], total).astype(BF)
 
     @pl.when(jnp.logical_not(first))
     def _():
-        out_ref[...] = (total + right[0][...].astype(F32) + right[1][...].astype(F32)).astype(BF)
+        out_ref[...] = sum([ref[...].astype(F32) for ref in right], total).astype(BF)
 
 
 def combine(kernel, plans, rows, first, steps, more, counts):
@@ -272,10 +281,10 @@
     mine = lax.all_gather(pack, "x")
     own = plan(group, slots, meta)
     arrived_own = over_y(gather(own[0], tokens), (-1, model))
-    near, near_metas, swapped, arrived_own = barrier((near, near_metas, swapped, arrived_own))
+    sides = plan(group, slots, *near_metas)
+    near, sides, swapped, arrived_own = barrier((near, sides, swapped, arrived_own))
     other = lax.all_gather(swapped, "x")
 
-    sides = plan(group, slots, *near_metas)
     arrived_sides = over_y(gather(sides[0], *near), (-1, model))
     far = [lax.ppermute(near[0][:half], "zh", ring(1)), lax.ppermute(near[1][half:], "zh", ring(3))]
     far_meta = lax.ppermute(near_metas[0], "zh", ring(1))
@@ -290,28 +299,26 @@
     made_sides = expert(place, arrived_sides, packs, 2)
     made_sides, arrived_across = barrier((made_sides, arrived_across))
     (made,) = expert(place, arrived_across, packs, 1)
-
+    made, arrived_own = barrier((made, arrived_own))
+    (made_own,) = expert(place, arrived_own, packs, 1)
+
+    left = over_y(made_sides[0], (YS, 2, slots, TILE))
+    left, made = barrier((left, made))
     back = over_y(made, (YS, 1, slots, model))
-    pieces = range(model // TILE)
-    parts = [combine(split_kernel, across, back, p, 1, [], (half, half)) for p in pieces]
-    passed = [
-        [lax.ppermute(top, "zh", ring(3)), lax.ppermute(bottom, "zh", ring(1))] for top, bottom in parts
-    ]
-    arrived_own, parts = barrier((arrived_own, parts))
-    (made_own,) = expert(place, arrived_own, packs, 1)
-    home, rows = [], made_sides[0]
-    for p in pieces:
-        rows, back = barrier((rows, back))
-        back = over_y(rows, (YS, 2, slots, TILE))
-        if p == 0:
-            rows, passed[0], made_own = barrier((made_sides[1], passed[0], made_own))
-            back, passed[1] = barrier((back, passed[1]))
-        below, above = combine(add_kernel, sides, back, 0, 1, passed[p], (tok_rows, tok_rows))
-        if p == 1:
-            made_own, home, below, above = barrier((made_own, home, below, above))
-        home = home + [lax.ppermute(below, "zh", ring(3)), lax.ppermute(above, "zh", ring(1))]
+    below, above = combine(pair_kernel, sides, left, 0, 1, [], (tok_rows, tok_rows))
+    home = [lax.ppermute(below, "zh", ring(3)), lax.ppermute(above, "zh", ring(1))]
+    back, made_own = barrier((back, made_own))
+    top, bottom = combine(split_kernel, across, back, 1, 1, [], (half, half))
+    (straight,) = combine(single_kernel, across, back, 0, 1, [], (tok_rows,))
+    rows, top, bottom, straight, home = barrier((made_sides[1], top, bottom, straight, home))
+    passed = [lax.ppermute(top, "zh", ring(3)), lax.ppermute(bottom, "zh", ring(1))]
+    straight = lax.ppermute(straight, "zh", ring(2))
+    right = over_y(rows, (YS, 2, slots, TILE))
+    below, above = combine(add_kernel, sides, right, 0, 1, passed, (tok_rows, tok_rows))
+    made_own, below, above, straight = barrier((made_own, below, above, straight))
+    home = home + [straight, lax.ppermute(below, "zh", ring(3)), lax.ppermute(above, "zh", ring(1))]
     back = over_y(made_own, (YS, 1, slots, model))
-    return combine(last_kernel, own, back, 0, len(pieces), home, (tok_rows,))[0]
+    return combine(last_kernel, own, back, 0, 2, home, (tok_rows,))[0]
 
 
 def solution(mesh):

time: 317 us -> 324 us (1.022)
  waiting for transfers between devices: 127 us -> 156 us
  blocking collectives: 25.7 us -> 0 us
    ppermute x2 -> x1, waiting for transfers between devices: 1.19 us -> 32.4 us  [on_device(): lax.ppermute(top, 'zh', ring(3))]
    all_to_all x1 -> x0, blocking collectives: 25.7 us -> none  [over_y(): lax.all_to_all(rows.reshape(YS, -1, rows.shape[-1]), 'y', split_axis=0, c...]
    all_to_all x6 -> x7, waiting for transfers between devices: 12.9 us -> 6.14 us  [over_y(): lax.all_to_all(rows.reshape(YS, -1, rows.shape[-1]), 'y', split_axis=0, c...]
    ppermute x2 -> x1, starting transfers between devices: 7.39 us -> 1.6 us  [on_device(): lax.ppermute(top, 'zh', ring(3))]
    ppermute x2, waiting for transfers between devices: 18.2 us -> 24 us  [on_device(): lax.ppermute(below, 'zh', ring(3))]
    ppermute x2, starting transfers between devices: 12.2 us -> 6.99 us  [on_device(): lax.ppermute(below, 'zh', ring(3))]
    ppermute x0 -> x1, starting transfers between devices: none -> 4.86 us  [on_device(): straight = lax.ppermute(straight, 'zh', ring(2))]
    all_to_all x6 -> x7, starting transfers between devices: 29.6 us -> 34.3 us  [over_y(): lax.all_to_all(rows.reshape(YS, -1, rows.shape[-1]), 'y', split_axis=0, c...]
  transfers between devices with their start and end apart: 26 -> 26, of which waited for: 10 -> 10; matrix products, arithmetic and copies ran while one was open for 1% -> 1% of each run, Pallas kernels for 18% -> 22%
where the time goes in v7:
time: 324 us; the launch traced here: 321 us
  waiting for transfers between devices  156 us (48%)
  Pallas kernels  75.9 us (23%)
  starting transfers between devices  62.5 us (19%)
  between operations  13.5 us (4%)
  local copies, waits for them, and re-layouts  12.3 us (4%)
    ppermute x2, waiting for transfers between devices, on_device(): near_metas = [lax.ppermute(meta, 'zh', ring(k)) for k in (1, 3)]  58.3 us
    pallas_call x3, Pallas kernels, expert(): pl.pallas_call(expert_kernel, grid_spec=pltpu.PrefetchScalarGridSpec(num_...  44.4 us
    all_to_all x7, starting transfers between devices, over_y(): lax.all_to_all(rows.reshape(YS, -1, rows.shape[-1]), 'y', split_axis=0, c...  34.3 us
    ppermute x1, waiting for transfers between devices, on_device(): lax.ppermute(top, 'zh', ring(3))  32.4 us
    ppermute x2, waiting for transfers between devices, on_device(): lax.ppermute(below, 'zh', ring(3))  24 us
    ppermute x1, waiting for transfers between devices, on_device(): far_meta = lax.ppermute(near_metas[0], 'zh', ring(1))  23.9 us
    pallas_call x5, Pallas kernels, combine(): pl.pallas_call(kernel, grid=(steps,), out_shape=[jax.ShapeDtypeStruct((n,...  15.2 us
    unnamed x52, local copies, waits for them, and re-layouts  10 us
  transfers between devices with their start and end apart: 26, of which 10 were waited for; matrix products, arithmetic and copies ran while one was open for 1% of the time, Pallas kernels for 22%

profile of v7, /device:TPU:10, one launch (start us, length us, event | category | flops | bytes accessed | tf_op | source)
XLA Modules:
  0.0 321.2 jit_solution(3564671841216095651)
XLA Ops:
  6.5 2.7 pack.1
  13.4 2.7 gather.3
  16.1 5.0 %all-to-all-start = ((bf16[4,48,4096]{2,1,0:T(8,128)(2,1)}), bf16[4,48,4096]{2,1,0:T(8,128)(2,1)S(1)}, u32[]{:S(2)}, u32[]{:S(2)}) async-start(bf16[4,48,4096]{2,1,0:T(8,128)(2,1)} %bitcast.49), calls=%async_computation | async-start | bytes 3145728 | tf_op jit(solution)/shard_map/all_to_all | solution.py:262
  21.1 3.3 %collective-permute-start.2 = (bf16[128,4096]{1,0:T(8,128)(2,1)}, bf16[128,4096]{1,0:T(8,128)(2,1)S(1)}, u32[]{:S(2)}, u32[]{:S(2)}) collective-permute-start(bf16[128,4096]{1,0:T(8,128)(2,1)} %refs_0_.1), channel_id=1, source_target_pairs={{0,64},{64,128},{128,192},{192,0},{1,65},{65,129},{129,193},{193,1... | collective-permute-start | bytes 3145736 | tf_op jit(solution)/shard_map/ppermute | solution.py:278
  26.5 2.9 collective-permute-start.4
  29.5 21.0 %collective-permute-done.4.refs_1_ = f32[8,128]{1,0:T(8,128)S(1)} collective-permute-done((f32[8,128]{1,0:T(8,128)S(1)}, f32[8,128]{1,0:T(8,128)S(1)}, u32[]{:S(2)}, u32[]{:S(2)}) %collective-permute-start.4) | collective-permute-done | bytes 4128 | tf_op jit(solution)/shard_map/ppermute | solution.py:279
  50.5 37.2 %collective-permute-done.refs_0_ = f32[8,128]{1,0:T(8,128)S(1)} collective-permute-done((f32[8,128]{1,0:T(8,128)S(1)}, f32[8,128]{1,0:T(8,128)S(1)}, u32[]{:S(2)}, u32[]{:S(2)}) %collective-permute-start) | collective-permute-done | bytes 4128 | tf_op jit(solution)/shard_map/ppermute | solution.py:279
  90.9 3.7 %gather.5 = bf16[4,2,48,4096]{3,2,1,0:T(8,128)(2,1)} custom-call(bf16[2,192,128]{2,1,0:T(8,128)(2,1)} %get-tuple-element.60.pick_ref, bf16[128,4096]{1,0:T(8,128)(2,1)} %copy-done.6, bf16[128,4096]{1,0:T(8,128)(2,1)} %collective-permute-done.3.refs_1_), custom_call_target="tpu_custom_call" | custom-call | tf_op jit(solution)/shard_map/gather/pallas_call | solution.py:106
  94.6 4.9 %all-to-all-start.1 = ((bf16[4,96,4096]{2,1,0:T(8,128)(2,1)}), bf16[4,96,4096]{2,1,0:T(8,128)(2,1)S(1)}, u32[]{:S(2)}, u32[]{:S(2)}) async-start(bf16[4,96,4096]{2,1,0:T(8,128)(2,1)} %bitcast.42), calls=%async_computation.1 | async-start | bytes 6291456 | tf_op jit(solution)/shard_map/all_to_all | solution.py:262
  104.8 23.9 %collective-permute-done.1.refs_0_ = f32[8,128]{1,0:T(8,128)S(1)} collective-permute-done((f32[8,128]{1,0:T(8,128)S(1)}, f32[8,128]{1,0:T(8,128)S(1)}, u32[]{:S(2)}, u32[]{:S(2)}) %collective-permute-start.1) | collective-permute-done | bytes 4128 | tf_op jit(solution)/shard_map/ppermute | solution.py:290
  131.8 2.7 gather.4
  134.7 8.2 %all-gather.7.cloned.1.call-done = bf16[36,256,256]{2,1,0:T(8,128)(2,1)} async-done(((bf16[9,256,256]{2,1,0:T(8,128)(2,1)}), bf16[36,256,256]{2,1,0:T(8,128)(2,1)}) %all-gather.7.cloned.1.call-update) | async-done | bytes 4718608 | tf_op jit(solution)/shard_map/all_gather | solution.py:286
  143.0 4.9 %all-to-all-start.2 = ((bf16[4,48,4096]{2,1,0:T(8,128)(2,1)}), bf16[4,48,4096]{2,1,0:T(8,128)(2,1)}, u32[]{:S(2)}, u32[]{:S(2)}) async-start(bf16[4,48,4096]{2,1,0:T(8,128)(2,1)} %bitcast.48), calls=%async_computation.2 | async-start | bytes 3145728 | tf_op jit(solution)/shard_map/all_to_all | solution.py:262
  148.4 2.8 collective-permute-done.9.refs_3_.refs_7_
  151.2 17.1 %expert.3 = (bf16[384,2048]{1,0:T(8,128)(2,1)}, bf16[384,2048]{1,0:T(8,128)(2,1)}) custom-call(s32[4]{0:T(128)} %pad_add_fusion.place_ref, bf16[384,4096]{1,0:T(8,128)(2,1)} %bitcast.43, bf16[4,9,256,256]{3,2,1,0:T(8,128)(2,1)} %bitcast.27, bf16[4,9,256,256]{3,2,1,0:T(8,128)(2,1)} %collective-permute-done.8.refs_1_.refs_5_, ...), custom_call_target="tpu_custom_call" | custom-call | tf_op jit(solution)/shard_map/expert/pallas_call | solution.py:163
  168.3 4.9 %all-to-all-start.3 = ((bf16[4,96,2048]{2,1,0:T(8,128)(2,1)}), bf16[4,96,2048]{2,1,0:T(8,128)(2,1)S(1)}, u32[]{:S(2)}, u32[]{:S(2)}) async-start(bf16[4,96,2048]{2,1,0:T(8,128)(2,1)} %bitcast.51), calls=%async_computation.3 | async-start | bytes 3145728 | tf_op jit(solution)/shard_map/all_to_all | solution.py:262
  173.1 13.7 %expert.4 = bf16[192,4096]{1,0:T(8,128)(2,1)} custom-call(s32[4]{0:T(128)} %pad_add_fusion.place_ref, bf16[192,4096]{1,0:T(8,128)(2,1)} %bitcast.16.x_ref, bf16[4,9,256,256]{3,2,1,0:T(8,128)(2,1)} %bitcast.29, bf16[4,9,256,256]{3,2,1,0:T(8,128)(2,1)} %collective-permute-done.8.refs_1_.refs_5_, bf16[4,9,256,256]{3,2,1,0:T(8,128)(2,1)} %bitcast.36, ...), custom_call_target="tpu_custom_call" | custom-call | tf_op jit(solution)/shard_map/expert/pallas_call | solution.py:163
  186.8 5.9 %all-to-all-done.3 = bf16[4,96,2048]{2,1,0:T(8,128)(2,1)S(1)} async-done(((bf16[4,96,2048]{2,1,0:T(8,128)(2,1)}), bf16[4,96,2048]{2,1,0:T(8,128)(2,1)S(1)}, u32[]{:S(2)}, u32[]{:S(2)}) %all-to-all-start.3) | async-done | bytes 1572896 | tf_op jit(solution)/shard_map/all_to_all | solution.py:262
  193.8 5.0 %all-to-all-start.4 = ((bf16[4,48,4096]{2,1,0:T(8,128)(2,1)}), bf16[4,48,4096]{2,1,0:T(8,128)(2,1)S(1)}, u32[]{:S(2)}, u32[]{:S(2)}) async-start(bf16[4,48,4096]{2,1,0:T(8,128)(2,1)} %bitcast.45), calls=%async_computation.4 | async-start | bytes 3145728 | tf_op jit(solution)/shard_map/all_to_all | solution.py:262
  198.8 3.0 combine.7
  201.9 4.1 %collective-permute-start.10 = (bf16[128,2048]{1,0:T(8,128)(2,1)}, bf16[128,2048]{1,0:T(8,128)(2,1)S(1)}, u32[]{:S(2)}, u32[]{:S(2)}) collective-permute-start(bf16[128,2048]{1,0:T(8,128)(2,1)} %get-tuple-element.83), channel_id=1, source_target_pairs={{0,192},{64,0},{128,64},{192,128},{1,193},{65,1},{129,65},{193,129... | collective-permute-start | bytes 1572872 | tf_op jit(solution)/shard_map/ppermute | solution.py:309
  206.0 13.7 %expert.5 = bf16[192,4096]{1,0:T(8,128)(2,1)} custom-call(s32[4]{0:T(128)} %pad_add_fusion.place_ref, bf16[192,4096]{1,0:T(8,128)(2,1)} %bitcast.44, bf16[4,9,256,256]{3,2,1,0:T(8,128)(2,1)} %bitcast.31, bf16[4,9,256,256]{3,2,1,0:T(8,128)(2,1)} %collective-permute-done.8.refs_1_.refs_5_, bf16[4,9,256,256]{3,2,1,0:T(8,128)(2,1)} %bitcast.38, ...), custom_call_target="tpu_custom_call" | custom-call | tf_op jit(solution)/shard_map/expert/pallas_call | solution.py:163
  220.8 2.5 combine.6
  223.3 2.4 combine.5
  228.6 4.8 %all-to-all-start.5 = ((bf16[4,96,2048]{2,1,0:T(8,128)(2,1)}), bf16[4,96,2048]{2,1,0:T(8,128)(2,1)S(1)}, u32[]{:S(2)}, u32[]{:S(2)}) async-start(bf16[4,96,2048]{2,1,0:T(8,128)(2,1)} %bitcast.21), calls=%async_computation.5 | async-start | bytes 3145728 | tf_op jit(solution)/shard_map/all_to_all | solution.py:262
  233.4 4.9 %collective-permute-start.14 = (bf16[128,2048]{1,0:T(8,128)(2,1)S(1)}, bf16[128,2048]{1,0:T(8,128)(2,1)S(1)}, u32[]{:S(2)}, u32[]{:S(2)}) collective-permute-start(bf16[128,2048]{1,0:T(8,128)(2,1)S(1)} %copy-done.7), channel_id=1, source_target_pairs={{0,128},{64,192},{128,0},{192,64},{1,129},{65,193},{129,1},{193,65... | collective-permute-start | bytes 1572872 | tf_op jit(solution)/shard_map/ppermute | solution.py:315
  241.2 32.4 %collective-permute-done.12.top_ref = bf16[64,2048]{1,0:T(8,128)(2,1)S(1)} collective-permute-done((bf16[64,2048]{1,0:T(8,128)(2,1)}, bf16[64,2048]{1,0:T(8,128)(2,1)S(1)}, u32[]{:S(2)}, u32[]{:S(2)}) %collective-permute-start.12) | collective-permute-done | bytes 262176 | tf_op jit(solution)/shard_map/ppermute | solution.py:314
  275.0 3.1 combine.8
  278.9 4.8 %all-to-all-start.6 = ((bf16[4,48,4096]{2,1,0:T(8,128)(2,1)}), bf16[4,48,4096]{2,1,0:T(8,128)(2,1)S(1)}, u32[]{:S(2)}, u32[]{:S(2)}) async-start(bf16[4,48,4096]{2,1,0:T(8,128)(2,1)} %bitcast.23), calls=%async_computation.6 | async-start | bytes 3145728 | tf_op jit(solution)/shard_map/all_to_all | solution.py:262
  283.7 2.9 collective-permute-start.15
  286.7 22.1 %collective-permute-done.15.refs_3_ = bf16[128,2048]{1,0:T(8,128)(2,1)S(1)} collective-permute-done((bf16[128,2048]{1,0:T(8,128)(2,1)}, bf16[128,2048]{1,0:T(8,128)(2,1)S(1)}, u32[]{:S(2)}, u32[]{:S(2)}) %collective-permute-start.15) | collective-permute-done | bytes 524320 | tf_op jit(solution)/shard_map/ppermute | solution.py:319
  310.3 4.1 %combine.9 = bf16[128,4096]{1,0:T(8,128)(2,1)} custom-call(bf16[1,192,128]{2,1,0:T(8,128)(2,1)} %get-tuple-element.51.high_ref, bf16[1,192,128]{2,1,0:T(8,128)(2,1)} %get-tuple-element.52.low_ref, bf16[4,1,48,4096]{3,2,1,0:T(8,128)(2,1)} %bitcast.50, bf16[128,2048]{1,0:T(8,128)(2,1)} %copy-done.10, bf16[128,2048]{1,0:T(8,128)(2,1)} %copy-done.11, ...), custom_call_target="tpu_custom_call" | custom-call | tf_op jit(solution)/shard_map/combine/pallas_call | solution.py:245
  (94 shorter events, 30.5 us)
Async XLA Ops:
  6.5 128.2 %all-gather.5.cloned.1.call-start = ((), (), s32[]{:S(2)}) async-start(), calls=%async_computation.7 | async-start | bytes 5898240 | tf_op jit(solution)/shard_map/all_gather | solution.py:281
  9.3 80.6 %collective-permute-start.5 = (bf16[9,256,256]{2,1,0:T(8,128)(2,1)}, bf16[9,256,256]{2,1,0:T(8,128)(2,1)}, u32[]{:S(2)}, u32[]{:S(2)}) collective-permute-start(bf16[9,256,256]{2,1,0:T(8,128)(2,1)} %pack.1), channel_id=1, source_target_pairs={{0,2},{2,0},{1,3},{3,1},{4,6},{6,4},{5,7},{7,5},{8,10},{10,8},{9,1... | collective-permute-start | bytes 3538952 | tf_op jit(solution)/shard_map/ppermute | solution.py:280
  16.1 10.5 %copy-start.17 = (f32[8,128]{1,0:T(8,128)S(1)}, f32[8,128]{1,0:T(8,128)}, u32[]{:S(2)}) copy-start(f32[8,128]{1,0:T(8,128)} %pad_maximum_fusion.refs_0_) | copy-start | bytes 12292
  16.1 73.8 %all-to-all-start = ((bf16[4,48,4096]{2,1,0:T(8,128)(2,1)}), bf16[4,48,4096]{2,1,0:T(8,128)(2,1)S(1)}, u32[]{:S(2)}, u32[]{:S(2)}) async-start(bf16[4,48,4096]{2,1,0:T(8,128)(2,1)} %bitcast.49), calls=%async_computation | async-start | bytes 3145728 | tf_op jit(solution)/shard_map/all_to_all | solution.py:262
  21.1 121.8 %all-gather.7.cloned.1.call-start = ((), (), s32[]{:S(2)}) async-start(), calls=%async_computation.8 | async-start | bytes 5898240 | tf_op jit(solution)/shard_map/all_gather | solution.py:286
  21.1 68.8 %collective-permute-start.2 = (bf16[128,4096]{1,0:T(8,128)(2,1)}, bf16[128,4096]{1,0:T(8,128)(2,1)S(1)}, u32[]{:S(2)}, u32[]{:S(2)}) collective-permute-start(bf16[128,4096]{1,0:T(8,128)(2,1)} %refs_0_.1), channel_id=1, source_target_pairs={{0,64},{64,128},{128,192},{192,0},{1,65},{65,129},{129,193},{193,1... | collective-permute-start | bytes 3145736 | tf_op jit(solution)/shard_map/ppermute | solution.py:278
  24.4 65.5 %collective-permute-start.3 = (bf16[128,4096]{1,0:T(8,128)(2,1)}, bf16[128,4096]{1,0:T(8,128)(2,1)}, u32[]{:S(2)}, u32[]{:S(2)}) collective-permute-start(bf16[128,4096]{1,0:T(8,128)(2,1)} %refs_0_.1), channel_id=1, source_target_pairs={{0,192},{64,0},{128,64},{192,128},{1,193},{65,1},{129,65},{193,129... | collective-permute-start | bytes 3145736 | tf_op jit(solution)/shard_map/ppermute | solution.py:278
  26.5 24.0 %collective-permute-start.4 = (f32[8,128]{1,0:T(8,128)S(1)}, f32[8,128]{1,0:T(8,128)S(1)}, u32[]{:S(2)}, u32[]{:S(2)}) collective-permute-start(f32[8,128]{1,0:T(8,128)S(1)} %copy-done.17), channel_id=1, source_target_pairs={{0,192},{64,0},{128,64},{192,128},{1,193},{65,1},{129,65},{193,129... | collective-permute-start | bytes 12296 | tf_op jit(solution)/shard_map/ppermute | solution.py:279
  29.5 58.3 %collective-permute-start = (f32[8,128]{1,0:T(8,128)S(1)}, f32[8,128]{1,0:T(8,128)S(1)}, u32[]{:S(2)}, u32[]{:S(2)}) collective-permute-start(f32[8,128]{1,0:T(8,128)S(1)} %copy-done.17), channel_id=1, source_target_pairs={{0,64},{64,128},{128,192},{192,0},{1,65},{65,129},{129,193},{193,1... | collective-permute-start | bytes 12296 | tf_op jit(solution)/shard_map/ppermute | solution.py:279
  50.5 37.2 %copy-start.21 = (f32[8,128]{1,0:T(8,128)}, f32[8,128]{1,0:T(8,128)S(1)}, u32[]{:S(2)}) copy-start(f32[8,128]{1,0:T(8,128)S(1)} %collective-permute-done.4.refs_1_) | copy-start | bytes 12292
  94.6 40.1 %all-to-all-start.1 = ((bf16[4,96,4096]{2,1,0:T(8,128)(2,1)}), bf16[4,96,4096]{2,1,0:T(8,128)(2,1)S(1)}, u32[]{:S(2)}, u32[]{:S(2)}) async-start(bf16[4,96,4096]{2,1,0:T(8,128)(2,1)} %bitcast.42), calls=%async_computation.1 | async-start | bytes 6291456 | tf_op jit(solution)/shard_map/all_to_all | solution.py:262
  101.8 29.1 %collective-permute-start.7 = (bf16[64,4096]{1,0:T(8,128)(2,1)S(1)}, bf16[64,4096]{1,0:T(8,128)(2,1)S(1)}, u32[]{:S(2)}, u32[]{:S(2)}) collective-permute-start(bf16[64,4096]{1,0:T(8,128)(2,1)S(1)} %slice.7), channel_id=1, source_target_pairs={{0,192},{64,0},{128,64},{192,128},{1,193},{65,1},{129,65},{193,129... | collective-permute-start | bytes 1572872 | tf_op jit(solution)/shard_map/ppermute | solution.py:289
  103.2 27.7 %collective-permute-start.6 = (bf16[64,4096]{1,0:T(8,128)(2,1)S(1)}, bf16[64,4096]{1,0:T(8,128)(2,1)S(1)}, u32[]{:S(2)}, u32[]{:S(2)}) collective-permute-start(bf16[64,4096]{1,0:T(8,128)(2,1)S(1)} %slice.6), channel_id=1, source_target_pairs={{0,64},{64,128},{128,192},{192,0},{1,65},{65,129},{129,193},{193,1... | collective-permute-start | bytes 1572872 | tf_op jit(solution)/shard_map/ppermute | solution.py:289
  104.8 24.0 %collective-permute-start.1 = (f32[8,128]{1,0:T(8,128)S(1)}, f32[8,128]{1,0:T(8,128)S(1)}, u32[]{:S(2)}, u32[]{:S(2)}) collective-permute-start(f32[8,128]{1,0:T(8,128)S(1)} %copy-done.20), channel_id=1, source_target_pairs={{0,64},{64,128},{128,192},{192,0},{1,65},{65,129},{129,193},{193,1... | collective-permute-start | bytes 12296 | tf_op jit(solution)/shard_map/ppermute | solution.py:290
  134.7 8.2 %copy-start.1 = (bf16[4,96,4096]{2,1,0:T(8,128)(2,1)}, bf16[4,96,4096]{2,1,0:T(8,128)(2,1)S(1)}, u32[]{:S(2)}) copy-start(bf16[4,96,4096]{2,1,0:T(8,128)(2,1)S(1)} %all-to-all-done.1) | copy-start | bytes 9437188
  134.7 13.7 %collective-permute-start.8 = (bf16[4,9,256,256]{3,2,1,0:T(8,128)(2,1)}, bf16[4,9,256,256]{3,2,1,0:T(8,128)(2,1)}, u32[]{:S(2)}, u32[]{:S(2)}) collective-permute-start(bf16[4,9,256,256]{3,2,1,0:T(8,128)(2,1)} %bitcast.26), channel_id=1, source_target_pairs={{0,1},{1,0},{2,3},{3,2},{4,5},{5,4},{6,7},{7,6},{8,9},{9,8},{10,11... | collective-permute-start | bytes 14155784 | tf_op jit(solution)/shard_map/ppermute | solution.py:293
  142.9 8.3 %collective-permute-start.9 = (bf16[4,9,256,256]{3,2,1,0:T(8,128)(2,1)}, bf16[4,9,256,256]{3,2,1,0:T(8,128)(2,1)}, u32[]{:S(2)}, u32[]{:S(2)}) collective-permute-start(bf16[4,9,256,256]{3,2,1,0:T(8,128)(2,1)} %bitcast.33), channel_id=1, source_target_pairs={{0,1},{1,0},{2,3},{3,2},{4,5},{5,4},{6,7},{7,6},{8,9},{9,8},{10,11... | collective-permute-start | bytes 14155784 | tf_op jit(solution)/shard_map/ppermute | solution.py:295
  143.0 25.3 %all-to-all-start.2 = ((bf16[4,48,4096]{2,1,0:T(8,128)(2,1)}), bf16[4,48,4096]{2,1,0:T(8,128)(2,1)}, u32[]{:S(2)}, u32[]{:S(2)}) async-start(bf16[4,48,4096]{2,1,0:T(8,128)(2,1)} %bitcast.48), calls=%async_computation.2 | async-start | bytes 3145728 | tf_op jit(solution)/shard_map/all_to_all | solution.py:262
  168.3 24.4 %all-to-all-start.3 = ((bf16[4,96,2048]{2,1,0:T(8,128)(2,1)}), bf16[4,96,2048]{2,1,0:T(8,128)(2,1)S(1)}, u32[]{:S(2)}, u32[]{:S(2)}) async-start(bf16[4,96,2048]{2,1,0:T(8,128)(2,1)} %bitcast.51), calls=%async_computation.3 | async-start | bytes 3145728 | tf_op jit(solution)/shard_map/all_to_all | solution.py:262
  193.8 25.8 %all-to-all-start.4 = ((bf16[4,48,4096]{2,1,0:T(8,128)(2,1)}), bf16[4,48,4096]{2,1,0:T(8,128)(2,1)S(1)}, u32[]{:S(2)}, u32[]{:S(2)}) async-start(bf16[4,48,4096]{2,1,0:T(8,128)(2,1)} %bitcast.45), calls=%async_computation.4 | async-start | bytes 3145728 | tf_op jit(solution)/shard_map/all_to_all | solution.py:262
  201.9 25.7 %collective-permute-start.10 = (bf16[128,2048]{1,0:T(8,128)(2,1)}, bf16[128,2048]{1,0:T(8,128)(2,1)S(1)}, u32[]{:S(2)}, u32[]{:S(2)}) collective-permute-start(bf16[128,2048]{1,0:T(8,128)(2,1)} %get-tuple-element.83), channel_id=1, source_target_pairs={{0,192},{64,0},{128,64},{192,128},{1,193},{65,1},{129,65},{193,129... | collective-permute-start | bytes 1572872 | tf_op jit(solution)/shard_map/ppermute | solution.py:309
  206.0 21.6 %collective-permute-start.11 = (bf16[128,2048]{1,0:T(8,128)(2,1)}, bf16[128,2048]{1,0:T(8,128)(2,1)S(1)}, u32[]{:S(2)}, u32[]{:S(2)}) collective-permute-start(bf16[128,2048]{1,0:T(8,128)(2,1)} %get-tuple-element.84), channel_id=1, source_target_pairs={{0,64},{64,128},{128,192},{192,0},{1,65},{65,129},{129,193},{193,1... | collective-permute-start | bytes 1572872 | tf_op jit(solution)/shard_map/ppermute | solution.py:309
  227.6 5.8 %copy-start.7 = (bf16[128,2048]{1,0:T(8,128)(2,1)S(1)}, bf16[128,2048]{1,0:T(8,128)(2,1)}, u32[]{:S(2)}) copy-start(bf16[128,2048]{1,0:T(8,128)(2,1)} %combine.6) | copy-start | bytes 1572868
  227.6 12.3 %copy-start.25 = (bf16[64,2048]{1,0:T(8,128)(2,1)S(1)}, bf16[64,2048]{1,0:T(8,128)(2,1)}, u32[]{:S(2)}) copy-start(bf16[64,2048]{1,0:T(8,128)(2,1)} %get-tuple-element.87) | copy-start | bytes 786436
  228.6 45.0 %all-to-all-start.5 = ((bf16[4,96,2048]{2,1,0:T(8,128)(2,1)}), bf16[4,96,2048]{2,1,0:T(8,128)(2,1)S(1)}, u32[]{:S(2)}, u32[]{:S(2)}) async-start(bf16[4,96,2048]{2,1,0:T(8,128)(2,1)} %bitcast.21), calls=%async_computation.5 | async-start | bytes 3145728 | tf_op jit(solution)/shard_map/all_to_all | solution.py:262
  233.4 44.7 %collective-permute-start.14 = (bf16[128,2048]{1,0:T(8,128)(2,1)S(1)}, bf16[128,2048]{1,0:T(8,128)(2,1)S(1)}, u32[]{:S(2)}, u32[]{:S(2)}) collective-permute-start(bf16[128,2048]{1,0:T(8,128)(2,1)S(1)} %copy-done.7), channel_id=1, source_target_pairs={{0,128},{64,192},{128,0},{192,64},{1,129},{65,193},{129,1},{193,65... | collective-permute-start | bytes 1572872 | tf_op jit(solution)/shard_map/ppermute | solution.py:315
  238.3 35.4 %collective-permute-start.12 = (bf16[64,2048]{1,0:T(8,128)(2,1)}, bf16[64,2048]{1,0:T(8,128)(2,1)S(1)}, u32[]{:S(2)}, u32[]{:S(2)}) collective-permute-start(bf16[64,2048]{1,0:T(8,128)(2,1)} %get-tuple-element.86), channel_id=1, source_target_pairs={{0,192},{64,0},{128,64},{192,128},{1,193},{65,1},{129,65},{193,129... | collective-permute-start | bytes 786440 | tf_op jit(solution)/shard_map/ppermute | solution.py:314
  239.9 33.8 %collective-permute-start.13 = (bf16[64,2048]{1,0:T(8,128)(2,1)S(1)}, bf16[64,2048]{1,0:T(8,128)(2,1)S(1)}, u32[]{:S(2)}, u32[]{:S(2)}) collective-permute-start(bf16[64,2048]{1,0:T(8,128)(2,1)S(1)} %copy-done.25), channel_id=1, source_target_pairs={{0,64},{64,128},{128,192},{192,0},{1,65},{65,129},{129,193},{193,1... | collective-permute-start | bytes 786440 | tf_op jit(solution)/shard_map/ppermute | solution.py:314
  278.1 8.5 %copy-start.24 = (bf16[128,2048]{1,0:T(8,128)(2,1)S(1)}, bf16[128,2048]{1,0:T(8,128)(2,1)}, u32[]{:S(2)}) copy-start(bf16[128,2048]{1,0:T(8,128)(2,1)} %get-tuple-element.96) | copy-start | bytes 1572868
  278.9 29.9 %all-to-all-start.6 = ((bf16[4,48,4096]{2,1,0:T(8,128)(2,1)}), bf16[4,48,4096]{2,1,0:T(8,128)(2,1)S(1)}, u32[]{:S(2)}, u32[]{:S(2)}) async-start(bf16[4,48,4096]{2,1,0:T(8,128)(2,1)} %bitcast.23), calls=%async_computation.6 | async-start | bytes 3145728 | tf_op jit(solution)/shard_map/all_to_all | solution.py:262
  283.7 25.1 %collective-permute-start.15 = (bf16[128,2048]{1,0:T(8,128)(2,1)}, bf16[128,2048]{1,0:T(8,128)(2,1)S(1)}, u32[]{:S(2)}, u32[]{:S(2)}) collective-permute-start(bf16[128,2048]{1,0:T(8,128)(2,1)} %get-tuple-element.95), channel_id=1, source_target_pairs={{0,192},{64,0},{128,64},{192,128},{1,193},{65,1},{129,65},{193,129... | collective-permute-start | bytes 1572872 | tf_op jit(solution)/shard_map/ppermute | solution.py:319
  286.6 22.2 %collective-permute-start.16 = (bf16[128,2048]{1,0:T(8,128)(2,1)S(1)}, bf16[128,2048]{1,0:T(8,128)(2,1)S(1)}, u32[]{:S(2)}, u32[]{:S(2)}) collective-permute-start(bf16[128,2048]{1,0:T(8,128)(2,1)S(1)} %copy-done.24), channel_id=1, source_target_pairs={{0,64},{64,128},{128,192},{192,0},{1,65},{65,129},{129,193},{193,1... | collective-permute-start | bytes 1572872 | tf_op jit(solution)/shard_map/ppermute | solution.py:319
  (20 other events, 34.5 us)
Sparse Core Ops, SparseCore 0:
  9.4 57.4 all-gather.4
  90.1 52.8 all-gather.6

commit v8 on v4

--- a/solution.py
+++ b/solution.py
@@ -266,20 +266,22 @@
     pack = pack_shards(w_gate_up[0], w_down[0])
     meta = jnp.concatenate([route_ids.astype(F32).T, gate_values.T], axis=0)
 
-    near = [lax.ppermute(tokens, "zh", ring(k)) for k in (1, 3)]
     near_metas = [lax.ppermute(meta, "zh", ring(k)) for k in (1, 3)]
+    far_meta = lax.ppermute(meta, "zh", ring(2))
     swapped = lax.ppermute(pack, "zl", swap)
     mine = lax.all_gather(pack, "x")
     own = plan(group, slots, meta)
-    arrived_own = over_y(gather(own[0], tokens), (-1, model))
-    near, near_metas, swapped, arrived_own = barrier((near, near_metas, swapped, arrived_own))
+    sent = gather(own[0], tokens)
+    sides = plan(group, slots, *near_metas)
+    across = plan(group, slots, far_meta)
+    swapped, sent, sides, across, moved = barrier((swapped, sent, sides, across, tokens))
     other = lax.all_gather(swapped, "x")
-
-    sides = plan(group, slots, *near_metas)
+    arrived_own = over_y(sent, (-1, model))
+    near = [lax.ppermute(moved, "zh", ring(k)) for k in (1, 3)]
+    near, arrived_own = barrier((near, arrived_own))
+
     arrived_sides = over_y(gather(sides[0], *near), (-1, model))
     far = [lax.ppermute(near[0][:half], "zh", ring(1)), lax.ppermute(near[1][half:], "zh", ring(3))]
-    far_meta = lax.ppermute(near_metas[0], "zh", ring(1))
-    across = plan(group, slots, far_meta)
     sent, mine, arrived_sides = barrier((gather(across[0], *far), mine, arrived_sides))
     mine_swapped = lax.ppermute(mine, "core", swap)
     arrived_across = over_y(sent, (-1, model))

time: 317 us -> 325 us (1.025)
  waiting for transfers between devices: 127 us -> 134 us
  local copies, waits for them, and re-layouts: 9.15 us -> 12.4 us
    ppermute x2, waiting for transfers between devices: 58.3 us -> 0.01 us  [on_device(): near_metas = [lax.ppermute(meta, 'zh', ring(k)) for k in (1, 3)]]
    ppermute x3, waiting for transfers between devices: 23.9 us -> 61.7 us  [the longest x2 42.7 us: on_device(): near = [lax.ppermute(moved, 'zh', ring(k)) for k in (1, 3)]]
    ppermute x1, waiting for transfers between devices: 0.01 us -> 21.3 us  [on_device(): lax.ppermute(near[1][half:], 'zh', ring(3))]
    ppermute x2, starting transfers between devices: 12.2 us -> 1.02 us  [on_device(): lax.ppermute(below, 'zh', ring(3))]
    all_gather x1, waiting for transfers between devices: 6.48 us -> 0.02 us  [on_device(): other = lax.all_gather(swapped, 'x')]
    ppermute x2, waiting for transfers between devices: 18.2 us -> 24.6 us  [on_device(): lax.ppermute(below, 'zh', ring(3))]
    all_to_all x6, waiting for transfers between devices: 12.9 us -> 7.11 us  [over_y(): lax.all_to_all(rows.reshape(YS, -1, rows.shape[-1]), 'y', split_axis=0, c...]
    ppermute x2, starting transfers between devices: 0.01 us -> 4.83 us  [on_device(): lax.ppermute(above, 'zh', ring(1))]
  transfers between devices with their start and end apart: 26 -> 26, of which waited for: 10 -> 14; matrix products, arithmetic and copies ran while one was open for 1% -> 1% of each run, Pallas kernels for 18% -> 17%
where the time goes in v8:
time: 325 us; the launch traced here: 323 us
  waiting for transfers between devices  134 us (41%)
  Pallas kernels  75.7 us (23%)
  starting transfers between devices  61.2 us (19%)
  blocking collectives  25.7 us (8%)
  between operations  13.5 us (4%)
  local copies, waits for them, and re-layouts  12.4 us (4%)
    pallas_call x3, Pallas kernels, expert(): pl.pallas_call(expert_kernel, grid_spec=pltpu.PrefetchScalarGridSpec(num_...  44.4 us
    ppermute x2, waiting for transfers between devices, on_device(): near = [lax.ppermute(moved, 'zh', ring(k)) for k in (1, 3)]  42.7 us
    all_to_all x6, starting transfers between devices, over_y(): lax.all_to_all(rows.reshape(YS, -1, rows.shape[-1]), 'y', split_axis=0, c...  30.1 us
    all_to_all x1, blocking collectives, over_y(): lax.all_to_all(rows.reshape(YS, -1, rows.shape[-1]), 'y', split_axis=0, c...  25.7 us
    ppermute x2, waiting for transfers between devices, on_device(): lax.ppermute(below, 'zh', ring(3))  24.6 us
    ppermute x1, waiting for transfers between devices, on_device(): lax.ppermute(near[1][half:], 'zh', ring(3))  21.3 us
    ppermute x1, waiting for transfers between devices, on_device(): far_meta = lax.ppermute(meta, 'zh', ring(2))  19 us
    pallas_call x5, Pallas kernels, combine(): pl.pallas_call(kernel, grid=(steps,), out_shape=[jax.ShapeDtypeStruct((n,...  15 us
  transfers between devices with their start and end apart: 26, of which 14 were waited for; matrix products, arithmetic and copies ran while one was open for 1% of the time, Pallas kernels for 17%

profile of v8, /device:TPU:10, one launch (start us, length us, event | category | flops | bytes accessed | tf_op | source)
XLA Modules:
  0.0 323.2 jit_solution(11757158453810637282)
XLA Ops:
  6.5 2.7 pack.1
  11.4 6.4 %collective-permute-start.3 = (f32[8,128]{1,0:T(8,128)S(1)}, f32[8,128]{1,0:T(8,128)S(1)}, u32[]{:S(2)}, u32[]{:S(2)}) collective-permute-start(f32[8,128]{1,0:T(8,128)S(1)} %pad_maximum_fusion.refs_0_), channel_id=1, source_target_pairs={{0,128},{64,192},{128,0},{192,64},{1,129},{65,193},{129,1},{193,65... | collective-permute-start | bytes 12296 | tf_op jit(solution)/shard_map/ppermute | solution.py:270
  22.2 2.7 gather.3
  24.8 19.0 %collective-permute-done.3.refs_0_ = f32[8,128]{1,0:T(8,128)S(1)} collective-permute-done((f32[8,128]{1,0:T(8,128)S(1)}, f32[8,128]{1,0:T(8,128)S(1)}, u32[]{:S(2)}, u32[]{:S(2)}) %collective-permute-start.3) | collective-permute-done | bytes 4128 | tf_op jit(solution)/shard_map/ppermute | solution.py:270
  49.7 4.9 %all-to-all-start = ((bf16[4,48,4096]{2,1,0:T(8,128)(2,1)}), bf16[4,48,4096]{2,1,0:T(8,128)(2,1)S(1)}, u32[]{:S(2)}, u32[]{:S(2)}) async-start(bf16[4,48,4096]{2,1,0:T(8,128)(2,1)} %bitcast.49), calls=%async_computation | async-start | bytes 3145728 | tf_op jit(solution)/shard_map/all_to_all | solution.py:253
  57.6 42.7 %collective-permute-done.5.refs_1_ = bf16[128,4096]{1,0:T(8,128)(2,1)S(1)} collective-permute-done((bf16[128,4096]{1,0:T(8,128)(2,1)}, bf16[128,4096]{1,0:T(8,128)(2,1)S(1)}, u32[]{:S(2)}, u32[]{:S(2)}) %collective-permute-start.5) | collective-permute-done | bytes 1048608 | tf_op jit(solution)/shard_map/ppermute | solution.py:280
  101.3 3.7 %gather.5 = bf16[4,2,48,4096]{3,2,1,0:T(8,128)(2,1)} custom-call(bf16[2,192,128]{2,1,0:T(8,128)(2,1)} %get-tuple-element.71.pick_ref, bf16[128,4096]{1,0:T(8,128)(2,1)} %collective-permute-done.4.refs_0_, bf16[128,4096]{1,0:T(8,128)(2,1)} %copy-done.5), custom_call_target="tpu_custom_call" | custom-call | tf_op jit(solution)/shard_map/gather/pallas_call | solution.py:106
  104.9 4.8 %all-to-all-start.1 = ((bf16[4,96,4096]{2,1,0:T(8,128)(2,1)}), bf16[4,96,4096]{2,1,0:T(8,128)(2,1)S(1)}, u32[]{:S(2)}, u32[]{:S(2)}) async-start(bf16[4,96,4096]{2,1,0:T(8,128)(2,1)} %bitcast.42), calls=%async_computation.1 | async-start | bytes 6291456 | tf_op jit(solution)/shard_map/all_to_all | solution.py:253
  111.9 2.9 collective-permute-start.7
  114.9 21.3 %collective-permute-done.7.refs_1_ = bf16[64,4096]{1,0:T(8,128)(2,1)S(1)} collective-permute-done((bf16[64,4096]{1,0:T(8,128)(2,1)S(1)}, bf16[64,4096]{1,0:T(8,128)(2,1)S(1)}, u32[]{:S(2)}, u32[]{:S(2)}) %collective-permute-start.7) | collective-permute-done | bytes 524320 | tf_op jit(solution)/shard_map/ppermute | solution.py:284
  136.3 4.3 %collective-permute-done.6.refs_0_ = bf16[64,4096]{1,0:T(8,128)(2,1)S(1)} collective-permute-done((bf16[64,4096]{1,0:T(8,128)(2,1)S(1)}, bf16[64,4096]{1,0:T(8,128)(2,1)S(1)}, u32[]{:S(2)}, u32[]{:S(2)}) %collective-permute-start.6) | collective-permute-done | bytes 524320 | tf_op jit(solution)/shard_map/ppermute | solution.py:284
  141.3 2.6 gather.4
  146.6 5.8 %all-to-all-start.2 = ((bf16[4,48,4096]{2,1,0:T(8,128)(2,1)}), bf16[4,48,4096]{2,1,0:T(8,128)(2,1)}, u32[]{:S(2)}, u32[]{:S(2)}) async-start(bf16[4,48,4096]{2,1,0:T(8,128)(2,1)} %bitcast.48), calls=%async_computation.2 | async-start | bytes 3145728 | tf_op jit(solution)/shard_map/all_to_all | solution.py:253
  153.2 6.7 %collective-permute-done.9.refs_3_.refs_7_ = bf16[4,9,256,256]{3,2,1,0:T(8,128)(2,1)} collective-permute-done((bf16[4,9,256,256]{3,2,1,0:T(8,128)(2,1)}, bf16[4,9,256,256]{3,2,1,0:T(8,128)(2,1)}, u32[]{:S(2)}, u32[]{:S(2)}) %collective-permute-start.9) | collective-permute-done | bytes 4718624 | tf_op jit(solution)/shard_map/ppermute | solution.py:288
  159.9 17.1 %expert.3 = (bf16[384,2048]{1,0:T(8,128)(2,1)}, bf16[384,2048]{1,0:T(8,128)(2,1)}) custom-call(s32[4]{0:T(128)} %pad_add_fusion.place_ref, bf16[384,4096]{1,0:T(8,128)(2,1)} %bitcast.43, bf16[4,9,256,256]{3,2,1,0:T(8,128)(2,1)} %bitcast.27, bf16[4,9,256,256]{3,2,1,0:T(8,128)(2,1)} %collective-permute-done.8.refs_1_.refs_5_, ...), custom_call_target="tpu_custom_call" | custom-call | tf_op jit(solution)/shard_map/expert/pallas_call | solution.py:163
  177.0 13.7 %expert.4 = bf16[192,4096]{1,0:T(8,128)(2,1)} custom-call(s32[4]{0:T(128)} %pad_add_fusion.place_ref, bf16[192,4096]{1,0:T(8,128)(2,1)} %bitcast.16.x_ref, bf16[4,9,256,256]{3,2,1,0:T(8,128)(2,1)} %bitcast.29, bf16[4,9,256,256]{3,2,1,0:T(8,128)(2,1)} %collective-permute-done.8.refs_1_.refs_5_, bf16[4,9,256,256]{3,2,1,0:T(8,128)(2,1)} %bitcast.36, ...), custom_call_target="tpu_custom_call" | custom-call | tf_op jit(solution)/shard_map/expert/pallas_call | solution.py:163
  190.7 25.7 %all_to_all.35 = bf16[4,48,4096]{2,1,0:T(8,128)(2,1)} all-to-all(bf16[4,48,4096]{2,1,0:T(8,128)(2,1)} %bitcast.45), channel_id=1, replica_groups=mesh['zh'=4,'y'=4,'x'=4,'zl'=2,'core'=2] {'y'}, dimensions={0} | all-to-all | bytes 3145728 | tf_op jit(solution)/shard_map/all_to_all | solution.py:253
  216.4 5.0 %all-to-all-start.4 = ((bf16[4,96,2048]{2,1,0:T(8,128)(2,1)}), bf16[4,96,2048]{2,1,0:T(8,128)(2,1)S(1)}, u32[]{:S(2)}, u32[]{:S(2)}) async-start(bf16[4,96,2048]{2,1,0:T(8,128)(2,1)} %bitcast.19), calls=%async_computation.4 | async-start | bytes 3145728 | tf_op jit(solution)/shard_map/all_to_all | solution.py:253
  223.8 3.3 %collective-permute-start.10 = (bf16[64,2048]{1,0:T(8,128)(2,1)}, bf16[64,2048]{1,0:T(8,128)(2,1)S(1)}, u32[]{:S(2)}, u32[]{:S(2)}) collective-permute-start(bf16[64,2048]{1,0:T(8,128)(2,1)} %get-tuple-element.82), channel_id=1, source_target_pairs={{0,192},{64,0},{128,64},{192,128},{1,193},{65,1},{129,65},{193,129... | collective-permute-start | bytes 786440 | tf_op jit(solution)/shard_map/ppermute | solution.py:300
  227.1 2.5 combine.6
  229.6 4.1 %collective-permute-start.12 = (bf16[64,2048]{1,0:T(8,128)(2,1)}, bf16[64,2048]{1,0:T(8,128)(2,1)S(1)}, u32[]{:S(2)}, u32[]{:S(2)}) collective-permute-start(bf16[64,2048]{1,0:T(8,128)(2,1)} %get-tuple-element.85), channel_id=1, source_target_pairs={{0,192},{64,0},{128,64},{192,128},{1,193},{65,1},{129,65},{193,129... | collective-permute-start | bytes 786440 | tf_op jit(solution)/shard_map/ppermute | solution.py:300
  233.7 13.7 %expert.5 = bf16[192,4096]{1,0:T(8,128)(2,1)} custom-call(s32[4]{0:T(128)} %pad_add_fusion.place_ref, bf16[192,4096]{1,0:T(8,128)(2,1)} %bitcast.44, bf16[4,9,256,256]{3,2,1,0:T(8,128)(2,1)} %bitcast.31, bf16[4,9,256,256]{3,2,1,0:T(8,128)(2,1)} %collective-permute-done.8.refs_1_.refs_5_, bf16[4,9,256,256]{3,2,1,0:T(8,128)(2,1)} %bitcast.38, ...), custom_call_target="tpu_custom_call" | custom-call | tf_op jit(solution)/shard_map/expert/pallas_call | solution.py:163
  249.3 3.9 %collective-permute-done.13.bottom_ref = bf16[64,2048]{1,0:T(8,128)(2,1)S(1)} collective-permute-done((bf16[64,2048]{1,0:T(8,128)(2,1)}, bf16[64,2048]{1,0:T(8,128)(2,1)S(1)}, u32[]{:S(2)}, u32[]{:S(2)}) %collective-permute-start.13) | collective-permute-done | bytes 262176 | tf_op jit(solution)/shard_map/ppermute | solution.py:300
  254.5 4.8 %all-to-all-start.5 = ((bf16[4,96,2048]{2,1,0:T(8,128)(2,1)}), bf16[4,96,2048]{2,1,0:T(8,128)(2,1)S(1)}, u32[]{:S(2)}, u32[]{:S(2)}) async-start(bf16[4,96,2048]{2,1,0:T(8,128)(2,1)} %bitcast.51), calls=%async_computation.5 | async-start | bytes 3145728 | tf_op jit(solution)/shard_map/all_to_all | solution.py:253
  259.3 3.1 combine.7
  265.3 6.2 %all-to-all-done.5 = bf16[4,96,2048]{2,1,0:T(8,128)(2,1)S(1)} async-done(((bf16[4,96,2048]{2,1,0:T(8,128)(2,1)}), bf16[4,96,2048]{2,1,0:T(8,128)(2,1)S(1)}, u32[]{:S(2)}, u32[]{:S(2)}) %all-to-all-start.5) | async-done | bytes 1572896 | tf_op jit(solution)/shard_map/all_to_all | solution.py:253
  272.7 3.1 combine.8
  275.8 8.6 %collective-permute-done.14.refs_0_ = bf16[128,2048]{1,0:T(8,128)(2,1)S(1)} collective-permute-done((bf16[128,2048]{1,0:T(8,128)(2,1)}, bf16[128,2048]{1,0:T(8,128)(2,1)S(1)}, u32[]{:S(2)}, u32[]{:S(2)}) %collective-permute-start.14) | collective-permute-done | bytes 524320 | tf_op jit(solution)/shard_map/ppermute | solution.py:314
  286.4 4.8 %all-to-all-start.6 = ((bf16[4,48,4096]{2,1,0:T(8,128)(2,1)}), bf16[4,48,4096]{2,1,0:T(8,128)(2,1)S(1)}, u32[]{:S(2)}, u32[]{:S(2)}) async-start(bf16[4,48,4096]{2,1,0:T(8,128)(2,1)} %bitcast.23), calls=%async_computation.6 | async-start | bytes 3145728 | tf_op jit(solution)/shard_map/all_to_all | solution.py:253
  291.6 2.6 collective-permute-start.17
  294.1 15.9 %collective-permute-done.16.refs_2_ = bf16[128,2048]{1,0:T(8,128)(2,1)S(1)} collective-permute-done((bf16[128,2048]{1,0:T(8,128)(2,1)}, bf16[128,2048]{1,0:T(8,128)(2,1)S(1)}, u32[]{:S(2)}, u32[]{:S(2)}) %collective-permute-start.16) | collective-permute-done | bytes 524320 | tf_op jit(solution)/shard_map/ppermute | solution.py:314
  312.5 3.8 %combine.9 = bf16[128,4096]{1,0:T(8,128)(2,1)} custom-call(bf16[1,192,128]{2,1,0:T(8,128)(2,1)} %get-tuple-element.57.high_ref, bf16[1,192,128]{2,1,0:T(8,128)(2,1)} %get-tuple-element.58.low_ref, bf16[4,1,48,4096]{3,2,1,0:T(8,128)(2,1)} %bitcast.50, bf16[128,2048]{1,0:T(8,128)(2,1)} %copy-done.7, bf16[128,2048]{1,0:T(8,128)(2,1)} %copy-done.8, ...), custom_call_target="tpu_custom_call" | custom-call | tf_op jit(solution)/shard_map/combine/pallas_call | solution.py:236
  (91 shorter events, 37.2 us)
Async XLA Ops:
  6.5 138.4 %all-gather.5.cloned.1.call-start = ((), (), s32[]{:S(2)}) async-start(), calls=%async_computation.7 | async-start | bytes 5898240 | tf_op jit(solution)/shard_map/all_gather | solution.py:272
  6.5 4.8 %copy-start.21 = (s32[128,4]{0,1:T(4,128)S(1)}, s32[128,4]{0,1:T(4,128)}, u32[]{:S(2)}) copy-start(s32[128,4]{0,1:T(4,128)} %param.6) | copy-start | bytes 6148
  6.5 4.8 %copy-start.22 = (f32[128,4]{0,1:T(4,128)S(1)}, f32[128,4]{0,1:T(4,128)}, u32[]{:S(2)}) copy-start(f32[128,4]{0,1:T(4,128)} %param.7) | copy-start | bytes 6148
  9.3 135.6 %all-gather.7.cloned.1.call-start = ((), (), s32[]{:S(2)}) async-start(), calls=%async_computation.8 | async-start | bytes 5898240 | tf_op jit(solution)/shard_map/all_gather | solution.py:278
  9.3 39.3 %collective-permute-start = (bf16[9,256,256]{2,1,0:T(8,128)(2,1)}, bf16[9,256,256]{2,1,0:T(8,128)(2,1)S(1)}, u32[]{:S(2)}, u32[]{:S(2)}) collective-permute-start(bf16[9,256,256]{2,1,0:T(8,128)(2,1)} %pack.1), channel_id=1, source_target_pairs={{0,2},{2,0},{1,3},{3,1},{4,6},{6,4},{5,7},{7,5},{8,10},{10,8},{9,1... | collective-permute-start | bytes 3538952 | tf_op jit(solution)/shard_map/ppermute | solution.py:271
  11.4 9.3 %copy-start.17 = (f32[8,128]{1,0:T(8,128)}, f32[8,128]{1,0:T(8,128)S(1)}, u32[]{:S(2)}) copy-start(f32[8,128]{1,0:T(8,128)S(1)} %pad_maximum_fusion.refs_0_) | copy-start | bytes 12292
  11.4 32.4 %collective-permute-start.3 = (f32[8,128]{1,0:T(8,128)S(1)}, f32[8,128]{1,0:T(8,128)S(1)}, u32[]{:S(2)}, u32[]{:S(2)}) collective-permute-start(f32[8,128]{1,0:T(8,128)S(1)} %pad_maximum_fusion.refs_0_), channel_id=1, source_target_pairs={{0,128},{64,192},{128,0},{192,64},{1,129},{65,193},{129,1},{193,65... | collective-permute-start | bytes 12296 | tf_op jit(solution)/shard_map/ppermute | solution.py:270
  17.8 28.2 %collective-permute-start.2 = (f32[8,128]{1,0:T(8,128)S(1)}, f32[8,128]{1,0:T(8,128)S(1)}, u32[]{:S(2)}, u32[]{:S(2)}) collective-permute-start(f32[8,128]{1,0:T(8,128)S(1)} %pad_maximum_fusion.refs_0_), channel_id=1, source_target_pairs={{0,192},{64,0},{128,64},{192,128},{1,193},{65,1},{129,65},{193,129... | collective-permute-start | bytes 12296 | tf_op jit(solution)/shard_map/ppermute | solution.py:269
  18.3 27.6 %collective-permute-start.1 = (f32[8,128]{1,0:T(8,128)S(1)}, f32[8,128]{1,0:T(8,128)S(1)}, u32[]{:S(2)}, u32[]{:S(2)}) collective-permute-start(f32[8,128]{1,0:T(8,128)S(1)} %pad_maximum_fusion.refs_0_), channel_id=1, source_target_pairs={{0,64},{64,128},{128,192},{192,0},{1,65},{65,129},{129,193},{193,1... | collective-permute-start | bytes 12296 | tf_op jit(solution)/shard_map/ppermute | solution.py:269
  49.7 50.6 %all-to-all-start = ((bf16[4,48,4096]{2,1,0:T(8,128)(2,1)}), bf16[4,48,4096]{2,1,0:T(8,128)(2,1)S(1)}, u32[]{:S(2)}, u32[]{:S(2)}) async-start(bf16[4,48,4096]{2,1,0:T(8,128)(2,1)} %bitcast.49), calls=%async_computation | async-start | bytes 3145728 | tf_op jit(solution)/shard_map/all_to_all | solution.py:253
  54.7 45.6 %collective-permute-start.5 = (bf16[128,4096]{1,0:T(8,128)(2,1)}, bf16[128,4096]{1,0:T(8,128)(2,1)S(1)}, u32[]{:S(2)}, u32[]{:S(2)}) collective-permute-start(bf16[128,4096]{1,0:T(8,128)(2,1)} %refs_0_.1), channel_id=1, source_target_pairs={{0,192},{64,0},{128,64},{192,128},{1,193},{65,1},{129,65},{193,129... | collective-permute-start | bytes 3145736 | tf_op jit(solution)/shard_map/ppermute | solution.py:280
  55.3 45.0 %collective-permute-start.4 = (bf16[128,4096]{1,0:T(8,128)(2,1)}, bf16[128,4096]{1,0:T(8,128)(2,1)}, u32[]{:S(2)}, u32[]{:S(2)}) collective-permute-start(bf16[128,4096]{1,0:T(8,128)(2,1)} %refs_0_.1), channel_id=1, source_target_pairs={{0,64},{64,128},{128,192},{192,0},{1,65},{65,129},{129,193},{193,1... | collective-permute-start | bytes 3145736 | tf_op jit(solution)/shard_map/ppermute | solution.py:280
  104.9 40.0 %all-to-all-start.1 = ((bf16[4,96,4096]{2,1,0:T(8,128)(2,1)}), bf16[4,96,4096]{2,1,0:T(8,128)(2,1)S(1)}, u32[]{:S(2)}, u32[]{:S(2)}) async-start(bf16[4,96,4096]{2,1,0:T(8,128)(2,1)} %bitcast.42), calls=%async_computation.1 | async-start | bytes 6291456 | tf_op jit(solution)/shard_map/all_to_all | solution.py:253
  111.9 24.3 %collective-permute-start.7 = (bf16[64,4096]{1,0:T(8,128)(2,1)S(1)}, bf16[64,4096]{1,0:T(8,128)(2,1)S(1)}, u32[]{:S(2)}, u32[]{:S(2)}) collective-permute-start(bf16[64,4096]{1,0:T(8,128)(2,1)S(1)} %slice.7), channel_id=1, source_target_pairs={{0,192},{64,0},{128,64},{192,128},{1,193},{65,1},{129,65},{193,129... | collective-permute-start | bytes 1572872 | tf_op jit(solution)/shard_map/ppermute | solution.py:284
  114.8 25.7 %collective-permute-start.6 = (bf16[64,4096]{1,0:T(8,128)(2,1)S(1)}, bf16[64,4096]{1,0:T(8,128)(2,1)S(1)}, u32[]{:S(2)}, u32[]{:S(2)}) collective-permute-start(bf16[64,4096]{1,0:T(8,128)(2,1)S(1)} %slice.6), channel_id=1, source_target_pairs={{0,64},{64,128},{128,192},{192,0},{1,65},{65,129},{129,193},{193,1... | collective-permute-start | bytes 1572872 | tf_op jit(solution)/shard_map/ppermute | solution.py:284
  144.9 8.3 %collective-permute-start.8 = (bf16[4,9,256,256]{3,2,1,0:T(8,128)(2,1)}, bf16[4,9,256,256]{3,2,1,0:T(8,128)(2,1)}, u32[]{:S(2)}, u32[]{:S(2)}) collective-permute-start(bf16[4,9,256,256]{3,2,1,0:T(8,128)(2,1)} %bitcast.26), channel_id=1, source_target_pairs={{0,1},{1,0},{2,3},{3,2},{4,5},{5,4},{6,7},{7,6},{8,9},{9,8},{10,11... | collective-permute-start | bytes 14155784 | tf_op jit(solution)/shard_map/ppermute | solution.py:286
  144.9 15.0 %collective-permute-start.9 = (bf16[4,9,256,256]{3,2,1,0:T(8,128)(2,1)}, bf16[4,9,256,256]{3,2,1,0:T(8,128)(2,1)}, u32[]{:S(2)}, u32[]{:S(2)}) collective-permute-start(bf16[4,9,256,256]{3,2,1,0:T(8,128)(2,1)} %bitcast.33), channel_id=1, source_target_pairs={{0,1},{1,0},{2,3},{3,2},{4,5},{5,4},{6,7},{7,6},{8,9},{9,8},{10,11... | collective-permute-start | bytes 14155784 | tf_op jit(solution)/shard_map/ppermute | solution.py:288
  146.6 30.4 %all-to-all-start.2 = ((bf16[4,48,4096]{2,1,0:T(8,128)(2,1)}), bf16[4,48,4096]{2,1,0:T(8,128)(2,1)}, u32[]{:S(2)}, u32[]{:S(2)}) async-start(bf16[4,48,4096]{2,1,0:T(8,128)(2,1)} %bitcast.48), calls=%async_computation.2 | async-start | bytes 3145728 | tf_op jit(solution)/shard_map/all_to_all | solution.py:253
  216.4 36.9 %all-to-all-start.4 = ((bf16[4,96,2048]{2,1,0:T(8,128)(2,1)}), bf16[4,96,2048]{2,1,0:T(8,128)(2,1)S(1)}, u32[]{:S(2)}, u32[]{:S(2)}) async-start(bf16[4,96,2048]{2,1,0:T(8,128)(2,1)} %bitcast.19), calls=%async_computation.4 | async-start | bytes 3145728 | tf_op jit(solution)/shard_map/all_to_all | solution.py:253
  223.8 23.6 %collective-permute-start.10 = (bf16[64,2048]{1,0:T(8,128)(2,1)}, bf16[64,2048]{1,0:T(8,128)(2,1)S(1)}, u32[]{:S(2)}, u32[]{:S(2)}) collective-permute-start(bf16[64,2048]{1,0:T(8,128)(2,1)} %get-tuple-element.82), channel_id=1, source_target_pairs={{0,192},{64,0},{128,64},{192,128},{1,193},{65,1},{129,65},{193,129... | collective-permute-start | bytes 786440 | tf_op jit(solution)/shard_map/ppermute | solution.py:300
  227.1 20.3 %collective-permute-start.11 = (bf16[64,2048]{1,0:T(8,128)(2,1)}, bf16[64,2048]{1,0:T(8,128)(2,1)S(1)}, u32[]{:S(2)}, u32[]{:S(2)}) collective-permute-start(bf16[64,2048]{1,0:T(8,128)(2,1)} %get-tuple-element.83), channel_id=1, source_target_pairs={{0,64},{64,128},{128,192},{192,0},{1,65},{65,129},{129,193},{193,1... | collective-permute-start | bytes 786440 | tf_op jit(solution)/shard_map/ppermute | solution.py:300
  229.6 19.8 %collective-permute-start.12 = (bf16[64,2048]{1,0:T(8,128)(2,1)}, bf16[64,2048]{1,0:T(8,128)(2,1)S(1)}, u32[]{:S(2)}, u32[]{:S(2)}) collective-permute-start(bf16[64,2048]{1,0:T(8,128)(2,1)} %get-tuple-element.85), channel_id=1, source_target_pairs={{0,192},{64,0},{128,64},{192,128},{1,193},{65,1},{129,65},{193,129... | collective-permute-start | bytes 786440 | tf_op jit(solution)/shard_map/ppermute | solution.py:300
  233.7 19.5 %collective-permute-start.13 = (bf16[64,2048]{1,0:T(8,128)(2,1)}, bf16[64,2048]{1,0:T(8,128)(2,1)S(1)}, u32[]{:S(2)}, u32[]{:S(2)}) collective-permute-start(bf16[64,2048]{1,0:T(8,128)(2,1)} %get-tuple-element.86), channel_id=1, source_target_pairs={{0,64},{64,128},{128,192},{192,0},{1,65},{65,129},{129,193},{193,1... | collective-permute-start | bytes 786440 | tf_op jit(solution)/shard_map/ppermute | solution.py:300
  247.4 5.9 %copy-start.15 = (bf16[64,2048]{1,0:T(8,128)(2,1)}, bf16[64,2048]{1,0:T(8,128)(2,1)S(1)}, u32[]{:S(2)}) copy-start(bf16[64,2048]{1,0:T(8,128)(2,1)S(1)} %collective-permute-done.10.top_ref) | copy-start | bytes 786436
  247.4 5.9 %copy-start.16 = (bf16[64,2048]{1,0:T(8,128)(2,1)}, bf16[64,2048]{1,0:T(8,128)(2,1)S(1)}, u32[]{:S(2)}) copy-start(bf16[64,2048]{1,0:T(8,128)(2,1)S(1)} %collective-permute-done.11.bottom_ref) | copy-start | bytes 786436
  254.5 17.0 %all-to-all-start.5 = ((bf16[4,96,2048]{2,1,0:T(8,128)(2,1)}), bf16[4,96,2048]{2,1,0:T(8,128)(2,1)S(1)}, u32[]{:S(2)}, u32[]{:S(2)}) async-start(bf16[4,96,2048]{2,1,0:T(8,128)(2,1)} %bitcast.51), calls=%async_computation.5 | async-start | bytes 3145728 | tf_op jit(solution)/shard_map/all_to_all | solution.py:253
  262.4 22.0 %collective-permute-start.14 = (bf16[128,2048]{1,0:T(8,128)(2,1)}, bf16[128,2048]{1,0:T(8,128)(2,1)S(1)}, u32[]{:S(2)}, u32[]{:S(2)}) collective-permute-start(bf16[128,2048]{1,0:T(8,128)(2,1)} %get-tuple-element.96), channel_id=1, source_target_pairs={{0,192},{64,0},{128,64},{192,128},{1,193},{65,1},{129,65},{193,129... | collective-permute-start | bytes 1572872 | tf_op jit(solution)/shard_map/ppermute | solution.py:314
  263.1 22.5 %collective-permute-start.15 = (bf16[128,2048]{1,0:T(8,128)(2,1)}, bf16[128,2048]{1,0:T(8,128)(2,1)S(1)}, u32[]{:S(2)}, u32[]{:S(2)}) collective-permute-start(bf16[128,2048]{1,0:T(8,128)(2,1)} %get-tuple-element.97), channel_id=1, source_target_pairs={{0,64},{64,128},{128,192},{192,0},{1,65},{65,129},{129,193},{193,1... | collective-permute-start | bytes 1572872 | tf_op jit(solution)/shard_map/ppermute | solution.py:314
  285.6 6.0 %copy-start.23 = (bf16[128,2048]{1,0:T(8,128)(2,1)S(1)}, bf16[128,2048]{1,0:T(8,128)(2,1)}, u32[]{:S(2)}) copy-start(bf16[128,2048]{1,0:T(8,128)(2,1)} %get-tuple-element.108) | copy-start | bytes 1572868
  286.4 24.7 %all-to-all-start.6 = ((bf16[4,48,4096]{2,1,0:T(8,128)(2,1)}), bf16[4,48,4096]{2,1,0:T(8,128)(2,1)S(1)}, u32[]{:S(2)}, u32[]{:S(2)}) async-start(bf16[4,48,4096]{2,1,0:T(8,128)(2,1)} %bitcast.23), calls=%async_computation.6 | async-start | bytes 3145728 | tf_op jit(solution)/shard_map/all_to_all | solution.py:253
  291.2 18.9 %collective-permute-start.16 = (bf16[128,2048]{1,0:T(8,128)(2,1)}, bf16[128,2048]{1,0:T(8,128)(2,1)S(1)}, u32[]{:S(2)}, u32[]{:S(2)}) collective-permute-start(bf16[128,2048]{1,0:T(8,128)(2,1)} %get-tuple-element.107), channel_id=1, source_target_pairs={{0,192},{64,0},{128,64},{192,128},{1,193},{65,1},{129,65},{193,129... | collective-permute-start | bytes 1572872 | tf_op jit(solution)/shard_map/ppermute | solution.py:314
  291.6 19.6 %collective-permute-start.17 = (bf16[128,2048]{1,0:T(8,128)(2,1)S(1)}, bf16[128,2048]{1,0:T(8,128)(2,1)S(1)}, u32[]{:S(2)}, u32[]{:S(2)}) collective-permute-start(bf16[128,2048]{1,0:T(8,128)(2,1)S(1)} %copy-done.23), channel_id=1, source_target_pairs={{0,64},{64,128},{128,192},{192,0},{1,65},{65,129},{129,193},{193,1... | collective-permute-start | bytes 1572872 | tf_op jit(solution)/shard_map/ppermute | solution.py:314
  (18 other events, 28.1 us)
Sparse Core Ops, SparseCore 0:
  9.4 57.4 all-gather.4
  68.7 55.5 all-gather.6

commit v9 on v4

--- a/solution.py
+++ b/solution.py
@@ -11,6 +11,7 @@
 ZH, YS, XS = 4, 4, 4
 PARAMS = pltpu.CompilerParams(vmem_limit_bytes=56 << 20)
 BLOCK = 256
+AHEAD = 3
 TILE = 2048
 
 
@@ -115,81 +116,100 @@
     )(pick, *blocks)
 
 
-def expert_kernel(place_ref, x_ref, *refs):
-    ins, downs, outs = refs[0:4], refs[4:8], refs[8:-2]
-    sums_ref, hidden_ref = refs[-2:]
-    step = pl.program_id(0)
+def expert_kernel(pieces, place_ref, x_hbm, *refs):
+    packs, outs = refs[:4], refs[4 : 4 + pieces]
+    x_ref, w_ref, sums_ref, hidden_ref, out_ref, x_sem, in_sems, down_sems, out_sems = refs[4 + pieces :]
     parts = sums_ref.shape[0]
     half = parts // 2
-    each = XS // len(outs)
+    wide = 4 * BLOCK
+
+    def copy_in(r, x):
+        return pltpu.make_async_copy(
+            packs[r].at[x, pl.ds(0, parts)], w_ref.at[r, x, pl.ds(0, parts)], in_sems.at[r, x]
+        )
+
+    def copy_down(r, x):
+        return pltpu.make_async_copy(
+            packs[r].at[x, pl.ds(parts, half)], w_ref.at[r, x, pl.ds(parts, half)], down_sems.at[r, x]
+        )
+
+    def copy_out(x):
+        at = x % (XS // pieces) * wide
+        return pltpu.make_async_copy(
+            out_ref.at[:, pl.ds(x * wide, wide)],
+            outs[x // (XS // pieces)].at[:, pl.ds(at, wide)],
+            out_sems.at[x],
+        )
 
     def columns(x, r):
         return pl.ds(pl.multiple_of((x * 4 + place_ref[r]) * BLOCK, BLOCK), BLOCK)
 
-    @pl.when(step == 0)
-    def _():
-        sums_ref[...] = jnp.zeros_like(sums_ref)
-
-    @pl.when(step < XS)
-    def _():
-        rows = [x_ref[:, columns(step, r)] for r in range(4)]
+    rows = pltpu.make_async_copy(x_hbm, x_ref, x_sem)
+    rows.start()
+    order = [(copy, x) for copy in (copy_in, copy_down) for x in range(XS)]
+
+    def start(i):
+        if i < len(order):
+            copy, x = order[i]
+            for r in range(4):
+                copy(r, x).start()
+
+    for i in range(AHEAD):
+        start(i)
+    sums_ref[...] = jnp.zeros_like(sums_ref)
+    rows.wait()
+    for x in range(XS):
+        for r in range(4):
+            copy_in(r, x).wait()
+        start(x + AHEAD)
+        taken = [x_ref[:, columns(x, r)] for r in range(4)]
         for n in range(parts):
             sums_ref[n] += sum(
-                jnp.dot(rows[r], ins[r][n], preferred_element_type=F32) for r in range(4)
+                jnp.dot(taken[r], w_ref[r, x, n], preferred_element_type=F32) for r in range(4)
             )
-
-    @pl.when(step == XS)
-    def _():
-        for n in range(half):
-            g, u = sums_ref[n], sums_ref[half + n]
-            hidden_ref[n] = (g / (1.0 + jnp.exp(-g)) * u).astype(BF)
-
+    for n in range(half):
+        g, u = sums_ref[n], sums_ref[half + n]
+        hidden_ref[n] = (g / (1.0 + jnp.exp(-g)) * u).astype(BF)
     for x in range(XS):
-
-        @pl.when(step == XS + x)
-        def _(x=x):
-            for r in range(4):
-                made = sum(
-                    jnp.dot(hidden_ref[n], downs[r][n], preferred_element_type=F32)
-                    for n in range(half)
-                )
-                outs[x // each][:, columns(x % each, r)] = made.astype(BF)
+        for r in range(4):
+            copy_down(r, x).wait()
+        start(XS + x + AHEAD)
+        for r in range(4):
+            made = sum(
+                jnp.dot(hidden_ref[n], w_ref[r, x, parts + n], preferred_element_type=F32)
+                for n in range(half)
+            )
+            out_ref[:, columns(x, r)] = made.astype(BF)
+        copy_out(x).start()
+    for x in range(XS):
+        copy_out(x).wait()
 
 
 def expert(place, rows, packs, pieces):
     count, width = rows.shape
-    half = packs[0].shape[1] // 3
+    total = packs[0].shape[1]
+    half = total // 3
     out = jax.ShapeDtypeStruct((count, width // pieces), BF)
-    return pl.pallas_call(
-        expert_kernel,
-        grid_spec=pltpu.PrefetchScalarGridSpec(
-            num_scalar_prefetch=1,
-            grid=(2 * XS,),
-            in_specs=[pl.BlockSpec((count, width), lambda s, p: (0, 0))]
-            + [
-                pl.BlockSpec(
-                    (pl.Squeezed(), 2 * half, BLOCK, BLOCK),
-                    lambda s, p: (jnp.minimum(s, XS - 1), 0, 0, 0),
-                )
-            ]
-            * 4
-            + [
-                pl.BlockSpec(
-                    (pl.Squeezed(), half, BLOCK, BLOCK),
-                    lambda s, p: (jnp.maximum(s - XS, 0), 2, 0, 0),
-                )
-            ]
-            * 4,
-            out_specs=[pl.BlockSpec(out.shape, lambda s, p: (0, 0))] * pieces,
-            scratch_shapes=[
-                pltpu.VMEM((2 * half, count, BLOCK), F32),
-                pltpu.VMEM((half, count, BLOCK), BF),
-            ],
-        ),
+    there = pl.BlockSpec(memory_space=pl.ANY)
+    return pl.pallas_call(
+        functools.partial(expert_kernel, pieces),
+        in_specs=[pl.BlockSpec(memory_space=pltpu.SMEM)] + [there] * 5,
+        out_specs=[there] * pieces,
         out_shape=[out] * pieces,
+        scratch_shapes=[
+            pltpu.VMEM((count, width), BF),
+            pltpu.VMEM((4,) + packs[0].shape, BF),
+            pltpu.VMEM((2 * half, count, BLOCK), F32),
+            pltpu.VMEM((half, count, BLOCK), BF),
+            pltpu.VMEM((count, width), BF),
+            pltpu.SemaphoreType.DMA(()),
+            pltpu.SemaphoreType.DMA((4, XS)),
+            pltpu.SemaphoreType.DMA((4, XS)),
+            pltpu.SemaphoreType.DMA((XS,)),
+        ],
         compiler_params=PARAMS,
         name="expert",
-    )(place, rows, *packs, *packs)
+    )(place, rows, *packs)
 
 
 def weighted(high_ref, low_ref, i, rows_ref):

time: 317 us -> 313 us (0.987)
  Pallas kernels: 75.7 us -> 67.6 us
  waiting for transfers between devices: 127 us -> 135 us
    pallas_call x3, Pallas kernels: 44.4 us -> 36.3 us  [expert(): pl.pallas_call(functools.partial(expert_kernel, pieces), in_specs=[pl.Blo...]
    ppermute x2, waiting for transfers between devices: 18.2 us -> 24.5 us  [on_device(): lax.ppermute(below, 'zh', ring(3))]
    ppermute x2, starting transfers between devices: 12.2 us -> 8.91 us  [on_device(): lax.ppermute(below, 'zh', ring(3))]
  transfers between devices with their start and end apart: 26 -> 26, of which waited for: 10 -> 12; matrix products, arithmetic and copies ran while one was open for 1% -> 1% of each run, Pallas kernels for 18% -> 16%
where the time goes in v9:
time: 313 us; the launch traced here: 312 us
  waiting for transfers between devices  135 us (43%)
  Pallas kernels  67.6 us (22%)
  starting transfers between devices  60 us (19%)
  blocking collectives  25.3 us (8%)
  between operations  13.6 us (4%)
  local copies, waits for them, and re-layouts  9.16 us (3%)
    ppermute x2, waiting for transfers between devices, on_device(): near_metas = [lax.ppermute(meta, 'zh', ring(k)) for k in (1, 3)]  58.3 us
    pallas_call x3, Pallas kernels, expert(): pl.pallas_call(functools.partial(expert_kernel, pieces), in_specs=[pl.Blo...  36.3 us
    all_to_all x6, starting transfers between devices, over_y(): lax.all_to_all(rows.reshape(YS, -1, rows.shape[-1]), 'y', split_axis=0, c...  29.4 us
    all_to_all x1, blocking collectives, over_y(): lax.all_to_all(rows.reshape(YS, -1, rows.shape[-1]), 'y', split_axis=0, c...  25.3 us
    ppermute x2, waiting for transfers between devices, on_device(): lax.ppermute(below, 'zh', ring(3))  24.5 us
    ppermute x1, waiting for transfers between devices, on_device(): far_meta = lax.ppermute(near_metas[0], 'zh', ring(1))  23.9 us
    pallas_call x5, Pallas kernels, combine(): pl.pallas_call(kernel, grid=(steps,), out_shape=[jax.ShapeDtypeStruct((n,...  15 us
    all_to_all x6, waiting for transfers between devices, over_y(): lax.all_to_all(rows.reshape(YS, -1, rows.shape[-1]), 'y', split_axis=0, c...  12 us
  transfers between devices with their start and end apart: 26, of which 12 were waited for; matrix products, arithmetic and copies ran while one was open for 1% of the time, Pallas kernels for 16%

profile of v9, /device:TPU:10, one launch (start us, length us, event | category | flops | bytes accessed | tf_op | source)
XLA Modules:
  0.0 312.0 jit_solution(49841446387840540)
XLA Ops:
  6.5 2.7 pack.1
  13.4 2.7 gather.3
  16.0 5.0 %all-to-all-start = ((bf16[4,48,4096]{2,1,0:T(8,128)(2,1)}), bf16[4,48,4096]{2,1,0:T(8,128)(2,1)S(1)}, u32[]{:S(2)}, u32[]{:S(2)}) async-start(bf16[4,48,4096]{2,1,0:T(8,128)(2,1)} %bitcast.43), calls=%async_computation | async-start | bytes 3145728 | tf_op jit(solution)/shard_map/all_to_all | solution.py:273
  21.1 3.3 %collective-permute-start = (bf16[128,4096]{1,0:T(8,128)(2,1)}, bf16[128,4096]{1,0:T(8,128)(2,1)S(1)}, u32[]{:S(2)}, u32[]{:S(2)}) collective-permute-start(bf16[128,4096]{1,0:T(8,128)(2,1)} %refs_0_.1), channel_id=1, source_target_pairs={{0,64},{64,128},{128,192},{192,0},{1,65},{65,129},{129,193},{193,1... | collective-permute-start | bytes 3145736 | tf_op jit(solution)/shard_map/ppermute | solution.py:289
  26.5 2.9 collective-permute-start.3
  29.4 21.0 %collective-permute-done.3.refs_1_ = f32[8,128]{1,0:T(8,128)S(1)} collective-permute-done((f32[8,128]{1,0:T(8,128)S(1)}, f32[8,128]{1,0:T(8,128)S(1)}, u32[]{:S(2)}, u32[]{:S(2)}) %collective-permute-start.3) | collective-permute-done | bytes 4128 | tf_op jit(solution)/shard_map/ppermute | solution.py:290
  50.5 37.2 %collective-permute-done.2.refs_0_ = f32[8,128]{1,0:T(8,128)S(1)} collective-permute-done((f32[8,128]{1,0:T(8,128)S(1)}, f32[8,128]{1,0:T(8,128)S(1)}, u32[]{:S(2)}, u32[]{:S(2)}) %collective-permute-start.2) | collective-permute-done | bytes 4128 | tf_op jit(solution)/shard_map/ppermute | solution.py:290
  89.9 3.7 %gather.5 = bf16[4,2,48,4096]{3,2,1,0:T(8,128)(2,1)} custom-call(bf16[2,192,128]{2,1,0:T(8,128)(2,1)} %get-tuple-element.59.pick_ref, bf16[128,4096]{1,0:T(8,128)(2,1)} %copy-done.5, bf16[128,4096]{1,0:T(8,128)(2,1)} %collective-permute-done.1.refs_1_), custom_call_target="tpu_custom_call" | custom-call | tf_op jit(solution)/shard_map/gather/pallas_call | solution.py:107
  93.6 4.9 %all-to-all-start.1 = ((bf16[4,96,4096]{2,1,0:T(8,128)(2,1)}), bf16[4,96,4096]{2,1,0:T(8,128)(2,1)S(1)}, u32[]{:S(2)}, u32[]{:S(2)}) async-start(bf16[4,96,4096]{2,1,0:T(8,128)(2,1)} %bitcast.37), calls=%async_computation.1 | async-start | bytes 6291456 | tf_op jit(solution)/shard_map/all_to_all | solution.py:273
  103.8 23.9 %collective-permute-done.5.refs_0_ = f32[8,128]{1,0:T(8,128)S(1)} collective-permute-done((f32[8,128]{1,0:T(8,128)S(1)}, f32[8,128]{1,0:T(8,128)S(1)}, u32[]{:S(2)}, u32[]{:S(2)}) %collective-permute-start.5) | collective-permute-done | bytes 4128 | tf_op jit(solution)/shard_map/ppermute | solution.py:301
  133.7 6.5 %all-gather.7.cloned.1.call-done = bf16[36,256,256]{2,1,0:T(8,128)(2,1)} async-done(((bf16[9,256,256]{2,1,0:T(8,128)(2,1)}), bf16[36,256,256]{2,1,0:T(8,128)(2,1)}) %all-gather.7.cloned.1.call-update) | async-done | bytes 4718608 | tf_op jit(solution)/shard_map/all_gather | solution.py:296
  140.2 4.9 %all-to-all-start.2 = ((bf16[4,48,4096]{2,1,0:T(8,128)(2,1)}), bf16[4,48,4096]{2,1,0:T(8,128)(2,1)}, u32[]{:S(2)}, u32[]{:S(2)}) async-start(bf16[4,48,4096]{2,1,0:T(8,128)(2,1)} %bitcast.42), calls=%async_computation.2 | async-start | bytes 3145728 | tf_op jit(solution)/shard_map/all_to_all | solution.py:273
  145.7 3.0 collective-permute-done.9.refs_3_
  148.7 15.1 %expert.3 = (bf16[384,2048]{1,0:T(8,128)(2,1)}, bf16[384,2048]{1,0:T(8,128)(2,1)}) custom-call(s32[4]{0:T(128)} %pad_add_fusion.place_ref, bf16[384,4096]{1,0:T(8,128)(2,1)} %bitcast.36, bf16[4,9,256,256]{3,2,1,0:T(8,128)(2,1)} %bitcast.27, bf16[4,9,256,256]{3,2,1,0:T(8,128)(2,1)} %collective-permute-done.8.refs_1_, bf16[4,9,256,256]{3,2,1,0:T(8,128)(2,1)} %bitcast.31, ...), custom_call_target="tpu_custom_call" | custom-call | tf_op jit(solution)/shard_map/expert/pallas_call | solution.py:194
  165.4 10.6 %expert.4 = bf16[192,4096]{1,0:T(8,128)(2,1)} custom-call(s32[4]{0:T(128)} %pad_add_fusion.place_ref, bf16[192,4096]{1,0:T(8,128)(2,1)} %bitcast.16.x_hbm, bf16[4,9,256,256]{3,2,1,0:T(8,128)(2,1)} %bitcast.28, bf16[4,9,256,256]{3,2,1,0:T(8,128)(2,1)} %collective-permute-done.8.refs_1_, bf16[4,9,256,256]{3,2,1,0:T(8,128)(2,1)} %bitcast.32, ...), custom_call_target="tpu_custom_call" | custom-call | tf_op jit(solution)/shard_map/expert/pallas_call | solution.py:194
  176.0 25.3 %all_to_all.35 = bf16[4,48,4096]{2,1,0:T(8,128)(2,1)} all-to-all(bf16[4,48,4096]{2,1,0:T(8,128)(2,1)} %bitcast.41), channel_id=1, replica_groups=mesh['zh'=4,'y'=4,'x'=4,'zl'=2,'core'=2] {'y'}, dimensions={0} | all-to-all | bytes 3145728 | tf_op jit(solution)/shard_map/all_to_all | solution.py:273
  201.3 5.0 %all-to-all-start.4 = ((bf16[4,96,2048]{2,1,0:T(8,128)(2,1)}), bf16[4,96,2048]{2,1,0:T(8,128)(2,1)S(1)}, u32[]{:S(2)}, u32[]{:S(2)}) async-start(bf16[4,96,2048]{2,1,0:T(8,128)(2,1)} %bitcast.19), calls=%async_computation.4 | async-start | bytes 3145728 | tf_op jit(solution)/shard_map/all_to_all | solution.py:273
  208.7 4.1 %collective-permute-start.10 = (bf16[64,2048]{1,0:T(8,128)(2,1)}, bf16[64,2048]{1,0:T(8,128)(2,1)S(1)}, u32[]{:S(2)}, u32[]{:S(2)}) collective-permute-start(bf16[64,2048]{1,0:T(8,128)(2,1)} %get-tuple-element.70), channel_id=1, source_target_pairs={{0,192},{64,0},{128,64},{192,128},{1,193},{65,1},{129,65},{193,129... | collective-permute-start | bytes 786440 | tf_op jit(solution)/shard_map/ppermute | solution.py:318
  215.3 4.1 %collective-permute-start.12 = (bf16[64,2048]{1,0:T(8,128)(2,1)}, bf16[64,2048]{1,0:T(8,128)(2,1)S(1)}, u32[]{:S(2)}, u32[]{:S(2)}) collective-permute-start(bf16[64,2048]{1,0:T(8,128)(2,1)} %get-tuple-element.73), channel_id=1, source_target_pairs={{0,192},{64,0},{128,64},{192,128},{1,193},{65,1},{129,65},{193,129... | collective-permute-start | bytes 786440 | tf_op jit(solution)/shard_map/ppermute | solution.py:318
  219.4 10.6 %expert.5 = bf16[192,4096]{1,0:T(8,128)(2,1)} custom-call(s32[4]{0:T(128)} %pad_add_fusion.place_ref, bf16[192,4096]{1,0:T(8,128)(2,1)} %bitcast.38, bf16[4,9,256,256]{3,2,1,0:T(8,128)(2,1)} %bitcast.29, bf16[4,9,256,256]{3,2,1,0:T(8,128)(2,1)} %collective-permute-done.8.refs_1_, bf16[4,9,256,256]{3,2,1,0:T(8,128)(2,1)} %bitcast.33, ...), custom_call_target="tpu_custom_call" | custom-call | tf_op jit(solution)/shard_map/expert/pallas_call | solution.py:194
  230.1 4.0 %collective-permute-done.12.top_ref = bf16[64,2048]{1,0:T(8,128)(2,1)S(1)} collective-permute-done((bf16[64,2048]{1,0:T(8,128)(2,1)}, bf16[64,2048]{1,0:T(8,128)(2,1)S(1)}, u32[]{:S(2)}, u32[]{:S(2)}) %collective-permute-start.12) | collective-permute-done | bytes 262176 | tf_op jit(solution)/shard_map/ppermute | solution.py:318
  235.3 4.8 %all-to-all-start.5 = ((bf16[4,96,2048]{2,1,0:T(8,128)(2,1)}), bf16[4,96,2048]{2,1,0:T(8,128)(2,1)S(1)}, u32[]{:S(2)}, u32[]{:S(2)}) async-start(bf16[4,96,2048]{2,1,0:T(8,128)(2,1)} %bitcast.45), calls=%async_computation.5 | async-start | bytes 3145728 | tf_op jit(solution)/shard_map/all_to_all | solution.py:273
  240.1 3.1 %combine.7 = (bf16[128,2048]{1,0:T(8,128)(2,1)}, bf16[128,2048]{1,0:T(8,128)(2,1)}) custom-call(bf16[2,192,128]{2,1,0:T(8,128)(2,1)} %get-tuple-element.77.high_ref, bf16[2,192,128]{2,1,0:T(8,128)(2,1)} %get-tuple-element.78.low_ref, bf16[4,2,48,2048]{3,2,1,0:T(8,128)(2,1)} %bitcast.39, bf16[64,2048]{1,0:T(8,128)(2,1)} %copy-done.14, bf16[64,2048]{1,0:T(8,128)(2,1)} %copy-done.15), custom_call_target="tpu_custom_call" | custom-call | tf_op jit(solution)/shard_map/combine/pallas_call | solution.py:256
  243.3 4.5 %collective-permute-start.14 = (bf16[128,2048]{1,0:T(8,128)(2,1)}, bf16[128,2048]{1,0:T(8,128)(2,1)S(1)}, u32[]{:S(2)}, u32[]{:S(2)}) collective-permute-start(bf16[128,2048]{1,0:T(8,128)(2,1)} %get-tuple-element.84), channel_id=1, source_target_pairs={{0,192},{64,0},{128,64},{192,128},{1,193},{65,1},{129,65},{193,129... | collective-permute-start | bytes 1572872 | tf_op jit(solution)/shard_map/ppermute | solution.py:332
  247.7 10.1 %all-to-all-done.5 = bf16[4,96,2048]{2,1,0:T(8,128)(2,1)S(1)} async-done(((bf16[4,96,2048]{2,1,0:T(8,128)(2,1)}), bf16[4,96,2048]{2,1,0:T(8,128)(2,1)S(1)}, u32[]{:S(2)}, u32[]{:S(2)}) %all-to-all-start.5) | async-done | bytes 1572896 | tf_op jit(solution)/shard_map/all_to_all | solution.py:273
  259.0 3.1 %combine.8 = (bf16[128,2048]{1,0:T(8,128)(2,1)}, bf16[128,2048]{1,0:T(8,128)(2,1)}) custom-call(bf16[2,192,128]{2,1,0:T(8,128)(2,1)} %get-tuple-element.77.high_ref, bf16[2,192,128]{2,1,0:T(8,128)(2,1)} %get-tuple-element.78.low_ref, bf16[4,2,48,2048]{3,2,1,0:T(8,128)(2,1)} %bitcast.40, bf16[64,2048]{1,0:T(8,128)(2,1)} %copy-done.12, bf16[64,2048]{1,0:T(8,128)(2,1)} %copy-done.13), custom_call_target="tpu_custom_call" | custom-call | tf_op jit(solution)/shard_map/combine/pallas_call | solution.py:256
  262.1 6.3 %collective-permute-done.14.refs_0_ = bf16[128,2048]{1,0:T(8,128)(2,1)S(1)} collective-permute-done((bf16[128,2048]{1,0:T(8,128)(2,1)}, bf16[128,2048]{1,0:T(8,128)(2,1)S(1)}, u32[]{:S(2)}, u32[]{:S(2)}) %collective-permute-start.14) | collective-permute-done | bytes 524320 | tf_op jit(solution)/shard_map/ppermute | solution.py:332
  269.4 4.8 %all-to-all-start.6 = ((bf16[4,48,4096]{2,1,0:T(8,128)(2,1)}), bf16[4,48,4096]{2,1,0:T(8,128)(2,1)S(1)}, u32[]{:S(2)}, u32[]{:S(2)}) async-start(bf16[4,48,4096]{2,1,0:T(8,128)(2,1)} %bitcast.23), calls=%async_computation.6 | async-start | bytes 3145728 | tf_op jit(solution)/shard_map/all_to_all | solution.py:273
  274.2 4.5 %collective-permute-start.16 = (bf16[128,2048]{1,0:T(8,128)(2,1)}, bf16[128,2048]{1,0:T(8,128)(2,1)S(1)}, u32[]{:S(2)}, u32[]{:S(2)}) collective-permute-start(bf16[128,2048]{1,0:T(8,128)(2,1)} %get-tuple-element.95), channel_id=1, source_target_pairs={{0,192},{64,0},{128,64},{192,128},{1,193},{65,1},{129,65},{193,129... | collective-permute-start | bytes 1572872 | tf_op jit(solution)/shard_map/ppermute | solution.py:332
  278.7 18.2 %collective-permute-done.16.refs_2_ = bf16[128,2048]{1,0:T(8,128)(2,1)S(1)} collective-permute-done((bf16[128,2048]{1,0:T(8,128)(2,1)}, bf16[128,2048]{1,0:T(8,128)(2,1)S(1)}, u32[]{:S(2)}, u32[]{:S(2)}) %collective-permute-start.16) | collective-permute-done | bytes 524320 | tf_op jit(solution)/shard_map/ppermute | solution.py:332
  296.9 3.0 collective-permute-done.17.refs_3_
  301.3 3.9 %combine.9 = bf16[128,4096]{1,0:T(8,128)(2,1)} custom-call(bf16[1,192,128]{2,1,0:T(8,128)(2,1)} %get-tuple-element.51.high_ref, bf16[1,192,128]{2,1,0:T(8,128)(2,1)} %get-tuple-element.52.low_ref, bf16[4,1,48,4096]{3,2,1,0:T(8,128)(2,1)} %bitcast.44, bf16[128,2048]{1,0:T(8,128)(2,1)} %copy-done.6, bf16[128,2048]{1,0:T(8,128)(2,1)} %copy-done.7, ...), custom_call_target="tpu_custom_call" | custom-call | tf_op jit(solution)/shard_map/combine/pallas_call | solution.py:256
  (91 shorter events, 31.7 us)
Async XLA Ops:
  6.5 127.2 %all-gather.5.cloned.1.call-start = ((), (), s32[]{:S(2)}) async-start(), calls=%async_computation.7 | async-start | bytes 5898240 | tf_op jit(solution)/shard_map/all_gather | solution.py:292
  9.3 78.4 %collective-permute-start.4 = (bf16[9,256,256]{2,1,0:T(8,128)(2,1)}, bf16[9,256,256]{2,1,0:T(8,128)(2,1)}, u32[]{:S(2)}, u32[]{:S(2)}) collective-permute-start(bf16[9,256,256]{2,1,0:T(8,128)(2,1)} %pack.1), channel_id=1, source_target_pairs={{0,2},{2,0},{1,3},{3,1},{4,6},{6,4},{5,7},{7,5},{8,10},{10,8},{9,1... | collective-permute-start | bytes 3538952 | tf_op jit(solution)/shard_map/ppermute | solution.py:291
  16.0 10.5 %copy-start.16 = (f32[8,128]{1,0:T(8,128)S(1)}, f32[8,128]{1,0:T(8,128)}, u32[]{:S(2)}) copy-start(f32[8,128]{1,0:T(8,128)} %pad_maximum_fusion.refs_0_) | copy-start | bytes 12292
  16.0 71.7 %all-to-all-start = ((bf16[4,48,4096]{2,1,0:T(8,128)(2,1)}), bf16[4,48,4096]{2,1,0:T(8,128)(2,1)S(1)}, u32[]{:S(2)}, u32[]{:S(2)}) async-start(bf16[4,48,4096]{2,1,0:T(8,128)(2,1)} %bitcast.43), calls=%async_computation | async-start | bytes 3145728 | tf_op jit(solution)/shard_map/all_to_all | solution.py:273
  21.1 119.1 %all-gather.7.cloned.1.call-start = ((), (), s32[]{:S(2)}) async-start(), calls=%async_computation.8 | async-start | bytes 5898240 | tf_op jit(solution)/shard_map/all_gather | solution.py:296
  21.1 66.6 %collective-permute-start = (bf16[128,4096]{1,0:T(8,128)(2,1)}, bf16[128,4096]{1,0:T(8,128)(2,1)S(1)}, u32[]{:S(2)}, u32[]{:S(2)}) collective-permute-start(bf16[128,4096]{1,0:T(8,128)(2,1)} %refs_0_.1), channel_id=1, source_target_pairs={{0,64},{64,128},{128,192},{192,0},{1,65},{65,129},{129,193},{193,1... | collective-permute-start | bytes 3145736 | tf_op jit(solution)/shard_map/ppermute | solution.py:289
  24.4 63.4 %collective-permute-start.1 = (bf16[128,4096]{1,0:T(8,128)(2,1)}, bf16[128,4096]{1,0:T(8,128)(2,1)}, u32[]{:S(2)}, u32[]{:S(2)}) collective-permute-start(bf16[128,4096]{1,0:T(8,128)(2,1)} %refs_0_.1), channel_id=1, source_target_pairs={{0,192},{64,0},{128,64},{192,128},{1,193},{65,1},{129,65},{193,129... | collective-permute-start | bytes 3145736 | tf_op jit(solution)/shard_map/ppermute | solution.py:289
  26.5 24.0 %collective-permute-start.3 = (f32[8,128]{1,0:T(8,128)S(1)}, f32[8,128]{1,0:T(8,128)S(1)}, u32[]{:S(2)}, u32[]{:S(2)}) collective-permute-start(f32[8,128]{1,0:T(8,128)S(1)} %copy-done.16), channel_id=1, source_target_pairs={{0,192},{64,0},{128,64},{192,128},{1,193},{65,1},{129,65},{193,129... | collective-permute-start | bytes 12296 | tf_op jit(solution)/shard_map/ppermute | solution.py:290
  29.4 58.3 %collective-permute-start.2 = (f32[8,128]{1,0:T(8,128)S(1)}, f32[8,128]{1,0:T(8,128)S(1)}, u32[]{:S(2)}, u32[]{:S(2)}) collective-permute-start(f32[8,128]{1,0:T(8,128)S(1)} %copy-done.16), channel_id=1, source_target_pairs={{0,64},{64,128},{128,192},{192,0},{1,65},{65,129},{129,193},{193,1... | collective-permute-start | bytes 12296 | tf_op jit(solution)/shard_map/ppermute | solution.py:290
  50.5 37.3 %copy-start.20 = (f32[8,128]{1,0:T(8,128)}, f32[8,128]{1,0:T(8,128)S(1)}, u32[]{:S(2)}) copy-start(f32[8,128]{1,0:T(8,128)S(1)} %collective-permute-done.3.refs_1_) | copy-start | bytes 12292
  87.7 5.8 %copy-start.1 = (bf16[4,48,4096]{2,1,0:T(8,128)(2,1)}, bf16[4,48,4096]{2,1,0:T(8,128)(2,1)S(1)}, u32[]{:S(2)}) copy-start(bf16[4,48,4096]{2,1,0:T(8,128)(2,1)S(1)} %all-to-all-done) | copy-start | bytes 4718596
  93.6 40.1 %all-to-all-start.1 = ((bf16[4,96,4096]{2,1,0:T(8,128)(2,1)}), bf16[4,96,4096]{2,1,0:T(8,128)(2,1)S(1)}, u32[]{:S(2)}, u32[]{:S(2)}) async-start(bf16[4,96,4096]{2,1,0:T(8,128)(2,1)} %bitcast.37), calls=%async_computation.1 | async-start | bytes 6291456 | tf_op jit(solution)/shard_map/all_to_all | solution.py:273
  98.5 5.3 %copy-start.19 = (f32[8,128]{1,0:T(8,128)S(1)}, f32[8,128]{1,0:T(8,128)}, u32[]{:S(2)}) copy-start(f32[8,128]{1,0:T(8,128)} %copy-done.18) | copy-start | bytes 12292
  100.7 29.0 %collective-permute-start.7 = (bf16[64,4096]{1,0:T(8,128)(2,1)S(1)}, bf16[64,4096]{1,0:T(8,128)(2,1)S(1)}, u32[]{:S(2)}, u32[]{:S(2)}) collective-permute-start(bf16[64,4096]{1,0:T(8,128)(2,1)S(1)} %slice.7), channel_id=1, source_target_pairs={{0,192},{64,0},{128,64},{192,128},{1,193},{65,1},{129,65},{193,129... | collective-permute-start | bytes 1572872 | tf_op jit(solution)/shard_map/ppermute | solution.py:300
  102.3 27.5 %collective-permute-start.6 = (bf16[64,4096]{1,0:T(8,128)(2,1)S(1)}, bf16[64,4096]{1,0:T(8,128)(2,1)S(1)}, u32[]{:S(2)}, u32[]{:S(2)}) collective-permute-start(bf16[64,4096]{1,0:T(8,128)(2,1)S(1)} %slice.6), channel_id=1, source_target_pairs={{0,64},{64,128},{128,192},{192,0},{1,65},{65,129},{129,193},{193,1... | collective-permute-start | bytes 1572872 | tf_op jit(solution)/shard_map/ppermute | solution.py:300
  103.7 23.9 %collective-permute-start.5 = (f32[8,128]{1,0:T(8,128)S(1)}, f32[8,128]{1,0:T(8,128)S(1)}, u32[]{:S(2)}, u32[]{:S(2)}) collective-permute-start(f32[8,128]{1,0:T(8,128)S(1)} %copy-done.19), channel_id=1, source_target_pairs={{0,64},{64,128},{128,192},{192,0},{1,65},{65,129},{129,193},{193,1... | collective-permute-start | bytes 12296 | tf_op jit(solution)/shard_map/ppermute | solution.py:301
  133.7 6.5 %copy-start = (bf16[4,96,4096]{2,1,0:T(8,128)(2,1)}, bf16[4,96,4096]{2,1,0:T(8,128)(2,1)S(1)}, u32[]{:S(2)}) copy-start(bf16[4,96,4096]{2,1,0:T(8,128)(2,1)S(1)} %all-to-all-done.1) | copy-start | bytes 9437188
  133.7 12.0 %collective-permute-start.8 = (bf16[4,9,256,256]{3,2,1,0:T(8,128)(2,1)}, bf16[4,9,256,256]{3,2,1,0:T(8,128)(2,1)}, u32[]{:S(2)}, u32[]{:S(2)}) collective-permute-start(bf16[4,9,256,256]{3,2,1,0:T(8,128)(2,1)} %bitcast.26), channel_id=1, source_target_pairs={{0,1},{1,0},{2,3},{3,2},{4,5},{5,4},{6,7},{7,6},{8,9},{9,8},{10,11... | collective-permute-start | bytes 14155784 | tf_op jit(solution)/shard_map/ppermute | solution.py:304
  140.2 8.5 %collective-permute-start.9 = (bf16[4,9,256,256]{3,2,1,0:T(8,128)(2,1)}, bf16[4,9,256,256]{3,2,1,0:T(8,128)(2,1)}, u32[]{:S(2)}, u32[]{:S(2)}) collective-permute-start(bf16[4,9,256,256]{3,2,1,0:T(8,128)(2,1)} %bitcast.30), channel_id=1, source_target_pairs={{0,1},{1,0},{2,3},{3,2},{4,5},{5,4},{6,7},{7,6},{8,9},{9,8},{10,11... | collective-permute-start | bytes 14155784 | tf_op jit(solution)/shard_map/ppermute | solution.py:306
  140.2 25.2 %all-to-all-start.2 = ((bf16[4,48,4096]{2,1,0:T(8,128)(2,1)}), bf16[4,48,4096]{2,1,0:T(8,128)(2,1)}, u32[]{:S(2)}, u32[]{:S(2)}) async-start(bf16[4,48,4096]{2,1,0:T(8,128)(2,1)} %bitcast.42), calls=%async_computation.2 | async-start | bytes 3145728 | tf_op jit(solution)/shard_map/all_to_all | solution.py:273
  201.3 32.8 %all-to-all-start.4 = ((bf16[4,96,2048]{2,1,0:T(8,128)(2,1)}), bf16[4,96,2048]{2,1,0:T(8,128)(2,1)S(1)}, u32[]{:S(2)}, u32[]{:S(2)}) async-start(bf16[4,96,2048]{2,1,0:T(8,128)(2,1)} %bitcast.19), calls=%async_computation.4 | async-start | bytes 3145728 | tf_op jit(solution)/shard_map/all_to_all | solution.py:273
  208.7 21.3 %collective-permute-start.10 = (bf16[64,2048]{1,0:T(8,128)(2,1)}, bf16[64,2048]{1,0:T(8,128)(2,1)S(1)}, u32[]{:S(2)}, u32[]{:S(2)}) collective-permute-start(bf16[64,2048]{1,0:T(8,128)(2,1)} %get-tuple-element.70), channel_id=1, source_target_pairs={{0,192},{64,0},{128,64},{192,128},{1,193},{65,1},{129,65},{193,129... | collective-permute-start | bytes 786440 | tf_op jit(solution)/shard_map/ppermute | solution.py:318
  212.8 17.2 %collective-permute-start.11 = (bf16[64,2048]{1,0:T(8,128)(2,1)}, bf16[64,2048]{1,0:T(8,128)(2,1)S(1)}, u32[]{:S(2)}, u32[]{:S(2)}) collective-permute-start(bf16[64,2048]{1,0:T(8,128)(2,1)} %get-tuple-element.71), channel_id=1, source_target_pairs={{0,64},{64,128},{128,192},{192,0},{1,65},{65,129},{129,193},{193,1... | collective-permute-start | bytes 786440 | tf_op jit(solution)/shard_map/ppermute | solution.py:318
  215.3 18.8 %collective-permute-start.12 = (bf16[64,2048]{1,0:T(8,128)(2,1)}, bf16[64,2048]{1,0:T(8,128)(2,1)S(1)}, u32[]{:S(2)}, u32[]{:S(2)}) collective-permute-start(bf16[64,2048]{1,0:T(8,128)(2,1)} %get-tuple-element.73), channel_id=1, source_target_pairs={{0,192},{64,0},{128,64},{192,128},{1,193},{65,1},{129,65},{193,129... | collective-permute-start | bytes 786440 | tf_op jit(solution)/shard_map/ppermute | solution.py:318
  219.4 14.6 %collective-permute-start.13 = (bf16[64,2048]{1,0:T(8,128)(2,1)}, bf16[64,2048]{1,0:T(8,128)(2,1)S(1)}, u32[]{:S(2)}, u32[]{:S(2)}) collective-permute-start(bf16[64,2048]{1,0:T(8,128)(2,1)} %get-tuple-element.74), channel_id=1, source_target_pairs={{0,64},{64,128},{128,192},{192,0},{1,65},{65,129},{129,193},{193,1... | collective-permute-start | bytes 786440 | tf_op jit(solution)/shard_map/ppermute | solution.py:318
  235.3 22.5 %all-to-all-start.5 = ((bf16[4,96,2048]{2,1,0:T(8,128)(2,1)}), bf16[4,96,2048]{2,1,0:T(8,128)(2,1)S(1)}, u32[]{:S(2)}, u32[]{:S(2)}) async-start(bf16[4,96,2048]{2,1,0:T(8,128)(2,1)} %bitcast.45), calls=%async_computation.5 | async-start | bytes 3145728 | tf_op jit(solution)/shard_map/all_to_all | solution.py:273
  243.3 25.1 %collective-permute-start.14 = (bf16[128,2048]{1,0:T(8,128)(2,1)}, bf16[128,2048]{1,0:T(8,128)(2,1)S(1)}, u32[]{:S(2)}, u32[]{:S(2)}) collective-permute-start(bf16[128,2048]{1,0:T(8,128)(2,1)} %get-tuple-element.84), channel_id=1, source_target_pairs={{0,192},{64,0},{128,64},{192,128},{1,193},{65,1},{129,65},{193,129... | collective-permute-start | bytes 1572872 | tf_op jit(solution)/shard_map/ppermute | solution.py:332
  247.7 20.7 %collective-permute-start.15 = (bf16[128,2048]{1,0:T(8,128)(2,1)}, bf16[128,2048]{1,0:T(8,128)(2,1)S(1)}, u32[]{:S(2)}, u32[]{:S(2)}) collective-permute-start(bf16[128,2048]{1,0:T(8,128)(2,1)} %get-tuple-element.85), channel_id=1, source_target_pairs={{0,64},{64,128},{128,192},{192,0},{1,65},{65,129},{129,193},{193,1... | collective-permute-start | bytes 1572872 | tf_op jit(solution)/shard_map/ppermute | solution.py:332
  268.4 10.3 %copy-start.23 = (bf16[128,2048]{1,0:T(8,128)(2,1)S(1)}, bf16[128,2048]{1,0:T(8,128)(2,1)}, u32[]{:S(2)}) copy-start(bf16[128,2048]{1,0:T(8,128)(2,1)} %get-tuple-element.96) | copy-start | bytes 1572868
  269.4 30.5 %all-to-all-start.6 = ((bf16[4,48,4096]{2,1,0:T(8,128)(2,1)}), bf16[4,48,4096]{2,1,0:T(8,128)(2,1)S(1)}, u32[]{:S(2)}, u32[]{:S(2)}) async-start(bf16[4,48,4096]{2,1,0:T(8,128)(2,1)} %bitcast.23), calls=%async_computation.6 | async-start | bytes 3145728 | tf_op jit(solution)/shard_map/all_to_all | solution.py:273
  274.2 22.7 %collective-permute-start.16 = (bf16[128,2048]{1,0:T(8,128)(2,1)}, bf16[128,2048]{1,0:T(8,128)(2,1)S(1)}, u32[]{:S(2)}, u32[]{:S(2)}) collective-permute-start(bf16[128,2048]{1,0:T(8,128)(2,1)} %get-tuple-element.95), channel_id=1, source_target_pairs={{0,192},{64,0},{128,64},{192,128},{1,193},{65,1},{129,65},{193,129... | collective-permute-start | bytes 1572872 | tf_op jit(solution)/shard_map/ppermute | solution.py:332
  278.7 21.2 %collective-permute-start.17 = (bf16[128,2048]{1,0:T(8,128)(2,1)S(1)}, bf16[128,2048]{1,0:T(8,128)(2,1)S(1)}, u32[]{:S(2)}, u32[]{:S(2)}) collective-permute-start(bf16[128,2048]{1,0:T(8,128)(2,1)S(1)} %copy-done.23), channel_id=1, source_target_pairs={{0,64},{64,128},{128,192},{192,0},{1,65},{65,129},{129,193},{193,1... | collective-permute-start | bytes 1572872 | tf_op jit(solution)/shard_map/ppermute | solution.py:332
  (18 other events, 33.7 us)
Sparse Core Ops, SparseCore 0:
  9.4 57.4 all-gather.4
  87.9 52.2 all-gather.6
